TPU v7x, 128 devices: a whole 4x4x4 slice. The times are simulated.
128 devices in a mesh: clus: 16 (over y, x_hi, core), theta: 8 (over x_lo, z).
Axes of the slice: x: 4 (x_hi: 2, x_lo: 2; x = x_hi * 2 + x_lo), y: 4, z: 4, core: 2. Of those that a mesh axis runs over, the one named last changes fastest.
Arguments:
- children: float32 [128, 2, 2, 128, 256], P('clus', None, None, 'theta'), may hold values from -6 to 6
- theta_band: float32 [256, 8], P('theta'), may hold values from -2 to 2
- phi_interp: float32 [256, 512], replicated, may hold values from -0.375 to 0.375
- child_shift: float32 [4, 2, 256, 512], P(None, None, 'theta'), may hold values from -4 to 4
- translators: float32 [40, 2, 256, 512], P(None, None, ('theta', 'clus')), may hold values from -1.5 to 1.5
- far_source: int32 [32, 32], replicated, may hold values from 0 to 31
- far_offset: int32 [32, 32], replicated, may hold values from 0 to 39
- far_count: int32 [32], replicated, may hold values from 4 to 32, as said below
Outputs:
- incoming: float32 [128, 2, 2, 128, 256], P('clus', None, None, 'theta')
Inputs may be any that keep to these rules, and one draw needn't show every extreme that they name: The first far_count[p] slots of row p of far_source and far_offset are valid; the remaining slots are padding and carry no interaction. A list is full in every draw.
All inputs are finite; a program needn't handle non-finite values.
Results may differ from a plain program's by a relative error of at most 0.0003.
Values sent between devices are 32-bit elements; how exact they have to be, the bound alone decides.
No kernel may reach another device: no remote copies, remote signals or barrier semaphores. Data moves between devices by JAX's collectives and lax.ppermute only.
A program may use at most 128 MiB of HBM per device.

v0:
```python
import jax
import jax.numpy as jnp
from jax import lax
from jax.experimental import pallas as pl
from jax.experimental.pallas import tpu as pltpu
from jax.sharding import PartitionSpec as P

KIDS = 4
GROUP = 4
HIGH = lax.Precision.HIGH


def shifted_ring(value, axis, step):
    count = lax.axis_size(axis)
    return lax.ppermute(value, axis, [(i, (i + step) % count) for i in range(count)])


def complex_times(left_side, right_side):
    real_part = (
        left_side[..., 0, :, :] * right_side[..., 0, :, :]
        - left_side[..., 1, :, :] * right_side[..., 1, :, :]
    )
    imag_part = (
        left_side[..., 0, :, :] * right_side[..., 1, :, :]
        + left_side[..., 1, :, :] * right_side[..., 0, :, :]
    )
    return jnp.stack([real_part, imag_part], axis=-3)


def band_table(theta_band, child_rows):
    parent_rows = theta_band.shape[0]
    row_index = jnp.arange(parent_rows, dtype=jnp.int32)
    column_index = jnp.arange(child_rows + 8, dtype=jnp.int32)
    table = jnp.zeros((parent_rows, child_rows + 8), jnp.float32)
    for tap_index in range(8):
        target = row_index // 2 + tap_index + 1
        hits = (column_index[None, :] == target[:, None]).astype(jnp.float32)
        table = table + theta_band[:, tap_index][:, None] * hits
    return table


def translate_kernel(source_ref, offset_ref, count_ref, field_ref, operator_ref, out_ref):
    parents = out_ref.shape[0]

    def one_parent(parent, carry):
        count = count_ref[parent]

        def some_slots(step, sums):
            sums = list(sums)
            for lane in range(GROUP):
                slot = step * GROUP + lane
                source = source_ref[parent, slot]
                offset = offset_ref[parent, slot]
                live = (slot < count).astype(jnp.float32)
                real = operator_ref[offset, 0] * live
                imag = operator_ref[offset, 1] * live
                for pol in range(2):
                    a = field_ref[source, pol * 2]
                    b = field_ref[source, pol * 2 + 1]
                    sums[pol * 2] = sums[pol * 2] + (real * a - imag * b)
                    sums[pol * 2 + 1] = sums[pol * 2 + 1] + (real * b + imag * a)
            return tuple(sums)

        zero = jnp.zeros(out_ref.shape[2:], jnp.float32)
        sums = lax.fori_loop(0, (count + GROUP - 1) // GROUP, some_slots, (zero,) * 4)
        for index in range(4):
            out_ref[parent, index] = sums[index]
        return carry

    lax.fori_loop(0, parents, one_parent, 0)


def translate(field, operators, far_source, far_offset, far_count):
    smem = pl.BlockSpec(memory_space=pltpu.SMEM)
    vmem = pl.BlockSpec(memory_space=pltpu.VMEM)
    return pl.pallas_call(
        translate_kernel,
        out_shape=jax.ShapeDtypeStruct(field.shape, jnp.float32),
        in_specs=[smem, smem, smem, vmem, vmem],
        out_specs=vmem,
        name="translate",
    )(far_source, far_offset, far_count, field, operators)


def on_device(
    children, theta_band, phi_interp, child_shift, translators, far_source, far_offset, far_count
):
    child_rows = children.shape[3]
    groups = lax.axis_size("clus")
    strips = lax.axis_size("theta")
    strip = lax.axis_index("theta")
    parents_here = children.shape[0] // KIDS
    rows = translators.shape[2]
    blocks = translators.shape[3] // 128
    first = (strip > 0).astype(jnp.float32)
    last = (strip < strips - 1).astype(jnp.float32)
    table = band_table(theta_band, child_rows)
    above = shifted_ring(children[:, :, :, child_rows - 4 :], "theta", 1) * first
    below = shifted_ring(children[:, :, :, :4], "theta", -1) * last
    padded = jnp.concatenate([above, children, below], axis=3)
    spread = jnp.einsum("rj,...jq->...rq", table, padded, precision=HIGH)
    fine = jnp.einsum("...q,qp->...p", spread, phi_interp, precision=HIGH)
    grouped = fine.reshape((parents_here, KIDS) + fine.shape[1:])
    parents = jnp.sum(complex_times(child_shift[None, :, None], grouped), axis=1)
    packed = parents.reshape(parents_here, 2, 2, groups, rows, blocks, 128)
    packed = packed.transpose(3, 0, 1, 2, 5, 4, 6).reshape(groups, parents_here, 4, 8, 128)
    field = lax.all_to_all(packed, "clus", 0, 0).reshape(groups * parents_here, 4, 8, 128)
    operators = translators.reshape(-1, 2, rows, blocks, 128).transpose(0, 1, 3, 2, 4)
    operators = operators.reshape(-1, 2, 8, 128)
    summed = translate(field, operators, far_source, far_offset, far_count)
    summed = summed.reshape(groups, parents_here, 4, 8, 128)
    local = lax.all_to_all(summed, "clus", 0, 0)
    local = local.reshape(groups, parents_here, 2, 2, blocks, rows, 128)
    local = local.transpose(1, 2, 3, 0, 5, 4, 6).reshape(parents.shape)
    conjugate = jnp.stack([child_shift[:, 0], -child_shift[:, 1]], axis=1)
    shifted = complex_times(conjugate[None, :, None], local[:, None])
    shifted = shifted.reshape((parents_here * KIDS,) + shifted.shape[2:])
    back_phi = jnp.einsum("...p,qp->...q", shifted, phi_interp, precision=HIGH)
    extended = jnp.einsum("rj,...rq->...jq", table, back_phi, precision=HIGH)
    own_part = extended[..., 4 : 4 + child_rows, :]
    from_below = shifted_ring(extended[..., child_rows + 4 :, :], "theta", 1) * first
    from_above = shifted_ring(extended[..., :4, :], "theta", -1) * last
    lead = [(0, 0)] * (own_part.ndim - 2)
    result = own_part + jnp.pad(from_below, lead + [(0, child_rows - 4), (0, 0)])
    result = result + jnp.pad(from_above, lead + [(child_rows - 4, 0), (0, 0)])
    return result


def solution(mesh):
    return jax.shard_map(
        on_device,
        mesh=mesh,
        in_specs=(
            P("clus", None, None, "theta", None),
            P("theta", None),
            P(),
            P(None, None, "theta", None),
            P(None, None, ("theta", "clus"), None),
            P(),
            P(),
            P(),
        ),
        out_specs=P("clus", None, None, "theta", None),
        check_vma=False,
    )
```

profile of v0, /device:TPU:0, one launch (start us, length us, event | category | flops | bytes accessed | tf_op | source)
XLA Modules:
  0.0 68.7 jit_solution(2628106408716436653)
XLA Ops:
  0.0 0.0 copy-start
  0.0 0.0 copy-start.2
  0.0 1.2 %fusion.21 = (f32[8,2,2,4,256]{4,3,2,1,0:T(4,128)S(1)}, f32[8,2,2,4,256]{4,3,2,1,0:T(4,128)S(1)}) fusion(f32[8,2,2,16,256]{4,3,2,1,0:T(8,128)} %param.8), kind=kLoop, calls=%fused_computation.70 | loop fusion | bytes 524288 | tf_op jit(solution)/shard_map/slice | solution.py:98
  1.2 5.1 %collective-permute-start.1 = (f32[8,2,2,4,256]{4,3,2,1,0:T(4,128)S(1)}, f32[8,2,2,4,256]{4,3,2,1,0:T(4,128)S(1)}, u32[]{:S(2)}, u32[]{:S(2)}) collective-permute-start(f32[8,2,2,4,256]{4,3,2,1,0:T(4,128)S(1)} %get-tuple-element.20), channel_id=1, source_target_pairs={{0,7},{1,0},{2,1},{3,2},{4,3},{5,4},{6,5},{7,6},{8,15},{9,8},{10,9... | collective-permute-start | bytes 393224 | tf_op jit(solution)/shard_map/ppermute | solution.py:15
  6.3 0.0 collective-permute-start
  6.3 1.0 %slice_bitcast_fusion.13 = (f32[32]{0:T(128)S(1)}, f32[32]{0:T(128)S(1)}, f32[32]{0:T(128)S(1)}, f32[32]{0:T(128)S(1)}, f32[32]{0:T(128)S(1)}, /*index=5*/f32[32]{0:T(128)S(1)}, f32[32]{0:T(128)S(1)}, f32[32]{0:T(128)S(1)}) fusion(f32[32,8]{0,1:T(8,128)} %param.9), kind=kLoop, calls=%fused_computation.55 | loop fusion | bytes 2048 | tf_op jit(solution)/shard_map/mul | solution.py:38
  7.3 1.1 %slice_bitcast_fusion.4 = (f32[4,32,512]{2,1,0:T(8,128)S(1)}, f32[4,32,512]{2,1,0:T(8,128)S(1)}) fusion(f32[1,4,1,2,32,512]{5,4,3,1,2,0:T(8,128)} %bitcast.85), kind=kLoop, calls=%fused_computation.26 | loop fusion | bytes 1048576 | tf_op jit(solution)/shard_map/mul | solution.py:20
  8.4 0.6 collective-permute-done.1
  9.1 4.3 %collective-permute-done = f32[8,2,2,4,256]{4,3,2,1,0:T(4,128)S(1)} collective-permute-done((f32[8,2,2,4,256]{4,3,2,1,0:T(4,128)S(1)}, f32[8,2,2,4,256]{4,3,2,1,0:T(4,128)S(1)}, u32[]{:S(2)}, u32[]{:S(2)}) %collective-permute-start) | collective-permute-done | bytes 131104 | tf_op jit(solution)/shard_map/ppermute | solution.py:15
  13.4 0.0 copy-done.2
  13.4 0.6 convolution_bitcast_fusion
  14.1 0.0 copy-done
  14.1 1.0 %fusion.11 = f32[8,2,2,32,512]{4,3,2,1,0:T(8,128)S(1)} fusion(f32[8,2,2,32,256]{4,3,2,1,0:T(8,128)S(1)} %convolution_bitcast_fusion, f32[256,512]{1,0:T(8,128)S(1)} %copy-done), kind=kOutput, calls=%fused_computation.20 | convolution fusion | flops 805306368 | bytes 3670016 | tf_op jit(solution)/shard_map/...q,qp->...p/dot_general | solution.py:102
  15.1 0.4 multiply_subtract_fusion.1
  15.6 0.2 maximum_reduce_fusion
  15.8 0.2 reshape.127
  16.0 0.1 copy.16
  16.1 0.0 copy-start.1
  16.1 0.2 copy.17
  16.3 19.0 %all_to_all.10 = f32[16,2,4,8,128]{4,3,2,1,0:T(8,128)} all-to-all(f32[16,2,4,8,128]{4,3,2,1,0:T(8,128)S(1)} %copy.17), channel_id=1, replica_groups=mesh['clus'=16,'theta'=8] {'clus'}, dimensions={0} | all-to-all | bytes 1048576 | tf_op jit(solution)/shard_map/all_to_all | solution.py:107
  35.3 6.1 %translate.1 = f32[32,4,8,128]{3,2,1,0:T(8,128)} custom-call(s32[32,32]{1,0:T(8,128)} %source_ref.1, s32[32,32]{1,0:T(8,128)} %offset_ref.1, s32[32]{0:T(128)} %count_ref.1, f32[32,4,8,128]{3,2,1,0:T(8,128)} %bitcast.84, f32[40,2,8,128]{3,2,1,0:T(8,128)} %bitcast.93), custom_call_target="tpu_custom_call" | custom-call | tf_op jit(solution)/shard_map/translate/pallas_call | solution.py:76
  41.3 3.6 %all-to-all-start.1 = ((f32[16,2,4,8,128]{4,3,2,1,0:T(8,128)}), f32[16,2,4,8,128]{4,3,2,1,0:T(8,128)S(1)}, u32[]{:S(2)}, u32[]{:S(2)}) async-start(f32[16,2,4,8,128]{4,3,2,1,0:T(8,128)} %bitcast.81), calls=%async_computation.1 | async-start | bytes 1048576 | tf_op jit(solution)/shard_map/all_to_all | solution.py:112
  44.9 0.0 copy-done.1
  45.1 12.2 %all-to-all-done.1 = f32[16,2,4,8,128]{4,3,2,1,0:T(8,128)S(1)} async-done(((f32[16,2,4,8,128]{4,3,2,1,0:T(8,128)}), f32[16,2,4,8,128]{4,3,2,1,0:T(8,128)S(1)}, u32[]{:S(2)}, u32[]{:S(2)}) %all-to-all-start.1) | async-done | bytes 524320 | tf_op jit(solution)/shard_map/all_to_all | solution.py:112
  57.2 0.3 copy.19
  57.5 0.3 copy.20
  57.9 0.2 broadcast_in_dim_reshape.3
  58.1 0.1 mul.273
  58.3 0.1 mul.281
  58.4 0.1 mul.233
  58.5 0.1 mul.277
  58.5 0.5 multiply_subtract_fusion
  59.1 1.0 %fusion = f32[8,2,2,32,256]{4,3,2,1,0:T(8,128)S(1)} fusion(f32[8,2,1,32,512]{4,3,2,1,0:T(8,128)S(1)} %get-tuple-element.6, f32[8,2,1,32,512]{4,3,2,1,0:T(8,128)S(1)} %get-tuple-element.5, f32[256,512]{1,0:T(8,128)S(1)} %copy-done), kind=kOutput, calls=%fused_computation.1 | convolution fusion | flops 805830656 | bytes 3670016 | tf_op jit(solution)/shard_map/...p,qp->...q/dot_general | solution.py:118
  60.1 0.5 convolution_bitcast_fusion.1
  60.6 0.1 fusion.19
  60.6 0.1 collective-permute-start.2
  60.7 4.1 %collective-permute-start.3 = (f32[8,2,2,4,256]{4,3,2,1,0:T(4,128)S(1)}, f32[8,2,2,4,256]{4,3,2,1,0:T(4,128)S(1)}, u32[]{:S(2)}, u32[]{:S(2)}) collective-permute-start(f32[8,2,2,4,256]{4,3,2,1,0:T(4,128)S(1)} %get-tuple-element.10), channel_id=1, source_target_pairs={{0,7},{1,0},{2,1},{3,2},{4,3},{5,4},{6,5},{7,6},{8,15},{9,8},{10,9... | collective-permute-start | bytes 393224 | tf_op jit(solution)/shard_map/ppermute | solution.py:15
  64.8 2.9 %collective-permute-done.2 = f32[8,2,2,4,256]{4,3,2,1,0:T(4,128)S(1)} collective-permute-done((f32[8,2,2,4,256]{4,3,2,1,0:T(4,128)S(1)}, f32[8,2,2,4,256]{4,3,2,1,0:T(4,128)S(1)}, u32[]{:S(2)}, u32[]{:S(2)}) %collective-permute-start.2) | collective-permute-done | bytes 131104 | tf_op jit(solution)/shard_map/ppermute | solution.py:15
  67.8 0.0 collective-permute-done.3
  67.8 0.9 %fusion.9 = f32[8,2,2,16,256]{4,3,2,1,0:T(8,128)} fusion(f32[8,2,2,24,256]{4,3,2,1,0:T(8,128)S(1)} %convolution_bitcast_fusion.1, f32[8,2,2,4,256]{4,3,2,1,0:T(4,128)S(1)} %bitcast.92, f32[8,2,2,4,256]{4,3,2,1,0:T(4,128)S(1)} %bitcast.91), kind=kLoop, calls=%fused_computation.17 | loop fusion | flops 262144 | bytes 1310720 | tf_op jit(solution)/shard_map/add | solution.py:125
  (12 shorter events, 0.2 us)
Async XLA Ops:
  0.0 14.1 %copy-start = (f32[256,512]{1,0:T(8,128)S(1)}, f32[256,512]{1,0:T(8,128)}, u32[]{:S(2)}) copy-start(f32[256,512]{1,0:T(8,128)} %param.10) | copy-start | bytes 1572868
  0.0 13.4 %copy-start.2 = (f32[8,2,2,16,256]{4,3,2,1,0:T(8,128)S(1)}, f32[8,2,2,16,256]{4,3,2,1,0:T(8,128)}, u32[]{:S(2)}) copy-start(f32[8,2,2,16,256]{4,3,2,1,0:T(8,128)} %param.8) | copy-start | bytes 1572868
  1.2 7.9 %collective-permute-start.1 = (f32[8,2,2,4,256]{4,3,2,1,0:T(4,128)S(1)}, f32[8,2,2,4,256]{4,3,2,1,0:T(4,128)S(1)}, u32[]{:S(2)}, u32[]{:S(2)}) collective-permute-start(f32[8,2,2,4,256]{4,3,2,1,0:T(4,128)S(1)} %get-tuple-element.20), channel_id=1, source_target_pairs={{0,7},{1,0},{2,1},{3,2},{4,3},{5,4},{6,5},{7,6},{8,15},{9,8},{10,9... | collective-permute-start | bytes 393224 | tf_op jit(solution)/shard_map/ppermute | solution.py:15
  6.3 7.1 %collective-permute-start = (f32[8,2,2,4,256]{4,3,2,1,0:T(4,128)S(1)}, f32[8,2,2,4,256]{4,3,2,1,0:T(4,128)S(1)}, u32[]{:S(2)}, u32[]{:S(2)}) collective-permute-start(f32[8,2,2,4,256]{4,3,2,1,0:T(4,128)S(1)} %get-tuple-element.19), channel_id=1, source_target_pairs={{0,1},{1,2},{2,3},{3,4},{4,5},{5,6},{6,7},{7,0},{8,9},{9,10},{10,1... | collective-permute-start | bytes 393224 | tf_op jit(solution)/shard_map/ppermute | solution.py:15
  16.1 28.8 %copy-start.1 = (f32[4,2,32,512]{3,2,1,0:T(8,128)S(1)}, f32[4,2,32,512]{3,2,1,0:T(8,128)}, u32[]{:S(2)}) copy-start(f32[4,2,32,512]{3,2,1,0:T(8,128)} %param.11) | copy-start | bytes 1572868
  41.3 15.9 %all-to-all-start.1 = ((f32[16,2,4,8,128]{4,3,2,1,0:T(8,128)}), f32[16,2,4,8,128]{4,3,2,1,0:T(8,128)S(1)}, u32[]{:S(2)}, u32[]{:S(2)}) async-start(f32[16,2,4,8,128]{4,3,2,1,0:T(8,128)} %bitcast.81), calls=%async_computation.1 | async-start | bytes 1048576 | tf_op jit(solution)/shard_map/all_to_all | solution.py:112
  60.6 7.1 %collective-permute-start.2 = (f32[8,2,2,4,256]{4,3,2,1,0:T(4,128)S(1)}, f32[8,2,2,4,256]{4,3,2,1,0:T(4,128)S(1)}, u32[]{:S(2)}, u32[]{:S(2)}) collective-permute-start(f32[8,2,2,4,256]{4,3,2,1,0:T(4,128)S(1)} %get-tuple-element.9), channel_id=1, source_target_pairs={{0,1},{1,2},{2,3},{3,4},{4,5},{5,6},{6,7},{7,0},{8,9},{9,10},{10,1... | collective-permute-start | bytes 393224 | tf_op jit(solution)/shard_map/ppermute | solution.py:15
  60.7 7.1 %collective-permute-start.3 = (f32[8,2,2,4,256]{4,3,2,1,0:T(4,128)S(1)}, f32[8,2,2,4,256]{4,3,2,1,0:T(4,128)S(1)}, u32[]{:S(2)}, u32[]{:S(2)}) collective-permute-start(f32[8,2,2,4,256]{4,3,2,1,0:T(4,128)S(1)} %get-tuple-element.10), channel_id=1, source_target_pairs={{0,7},{1,0},{2,1},{3,2},{4,3},{5,4},{6,5},{7,6},{8,15},{9,8},{10,9... | collective-permute-start | bytes 393224 | tf_op jit(solution)/shard_map/ppermute | solution.py:15
where the time goes:
time: 69.4 us; the launch traced here: 68.7 us
  waiting for transfers between devices  20 us (29%)
  blocking collectives  19 us (27%)
  starting transfers between devices  12.9 us (19%)
  Pallas kernels  6.08 us (9%)
  local copies, waits for them, and re-layouts  5.03 us (7%)
  matrix products  3.16 us (5%)
  other arithmetic  2.21 us (3%)
    all_to_all x1, blocking collectives, on_device(): lax.all_to_all(packed, 'clus', 0, 0)  19 us
    all_to_all x1, waiting for transfers between devices, on_device(): local = lax.all_to_all(summed, 'clus', 0, 0)  12.2 us
    ppermute x4, starting transfers between devices, shifted_ring(): lax.ppermute(value, axis, [(i, (i + step) % count) for i in range(count)])  9.34 us
    ppermute x4, waiting for transfers between devices, shifted_ring(): lax.ppermute(value, axis, [(i, (i + step) % count) for i in range(count)])  7.89 us
    pallas_call x1, Pallas kernels, translate(): pl.pallas_call(translate_kernel, out_shape=jax.ShapeDtypeStruct(field.sha...  6.08 us
    all_to_all x1, starting transfers between devices, on_device(): local = lax.all_to_all(summed, 'clus', 0, 0)  3.57 us
  transfers between devices with their start and end apart: 5, of which 4 were waited for; matrix products, arithmetic and copies ran while one was open for 3% of the time, Pallas kernels for 0%

commit v1 on v0

v1 whole, which is shorter than its diff:
```python
import jax
import jax.numpy as jnp
from jax import lax
from jax.experimental import pallas as pl
from jax.experimental.pallas import tpu as pltpu
from jax.sharding import PartitionSpec as P

KIDS = 4
LIST = 32
GROUP = 4
HIGH = lax.Precision.HIGH


def shifted_ring(value, axis, step):
    count = lax.axis_size(axis)
    return lax.ppermute(value, axis, [(i, (i + step) % count) for i in range(count)])


def complex_times(left_side, right_side):
    real_part = (
        left_side[..., 0, :, :] * right_side[..., 0, :, :]
        - left_side[..., 1, :, :] * right_side[..., 1, :, :]
    )
    imag_part = (
        left_side[..., 0, :, :] * right_side[..., 1, :, :]
        + left_side[..., 1, :, :] * right_side[..., 0, :, :]
    )
    return jnp.stack([real_part, imag_part], axis=-3)


def band_table(theta_band, child_rows):
    parent_rows = theta_band.shape[0]
    row_index = jnp.arange(parent_rows, dtype=jnp.int32)
    column_index = jnp.arange(child_rows + 8, dtype=jnp.int32)
    table = jnp.zeros((parent_rows, child_rows + 8), jnp.float32)
    for tap_index in range(8):
        target = row_index // 2 + tap_index + 1
        hits = (column_index[None, :] == target[:, None]).astype(jnp.float32)
        table = table + theta_band[:, tap_index][:, None] * hits
    return table


def translate_kernel(source_ref, offset_ref, steps_ref, field_ref, operator_ref, out_ref):
    pairs = steps_ref.shape[0]

    def one_pair(pair, carry):
        def some_slots(step, sums):
            sums = list(sums)
            for member in range(2):
                for lane in range(GROUP):
                    slot = pair * (2 * LIST) + step * GROUP + (member * LIST + lane)
                    source = pl.multiple_of(source_ref[slot], 8)
                    offset = pl.multiple_of(offset_ref[slot], 8)
                    real = operator_ref[pl.ds(offset, 8), :]
                    imag = operator_ref[pl.ds(offset + 8, 8), :]
                    for pol in range(2):
                        at = member * 4 + pol * 2
                        a = field_ref[pl.ds(source + pol * 16, 8), :]
                        b = field_ref[pl.ds(source + (pol * 16 + 8), 8), :]
                        sums[at] = sums[at] + (real * a - imag * b)
                        sums[at + 1] = sums[at + 1] + (real * b + imag * a)
            return tuple(sums)

        zero = jnp.zeros((8, 128), jnp.float32)
        sums = lax.fori_loop(0, steps_ref[pair], some_slots, (zero,) * 8)
        for index in range(8):
            out_ref[pl.ds(pl.multiple_of(pair * 64 + index * 8, 8), 8), :] = sums[index]
        return carry

    lax.fori_loop(0, pairs, one_pair, 0)


def translate(field, translators, far_source, far_offset, far_count):
    parents, slots = far_source.shape
    kinds, _, rows, samples = translators.shape
    operators = translators.reshape(kinds, 2, rows, samples // 128, 128).transpose(0, 1, 3, 2, 4)
    operators = jnp.pad(operators.reshape(kinds * 16, 128), ((0, 16), (0, 0)))
    live = jnp.arange(slots, dtype=jnp.int32)[None, :] < far_count[:, None]
    source = (far_source * 32).reshape(-1)
    offset = (jnp.where(live, far_offset, kinds) * 16).reshape(-1)
    longest = jnp.max(far_count.reshape(parents // 2, 2), axis=1)
    steps = (longest + (GROUP - 1)) // GROUP
    smem = pl.BlockSpec(memory_space=pltpu.SMEM)
    vmem = pl.BlockSpec(memory_space=pltpu.VMEM)
    return pl.pallas_call(
        translate_kernel,
        out_shape=jax.ShapeDtypeStruct((parents * 32, 128), jnp.float32),
        in_specs=[smem, smem, smem, vmem, vmem],
        out_specs=vmem,
        name="translate",
    )(source, offset, steps, field.reshape(parents * 32, 128), operators)


def on_device(
    children, theta_band, phi_interp, child_shift, translators, far_source, far_offset, far_count
):
    child_rows = children.shape[3]
    groups = lax.axis_size("clus")
    strips = lax.axis_size("theta")
    strip = lax.axis_index("theta")
    parents_here = children.shape[0] // KIDS
    rows = translators.shape[2]
    blocks = translators.shape[3] // 128
    first = (strip > 0).astype(jnp.float32)
    last = (strip < strips - 1).astype(jnp.float32)
    table = band_table(theta_band, child_rows)
    own_table = table[:, 4 : 4 + child_rows]
    edge_table = jnp.concatenate([table[:8], table[-8:]], axis=0)
    edge_table = jnp.concatenate([edge_table[:, :4], edge_table[:, -4:]], axis=1)
    edge_shift = jnp.concatenate([child_shift[:, :, :8], child_shift[:, :, -8:]], axis=2)
    above = shifted_ring(children[:, :, :, child_rows - 4 :], "theta", 1) * first
    below = shifted_ring(children[:, :, :, :4], "theta", -1) * last

    def pack(parents):
        strips_in = parents.shape[3] // rows
        packed = parents.reshape(parents_here, 2, 2, strips_in, rows, blocks, 128)
        packed = packed.transpose(3, 0, 1, 2, 5, 4, 6)
        return packed.reshape(strips_in, parents_here, 4, 8, 128)

    def unpack(packed):
        strips_in = packed.shape[0]
        local = packed.reshape(strips_in, parents_here, 2, 2, blocks, rows, 128)
        local = local.transpose(1, 2, 3, 0, 5, 4, 6)
        return local.reshape(parents_here, 2, 2, strips_in * rows, blocks * 128)

    def gathered(fine, shift):
        grouped = fine.reshape((parents_here, KIDS) + fine.shape[1:])
        return pack(jnp.sum(complex_times(shift[None, :, None], grouped), axis=1))

    def scattered(packed, shift):
        conjugate = jnp.stack([shift[:, 0], -shift[:, 1]], axis=1)
        shifted = complex_times(conjugate[None, :, None], unpack(packed)[:, None])
        return shifted.reshape((parents_here * KIDS,) + shifted.shape[2:])

    spread = jnp.einsum("rj,...jq->...rq", own_table, children, precision=HIGH)
    fine = jnp.einsum("...q,qp->...p", spread, phi_interp, precision=HIGH)
    packed = gathered(fine, child_shift)
    edge = jnp.concatenate([above, below], axis=3)
    edge_fine = jnp.einsum("...q,qp->...p", edge, phi_interp, precision=HIGH)
    edge_fine = jnp.einsum("rj,...jp->...rp", edge_table, edge_fine, precision=HIGH)
    edge_packed = gathered(edge_fine, edge_shift)
    half = edge_packed.shape[0] // 2
    packed = jnp.concatenate(
        [packed[:half] + edge_packed[:half], packed[half:-half], packed[-half:] + edge_packed[half:]]
    )
    field = lax.all_to_all(packed, "clus", 0, 0)
    summed = translate(field, translators, far_source, far_offset, far_count)
    summed = summed.reshape(groups, parents_here, 4, 8, 128)
    local = lax.all_to_all(summed, "clus", 0, 0)
    edge_local = jnp.concatenate([local[:half], local[-half:]])
    edge_shifted = scattered(edge_local, edge_shift)
    edge_back = jnp.einsum("rj,...rp->...jp", edge_table, edge_shifted, precision=HIGH)
    edge_back = jnp.einsum("...p,qp->...q", edge_back, phi_interp, precision=HIGH)
    from_below = shifted_ring(edge_back[..., 4:, :], "theta", 1) * first
    from_above = shifted_ring(edge_back[..., :4, :], "theta", -1) * last
    back_phi = jnp.einsum("...p,qp->...q", scattered(local, child_shift), phi_interp, precision=HIGH)
    own_part = jnp.einsum("rj,...rq->...jq", own_table, back_phi, precision=HIGH)
    lead = [(0, 0)] * (own_part.ndim - 2)
    result = own_part + jnp.pad(from_below, lead + [(0, child_rows - 4), (0, 0)])
    result = result + jnp.pad(from_above, lead + [(child_rows - 4, 0), (0, 0)])
    return result


def solution(mesh):
    return jax.shard_map(
        on_device,
        mesh=mesh,
        in_specs=(
            P("clus", None, None, "theta", None),
            P("theta", None),
            P(),
            P(None, None, "theta", None),
            P(None, None, ("theta", "clus"), None),
            P(),
            P(),
            P(),
        ),
        out_specs=P("clus", None, None, "theta", None),
        check_vma=False,
    )
```

time: 69.4 us -> 69.2 us (level)
  blocking collectives: 19 us -> 0 us
  waiting for transfers between devices: 20 us -> 27.4 us
  starting transfers between devices: 12.9 us -> 17.7 us
  local copies, waits for them, and re-layouts: 5.03 us -> 9.22 us
  matrix products: 3.16 us -> 6.77 us
  Pallas kernels: 6.08 us -> 4.07 us
  other arithmetic: 2.21 us -> 3.03 us
    all_to_all x1 -> x0, blocking collectives: 19 us -> none  [on_device(): lax.all_to_all(packed, 'clus', 0, 0)]
    all_to_all x0 -> x1, waiting for transfers between devices: none -> 9.34 us  [on_device(): field = lax.all_to_all(packed, 'clus', 0, 0)]
    all_to_all x0 -> x1, starting transfers between devices: none -> 6.74 us  [on_device(): field = lax.all_to_all(packed, 'clus', 0, 0)]
    dot_general x3 -> x7, matrix products: 2.13 us -> 5.74 us  [the longest x1 1.65 us: on_device(): spread = jnp.einsum('rj,...jq->...rq', own_table, children, precision=HIGH)]
    pallas_call x1, Pallas kernels: 6.08 us -> 4.07 us  [translate(): pl.pallas_call(translate_kernel, out_shape=jax.ShapeDtypeStruct((parents...]
    ppermute x4, waiting for transfers between devices: 7.89 us -> 5.89 us  [shifted_ring(): lax.ppermute(value, axis, [(i, (i + step) % count) for i in range(count)])]
    ppermute x4, starting transfers between devices: 9.34 us -> 7.37 us  [shifted_ring(): lax.ppermute(value, axis, [(i, (i + step) % count) for i in range(count)])]
    unnamed x6 -> x14, local copies, waits for them, and re-layouts: 0.01 us -> 1.35 us
  transfers between devices with their start and end apart: 5 -> 6, of which waited for: 4 -> 5; matrix products, arithmetic and copies ran while one was open for 3% -> 15% of each run, Pallas kernels for 0% -> 0%
where the time goes in v1:
time: 69.2 us; the launch traced here: 68.7 us
  waiting for transfers between devices  27.4 us (40%)
  starting transfers between devices  17.7 us (26%)
  local copies, waits for them, and re-layouts  9.22 us (13%)
  matrix products  6.77 us (10%)
  Pallas kernels  4.07 us (6%)
  other arithmetic  3.03 us (4%)
    all_to_all x1, waiting for transfers between devices, on_device(): local = lax.all_to_all(summed, 'clus', 0, 0)  12.2 us
    all_to_all x1, waiting for transfers between devices, on_device(): field = lax.all_to_all(packed, 'clus', 0, 0)  9.34 us
    ppermute x4, starting transfers between devices, shifted_ring(): lax.ppermute(value, axis, [(i, (i + step) % count) for i in range(count)])  7.37 us
    all_to_all x1, starting transfers between devices, on_device(): field = lax.all_to_all(packed, 'clus', 0, 0)  6.74 us
    ppermute x4, waiting for transfers between devices, shifted_ring(): lax.ppermute(value, axis, [(i, (i + step) % count) for i in range(count)])  5.89 us
    pallas_call x1, Pallas kernels, translate(): pl.pallas_call(translate_kernel, out_shape=jax.ShapeDtypeStruct((parents...  4.07 us
    all_to_all x1, starting transfers between devices, on_device(): local = lax.all_to_all(summed, 'clus', 0, 0)  3.57 us
    dot_general x1, matrix products, on_device(): spread = jnp.einsum('rj,...jq->...rq', own_table, children, precision=HIGH)  1.65 us
  transfers between devices with their start and end apart: 6, of which 5 were waited for; matrix products, arithmetic and copies ran while one was open for 15% of the time, Pallas kernels for 0%

profile of v1, /device:TPU:0, one launch (start us, length us, event | category | flops | bytes accessed | tf_op | source)
XLA Modules:
  0.0 68.7 jit_solution(8515679812082306201)
XLA Ops:
  0.0 1.2 %fusion.29 = (f32[8,2,2,4,256]{4,3,2,1,0:T(4,128)S(1)}, f32[8,2,2,4,256]{4,3,2,1,0:T(4,128)S(1)}) fusion(f32[8,2,2,16,256]{4,3,2,1,0:T(8,128)} %param.8), kind=kLoop, calls=%fused_computation.112 | loop fusion | bytes 524288 | tf_op jit(solution)/shard_map/slice | solution.py:111
  1.2 5.1 %collective-permute-start.1 = (f32[8,2,2,4,256]{4,3,2,1,0:T(4,128)S(1)}, f32[8,2,2,4,256]{4,3,2,1,0:T(4,128)S(1)}, u32[]{:S(2)}, u32[]{:S(2)}) collective-permute-start(f32[8,2,2,4,256]{4,3,2,1,0:T(4,128)S(1)} %get-tuple-element.28), channel_id=1, source_target_pairs={{0,7},{1,0},{2,1},{3,2},{4,3},{5,4},{6,5},{7,6},{8,15},{9,8},{10,9... | collective-permute-start | bytes 393224 | tf_op jit(solution)/shard_map/ppermute | solution.py:16
  6.4 1.0 %slice_bitcast_fusion.24 = (f32[32]{0:T(128)S(1)}, f32[32]{0:T(128)S(1)}, f32[32]{0:T(128)S(1)}, f32[32]{0:T(128)S(1)}, f32[32]{0:T(128)S(1)}, /*index=5*/f32[32]{0:T(128)S(1)}, f32[32]{0:T(128)S(1)}, f32[32]{0:T(128)S(1)}) fusion(f32[32,8]{0,1:T(8,128)} %param.9), kind=kLoop, calls=%fused_computation.97 | loop fusion | bytes 2048 | tf_op jit(solution)/shard_map/mul | solution.py:39
  7.4 1.6 %convolution_bitcast_fusion = f32[8,2,2,32,256]{4,3,2,1,0:T(8,128)S(1)} fusion(f32[8,2,2,16,256]{4,3,2,1,0:T(8,128)} %param.8, f32[32,24]{0,1:T(8,128)S(1)} %select_add_fusion), kind=kOutput, calls=%fused_computation.5 | convolution fusion | flops 25165824 | bytes 1581056 | tf_op jit(solution)/shard_map/rj,...jq->...rq/dot_general | solution.py:135
  9.3 0.5 copy-done.4
  9.9 1.0 %fusion.12 = f32[8,2,2,32,512]{4,3,2,1,0:T(8,128)S(1)} fusion(f32[8,2,2,32,256]{4,3,2,1,0:T(8,128)S(1)} %convolution_bitcast_fusion, f32[256,512]{1,0:T(8,128)S(1)} %copy-done), kind=kOutput, calls=%fused_computation.23 | convolution fusion | flops 805306368 | bytes 3670016 | tf_op jit(solution)/shard_map/...q,qp->...p/dot_general | solution.py:136
  10.9 0.5 multiply_subtract_fusion.1
  11.4 0.2 maximum_reduce_fusion
  11.6 0.2 reshape.222
  11.9 0.1 fusion.22
  12.0 1.4 %collective-permute-done = f32[8,2,2,4,256]{4,3,2,1,0:T(4,128)S(1)} collective-permute-done((f32[8,2,2,4,256]{4,3,2,1,0:T(4,128)S(1)}, f32[8,2,2,4,256]{4,3,2,1,0:T(4,128)S(1)}, u32[]{:S(2)}, u32[]{:S(2)}) %collective-permute-start) | collective-permute-done | bytes 131104 | tf_op jit(solution)/shard_map/ppermute | solution.py:16
  13.4 0.4 fusion.10
  13.8 0.7 fusion.32
  14.5 0.2 multiply_subtract_fusion.3
  14.7 0.1 maximum_reduce_fusion.1
  14.8 0.1 reshape.224
  15.1 0.1 copy.25
  15.3 0.1 copy.24
  15.4 0.1 pad_maximum_fusion
  15.5 1.0 %copy.26 = f32[16,2,4,8,128]{4,3,2,1,0:T(8,128)} copy(f32[16,2,4,8,128]{4,0,3,2,1:T(8,128)S(1)} %pad_maximum_fusion) | data formatting | bytes 1048576 | tf_op jit(solution)/shard_map/concatenate | solution.py:143
  16.4 6.7 %all-to-all-start = ((f32[16,2,4,8,128]{4,3,2,1,0:T(8,128)}), f32[16,2,4,8,128]{4,3,2,1,0:T(8,128)S(1)}, u32[]{:S(2)}, u32[]{:S(2)}) async-start(f32[16,2,4,8,128]{4,3,2,1,0:T(8,128)} %copy.26), calls=%async_computation | async-start | bytes 1048576 | tf_op jit(solution)/shard_map/all_to_all | solution.py:146
  23.2 0.1 reshape.220
  23.3 0.7 reshape.218.source_ref
  23.9 0.7 reshape.219.offset_ref
  24.6 0.1 reduce_max.9
  24.7 0.8 %pad.12.operator_ref = f32[656,128]{1,0:T(8,128)} pad(f32[640,128]{1,0:T(8,128)S(1)} %bitcast.152, f32[]{:T(128)} %constant.95.clone.1), padding=0_16x0_0 | pad | bytes 663556 | tf_op jit(solution)/shard_map/jit(_pad)/pad | solution.py:77
  25.6 0.6 and_select_fusion.1.steps_ref
  26.2 9.3 %all-to-all-done = f32[16,2,4,8,128]{4,3,2,1,0:T(8,128)S(1)} async-done(((f32[16,2,4,8,128]{4,3,2,1,0:T(8,128)}), f32[16,2,4,8,128]{4,3,2,1,0:T(8,128)S(1)}, u32[]{:S(2)}, u32[]{:S(2)}) %all-to-all-start) | async-done | bytes 524320 | tf_op jit(solution)/shard_map/all_to_all | solution.py:146
  35.5 0.8 %copy-done.2 = f32[16,2,4,8,128]{4,3,2,1,0:T(8,128)} copy-done((f32[16,2,4,8,128]{4,3,2,1,0:T(8,128)}, f32[16,2,4,8,128]{4,3,2,1,0:T(8,128)S(1)}, u32[]{:S(2)}) %copy-start.2) | copy-done | bytes 524312
  36.3 4.1 %translate.1 = f32[1024,128]{1,0:T(8,128)} custom-call(s32[1024]{0:T(1024)} %reshape.218.source_ref, s32[1024]{0:T(1024)} %reshape.219.offset_ref, s32[16]{0:T(128)} %and_select_fusion.1.steps_ref, f32[1024,128]{1,0:T(8,128)} %bitcast.135, f32[656,128]{1,0:T(8,128)} %pad.12.operator_ref), custom_call_target="tpu_custom_call" | custom-call | tf_op jit(solution)/shard_map/translate/pallas_call | solution.py:85
  40.4 3.6 %all-to-all-start.1 = ((f32[16,2,4,8,128]{4,3,2,1,0:T(8,128)}), f32[16,2,4,8,128]{4,3,2,1,0:T(8,128)S(1)}, u32[]{:S(2)}, u32[]{:S(2)}) async-start(f32[16,2,4,8,128]{4,3,2,1,0:T(8,128)} %bitcast.136), calls=%async_computation.1 | async-start | bytes 1048576 | tf_op jit(solution)/shard_map/all_to_all | solution.py:149
  44.0 12.2 %all-to-all-done.1 = f32[16,2,4,8,128]{4,3,2,1,0:T(8,128)S(1)} async-done(((f32[16,2,4,8,128]{4,3,2,1,0:T(8,128)}), f32[16,2,4,8,128]{4,3,2,1,0:T(8,128)S(1)}, u32[]{:S(2)}, u32[]{:S(2)}) %all-to-all-start.1) | async-done | bytes 524320 | tf_op jit(solution)/shard_map/all_to_all | solution.py:149
  56.2 0.3 copy.28
  56.7 0.1 copy.32
  56.8 0.1 broadcast_in_dim_reshape.7
  57.1 0.2 multiply_subtract_fusion.2
  57.3 0.4 convolution_bitcast_fusion.1
  57.8 0.4 fusion.7
  58.2 2.2 %collective-permute-start.3 = (f32[8,2,2,4,256]{4,3,2,1,0:T(4,128)S(1)}, f32[8,2,2,4,256]{4,3,2,1,0:T(4,128)S(1)}, u32[]{:S(2)}, u32[]{:S(2)}) collective-permute-start(f32[8,2,2,4,256]{4,3,2,1,0:T(4,128)S(1)} %get-tuple-element.30), channel_id=1, source_target_pairs={{0,7},{1,0},{2,1},{3,2},{4,3},{5,4},{6,5},{7,6},{8,15},{9,8},{10,9... | collective-permute-start | bytes 393224 | tf_op jit(solution)/shard_map/ppermute | solution.py:16
  60.4 0.3 copy.29
  60.8 0.2 broadcast_in_dim_reshape.6
  61.1 0.1 mul.437
  61.2 0.1 mul.429
  61.4 0.5 multiply_subtract_fusion
  62.0 1.0 %fusion = f32[8,2,2,32,256]{4,3,2,1,0:T(8,128)S(1)} fusion(f32[8,2,1,32,512]{4,3,2,1,0:T(8,128)S(1)} %get-tuple-element.6, f32[8,2,1,32,512]{4,3,2,1,0:T(8,128)S(1)} %get-tuple-element.5, f32[256,512]{1,0:T(8,128)S(1)} %copy-done), kind=kOutput, calls=%fused_computation.1 | convolution fusion | flops 805830656 | bytes 3670016 | tf_op jit(solution)/shard_map/...p,qp->...q/dot_general | solution.py:156
  63.0 0.3 collective-permute-done.3
  63.3 4.2 %collective-permute-done.2 = f32[8,2,2,4,256]{4,3,2,1,0:T(4,128)S(1)} collective-permute-done((f32[8,2,2,4,256]{4,3,2,1,0:T(4,128)S(1)}, f32[8,2,2,4,256]{4,3,2,1,0:T(4,128)S(1)}, u32[]{:S(2)}, u32[]{:S(2)}) %collective-permute-start.2) | collective-permute-done | bytes 131104 | tf_op jit(solution)/shard_map/ppermute | solution.py:16
  67.5 1.2 %pad_add_fusion = f32[8,2,2,16,256]{4,3,2,1,0:T(8,128)} fusion(f32[8,2,2,4,256]{4,3,2,1,0:T(4,128)S(1)} %bitcast.146, f32[8,2,2,4,256]{4,3,2,1,0:T(4,128)S(1)} %bitcast.147, f32[8,2,2,32,256]{4,3,2,1,0:T(8,128)S(1)} %fusion, f32[32,24]{0,1:T(8,128)S(1)} %select_add_fusion), kind=kOutput, calls=%fused_computation.25 | convolution fusion | flops 25427968 | bytes 1843200 | tf_op jit(solution)/shard_map/rj,...rq->...jq/dot_general | solution.py:157
  (53 shorter events, 1.3 us)
Async XLA Ops:
  0.0 9.9 %copy-start = (f32[256,512]{1,0:T(8,128)S(1)}, f32[256,512]{1,0:T(8,128)}, u32[]{:S(2)}) copy-start(f32[256,512]{1,0:T(8,128)} %param.10) | copy-start | bytes 1572868
  0.0 9.1 %copy-start.1 = (f32[4,2,32,512]{3,2,1,0:T(8,128)S(1)}, f32[4,2,32,512]{3,2,1,0:T(8,128)}, u32[]{:S(2)}) copy-start(f32[4,2,32,512]{3,2,1,0:T(8,128)} %param.11) | copy-start | bytes 1572868
  1.2 10.8 %collective-permute-start.1 = (f32[8,2,2,4,256]{4,3,2,1,0:T(4,128)S(1)}, f32[8,2,2,4,256]{4,3,2,1,0:T(4,128)S(1)}, u32[]{:S(2)}, u32[]{:S(2)}) collective-permute-start(f32[8,2,2,4,256]{4,3,2,1,0:T(4,128)S(1)} %get-tuple-element.28), channel_id=1, source_target_pairs={{0,7},{1,0},{2,1},{3,2},{4,3},{5,4},{6,5},{7,6},{8,15},{9,8},{10,9... | collective-permute-start | bytes 393224 | tf_op jit(solution)/shard_map/ppermute | solution.py:16
  6.3 7.1 %collective-permute-start = (f32[8,2,2,4,256]{4,3,2,1,0:T(4,128)S(1)}, f32[8,2,2,4,256]{4,3,2,1,0:T(4,128)S(1)}, u32[]{:S(2)}, u32[]{:S(2)}) collective-permute-start(f32[8,2,2,4,256]{4,3,2,1,0:T(4,128)S(1)} %get-tuple-element.27), channel_id=1, source_target_pairs={{0,1},{1,2},{2,3},{3,4},{4,5},{5,6},{6,7},{7,0},{8,9},{9,10},{10,1... | collective-permute-start | bytes 393224 | tf_op jit(solution)/shard_map/ppermute | solution.py:16
  9.1 0.7 %copy-start.4 = (s32[32,32]{1,0:T(8,128)S(1)}, s32[32,32]{1,0:T(8,128)}, u32[]{:S(2)}) copy-start(s32[32,32]{1,0:T(8,128)} %param.14) | copy-start | bytes 12292
  9.1 0.7 %copy-start.6 = (s32[32]{0:T(128)S(1)}, s32[32]{0:T(128)}, u32[]{:S(2)}) copy-start(s32[32]{0:T(128)} %param.15) | copy-start | bytes 388
  15.0 8.2 %copy-start.5 = (s32[32,32]{1,0:T(8,128)S(1)}, s32[32,32]{1,0:T(8,128)}, u32[]{:S(2)}) copy-start(s32[32,32]{1,0:T(8,128)} %param.13) | copy-start | bytes 12292
  15.0 9.7 %copy-start.3 = (f32[40,2,2,512]{3,2,1,0:T(2,128)S(1)}, f32[40,2,2,512]{3,2,1,0:T(2,128)}, u32[]{:S(2)}) copy-start(f32[40,2,2,512]{3,2,1,0:T(2,128)} %param.12) | copy-start | bytes 983044
  16.4 19.1 %all-to-all-start = ((f32[16,2,4,8,128]{4,3,2,1,0:T(8,128)}), f32[16,2,4,8,128]{4,3,2,1,0:T(8,128)S(1)}, u32[]{:S(2)}, u32[]{:S(2)}) async-start(f32[16,2,4,8,128]{4,3,2,1,0:T(8,128)} %copy.26), calls=%async_computation | async-start | bytes 1048576 | tf_op jit(solution)/shard_map/all_to_all | solution.py:146
  35.5 0.8 %copy-start.2 = (f32[16,2,4,8,128]{4,3,2,1,0:T(8,128)}, f32[16,2,4,8,128]{4,3,2,1,0:T(8,128)S(1)}, u32[]{:S(2)}) copy-start(f32[16,2,4,8,128]{4,3,2,1,0:T(8,128)S(1)} %all-to-all-done) | copy-start | bytes 1572868
  40.4 15.9 %all-to-all-start.1 = ((f32[16,2,4,8,128]{4,3,2,1,0:T(8,128)}), f32[16,2,4,8,128]{4,3,2,1,0:T(8,128)S(1)}, u32[]{:S(2)}, u32[]{:S(2)}) async-start(f32[16,2,4,8,128]{4,3,2,1,0:T(8,128)} %bitcast.136), calls=%async_computation.1 | async-start | bytes 1048576 | tf_op jit(solution)/shard_map/all_to_all | solution.py:149
  58.2 5.0 %collective-permute-start.3 = (f32[8,2,2,4,256]{4,3,2,1,0:T(4,128)S(1)}, f32[8,2,2,4,256]{4,3,2,1,0:T(4,128)S(1)}, u32[]{:S(2)}, u32[]{:S(2)}) collective-permute-start(f32[8,2,2,4,256]{4,3,2,1,0:T(4,128)S(1)} %get-tuple-element.30), channel_id=1, source_target_pairs={{0,7},{1,0},{2,1},{3,2},{4,3},{5,4},{6,5},{7,6},{8,15},{9,8},{10,9... | collective-permute-start | bytes 393224 | tf_op jit(solution)/shard_map/ppermute | solution.py:16
  60.4 7.1 %collective-permute-start.2 = (f32[8,2,2,4,256]{4,3,2,1,0:T(4,128)S(1)}, f32[8,2,2,4,256]{4,3,2,1,0:T(4,128)S(1)}, u32[]{:S(2)}, u32[]{:S(2)}) collective-permute-start(f32[8,2,2,4,256]{4,3,2,1,0:T(4,128)S(1)} %get-tuple-element.29), channel_id=1, source_target_pairs={{0,1},{1,2},{2,3},{3,4},{4,5},{5,6},{6,7},{7,0},{8,9},{9,10},{10,1... | collective-permute-start | bytes 393224 | tf_op jit(solution)/shard_map/ppermute | solution.py:16

commit v2 on v1

v2 whole, which is shorter than its diff:
```python
import jax
import jax.numpy as jnp
from jax import lax
from jax.experimental import pallas as pl
from jax.experimental.pallas import tpu as pltpu
from jax.sharding import PartitionSpec as P

KIDS = 4
LIST = 32
GROUP = 4
PLANES = 32
ROWS = 32
OWN = 16
PHI = 256
SAMPLES = 512
HALF = jnp.bfloat16
WHOLE = jnp.float32


def shifted_ring(value, axis, step):
    count = lax.axis_size(axis)
    return lax.ppermute(value, axis, [(i, (i + step) % count) for i in range(count)])


def halves(value):
    high = value.astype(HALF)
    return high, (value - high.astype(WHOLE)).astype(HALF)


def dot3(left, right, contract=0):
    dims = (((1,), (contract,)), ((), ()))
    total = None
    for a, b in ((0, 0), (0, 1), (1, 0)):
        part = lax.dot_general(left[a], right[b], dims, preferred_element_type=WHOLE)
        total = part if total is None else total + part
    return total


def swap_blocks(tiles):
    sub = lax.broadcasted_iota(jnp.int32, (8, 128), 0)
    even = (sub // 2) % 2 == 0
    low = sub < 4
    a, b, c, d = tiles

    def step(first, second, shift, mask):
        one = jnp.where(mask, first, pltpu.roll(second, shift, 0))
        two = jnp.where(mask, pltpu.roll(first, 8 - shift, 0), second)
        return one, two

    a, b = step(a, b, 2, even)
    c, d = step(c, d, 2, even)
    a, c = step(a, c, 4, low)
    b, d = step(b, d, 4, low)
    return a, b, c, d


def lane_blocks(value):
    return [value[:, 128 * i : 128 * (i + 1)] for i in range(4)]


def band_tables(bands, planes, inner, outer, edge):
    shape = (planes * inner, planes * outer)
    row = lax.broadcasted_iota(jnp.int32, shape, 0)
    column = lax.broadcasted_iota(jnp.int32, shape, 1)
    child = row % inner
    parent = column % outer
    if edge:
        child = jnp.where(child < 4, child - 4, child + 12)
        parent = jnp.where(parent < 8, parent, parent + 16)
    tap = child - parent // 2 + 3
    tap = jnp.where(row // inner == column // outer, tap, -1)
    table = jnp.zeros(shape, WHOLE)
    for t in range(8):
        table = jnp.where(tap == t, jnp.broadcast_to(bands[t : t + 1], shape), table)
    return table


def own_forward_kernel(
    bands_ref, children_ref, phi_ref, shift_ref,
    packed_ref, phi_high_ref, phi_low_ref, edge_high_ref, edge_low_ref,
    back_high_ref, back_low_ref, edge_back_high_ref, edge_back_low_ref, fine_ref,
):
    phi = halves(phi_ref[...])
    phi_high_ref[...], phi_low_ref[...] = phi
    table = band_tables(bands_ref[:, :256], 8, 16, 32, False)
    back_high_ref[...], back_low_ref[...] = halves(table)
    own = halves(table.T)
    table = band_tables(bands_ref[:, 256:], 16, 8, 16, True)
    edge_back_high_ref[...], edge_back_low_ref[...] = halves(table)
    edge_high_ref[...], edge_low_ref[...] = halves(table.T)
    for group in range(4):
        rows = slice(128 * group, 128 * (group + 1))
        mixed = dot3(halves(children_ref[rows]), phi)
        fine_ref[256 * group : 256 * (group + 1)] = dot3(own, halves(mixed))
    for parent in range(2):
        for pol in range(2):
            for block in range(4):
                rows = slice(8 * block, 8 * (block + 1))
                real, imag = gathered(fine_ref, shift_ref, parent, pol, 32, 8 * block, rows)
                for part, value in enumerate((real, imag)):
                    for pair, tile in enumerate(swap_blocks(lane_blocks(value))):
                        packed_ref[4 * block + pair, parent, 2 * pol + part] = tile


def gathered(fine_ref, shift_ref, parent, pol, per_plane, first, rows):
    real = imag = None
    for kid in range(KIDS):
        at = ((parent * KIDS + kid) * 4 + pol * 2) * per_plane + first
        a = fine_ref[at : at + 8]
        b = fine_ref[at + per_plane : at + per_plane + 8]
        c = shift_ref[kid, 0, rows]
        d = shift_ref[kid, 1, rows]
        one, two = c * a - d * b, c * b + d * a
        real = one if real is None else real + one
        imag = two if imag is None else imag + two
    return real, imag


def edge_forward_kernel(
    above_ref, below_ref, phi_high_ref, phi_low_ref, edge_high_ref, edge_low_ref, shift_ref,
    packed_ref, out_ref, halo_ref, fine_ref, edge_ref, sems,
):
    middle = pltpu.make_async_copy(packed_ref.at[4:12], out_ref.at[4:12], sems.at[0])
    middle.start()
    for plane in range(PLANES):
        halo_ref[8 * plane : 8 * plane + 4] = above_ref[plane]
        halo_ref[8 * plane + 4 : 8 * plane + 8] = below_ref[plane]
    phi = (phi_high_ref[...], phi_low_ref[...])
    edge = (edge_high_ref[...], edge_low_ref[...])
    for parent in range(2):
        mixed = dot3(halves(halo_ref[128 * parent : 128 * (parent + 1)]), phi)
        fine_ref[256 * parent : 256 * (parent + 1)] = dot3(edge, halves(mixed))
    copies = []
    for side in range(2):
        rows = slice(24 * side, 24 * side + 8)
        for parent in range(2):
            for pol in range(2):
                real, imag = gathered(fine_ref, shift_ref, parent, pol, 16, 8 * side, rows)
                for part, value in enumerate((real, imag)):
                    for pair, tile in enumerate(swap_blocks(lane_blocks(value))):
                        own = packed_ref[12 * side + pair, parent, 2 * pol + part]
                        edge_ref[4 * side + pair, parent, 2 * pol + part] = own + tile
        target = out_ref.at[12 * side : 12 * side + 4]
        copy = pltpu.make_async_copy(edge_ref.at[4 * side : 4 * side + 4], target, sems.at[1 + side])
        copy.start()
        copies.append(copy)
    middle.wait()
    for copy in copies:
        copy.wait()


def spread_back(local_ref, shift_ref, parent, pol, blocks, store):
    parts = []
    for part in range(2):
        pieces = []
        for first in blocks:
            tiles = [local_ref[first + pair, parent, 2 * pol + part] for pair in range(4)]
            pieces.append(jnp.concatenate(swap_blocks(tiles), axis=1))
        parts.append(pieces)
    for kid in range(KIDS):
        real, imag = [], []
        for index, first in enumerate(blocks):
            a, b = parts[0][index], parts[1][index]
            c = shift_ref[kid, 0, 2 * first : 2 * first + 8]
            d = shift_ref[kid, 1, 2 * first : 2 * first + 8]
            real.append(c * a + d * b)
            imag.append(c * b - d * a)
        plane = (parent * KIDS + kid) * 4 + pol * 2
        store(plane, halves(jnp.concatenate(real, axis=0)))
        store(plane + 1, halves(jnp.concatenate(imag, axis=0)))


def edge_back_kernel(
    local_ref, shift_ref, phi_high_ref, phi_low_ref, table_high_ref, table_low_ref,
    up_ref, down_ref, high_ref, low_ref,
):
    phi = (phi_high_ref[...], phi_low_ref[...])
    table = (table_high_ref[...], table_low_ref[...])

    def store(plane, value):
        high_ref[16 * plane : 16 * plane + 16], low_ref[16 * plane : 16 * plane + 16] = value

    for parent in range(2):
        for pol in range(2):
            spread_back(local_ref, shift_ref, parent, pol, (0, 12), store)
        rows = slice(256 * parent, 256 * (parent + 1))
        narrowed = dot3(table, (high_ref[rows], low_ref[rows]))
        result = dot3(halves(narrowed), phi, contract=1)
        for plane in range(16):
            up_ref[16 * parent + plane] = result[8 * plane : 8 * plane + 4]
            down_ref[16 * parent + plane] = result[8 * plane + 4 : 8 * plane + 8]


def own_back_kernel(
    local_ref, shift_ref, phi_high_ref, phi_low_ref, table_high_ref, table_low_ref,
    own_ref, high_ref, low_ref,
):
    phi = (phi_high_ref[...], phi_low_ref[...])
    table = (table_high_ref[...], table_low_ref[...])

    def store(plane, value):
        high_ref[32 * plane : 32 * plane + 32], low_ref[32 * plane : 32 * plane + 32] = value

    for parent in range(2):
        for pol in range(2):
            spread_back(local_ref, shift_ref, parent, pol, (0, 4, 8, 12), store)
        for group in (2 * parent, 2 * parent + 1):
            rows = slice(256 * group, 256 * (group + 1))
            narrowed = dot3(table, (high_ref[rows], low_ref[rows]))
            own_ref[128 * group : 128 * (group + 1)] = dot3(halves(narrowed), phi, contract=1)


def translate_kernel(source_ref, offset_ref, steps_ref, field_ref, operator_ref, out_ref):
    pairs = out_ref.shape[0] // 64
    start = pl.program_id(0) * pairs

    def one_pair(index, carry):
        pair = start + index

        def some_slots(step, sums):
            sums = list(sums)
            for member in range(2):
                for lane in range(GROUP):
                    slot = pair * (2 * LIST) + step * GROUP + (member * LIST + lane)
                    source = pl.multiple_of(source_ref[slot], 8)
                    offset = pl.multiple_of(offset_ref[slot], 8)
                    real = operator_ref[pl.ds(offset, 8), :]
                    imag = operator_ref[pl.ds(offset + 8, 8), :]
                    for pol in range(2):
                        at = member * 4 + pol * 2
                        a = field_ref[pl.ds(source + pol * 16, 8), :]
                        b = field_ref[pl.ds(source + (pol * 16 + 8), 8), :]
                        sums[at] = sums[at] + (real * a - imag * b)
                        sums[at + 1] = sums[at + 1] + (real * b + imag * a)
            return tuple(sums)

        zero = jnp.zeros((8, 128), jnp.float32)
        sums = lax.fori_loop(0, steps_ref[pair], some_slots, (zero,) * 8)
        for part in range(8):
            out_ref[pl.ds(pl.multiple_of(index * 64 + part * 8, 8), 8), :] = sums[part]
        return carry

    lax.fori_loop(0, pairs, one_pair, 0)


def in_vmem(value):
    return pltpu.with_memory_space_constraint(value, pltpu.VMEM)


def call(kernel, name, outs, scratch, *operands, out_specs=None):
    vmem = pl.BlockSpec(memory_space=pltpu.VMEM)
    return pl.pallas_call(
        kernel,
        out_shape=outs,
        in_specs=[vmem] * len(operands),
        out_specs=out_specs if out_specs is not None else jax.tree.map(lambda _: vmem, outs),
        scratch_shapes=scratch,
        name=name,
    )(*[in_vmem(operand) for operand in operands])


def translate(field, translators, far_source, far_offset, far_count):
    parents, slots = far_source.shape
    kinds, _, rows, samples = translators.shape
    operators = translators.reshape(kinds, 2, rows, samples // 128, 128).transpose(0, 1, 3, 2, 4)
    operators = jnp.pad(operators.reshape(kinds * 16, 128), ((0, 16), (0, 0)))
    live = jnp.arange(slots, dtype=jnp.int32)[None, :] < far_count[:, None]
    source = (far_source * 32).reshape(-1)
    offset = (jnp.where(live, far_offset, kinds) * 16).reshape(-1)
    longest = jnp.max(far_count.reshape(parents // 2, 2), axis=1)
    steps = (longest + (GROUP - 1)) // GROUP
    smem = pl.BlockSpec(memory_space=pltpu.SMEM)
    vmem = pl.BlockSpec(memory_space=pltpu.VMEM)
    return pl.pallas_call(
        translate_kernel,
        grid=(4,),
        out_shape=jax.ShapeDtypeStruct((parents * 32, 128), jnp.float32),
        in_specs=[smem, smem, smem, vmem, vmem],
        out_specs=pl.BlockSpec((parents * 8, 128), lambda i: (i, 0)),
        name="translate",
    )(source, offset, steps, in_vmem(field.reshape(parents * 32, 128)), in_vmem(operators))


def on_device(
    children, theta_band, phi_interp, child_shift, translators, far_source, far_offset, far_count
):
    strips = lax.axis_size("theta")
    strip = lax.axis_index("theta")
    first = (strip > 0).astype(jnp.float32)
    last = (strip < strips - 1).astype(jnp.float32)
    planes = children.reshape(PLANES, OWN, PHI)
    above = shifted_ring(planes[:, OWN - 4 :], "theta", 1)
    below = shifted_ring(planes[:, :4], "theta", -1)
    taps = theta_band.T
    edge_taps = jnp.concatenate([taps[:, :8] * first, taps[:, -8:] * last], axis=1)
    bands = jnp.concatenate([jnp.tile(taps, (1, 8)), jnp.tile(edge_taps, (1, 16))], axis=1)
    half = lambda *shape: pltpu.VMEM(shape, HALF)
    whole = lambda *shape: pltpu.VMEM(shape, WHOLE)
    tables = (half(256, 512),) * 2 + (half(256, 128),) * 2 + (half(128, 256),) * 4
    packed, phi_high, phi_low, edge_high, edge_low, *backs = call(
        own_forward_kernel, "own_forward", (whole(16, 2, 4, 8, 128),) + tables,
        [whole(1024, SAMPLES)], bands, planes.reshape(-1, PHI), phi_interp, child_shift,
    )
    packed = call(
        edge_forward_kernel, "edge_forward", jax.ShapeDtypeStruct((16, 2, 4, 8, 128), WHOLE),
        [whole(256, PHI), whole(512, SAMPLES), whole(8, 2, 4, 8, 128), pltpu.SemaphoreType.DMA((3,))],
        above, below, phi_high, phi_low, edge_high, edge_low, child_shift, packed,
        out_specs=pl.BlockSpec(memory_space=pl.ANY),
    )
    field = lax.all_to_all(packed, "clus", 0, 0)
    summed = translate(field, translators, far_source, far_offset, far_count)
    local = lax.all_to_all(summed.reshape(packed.shape), "clus", 0, 0)
    up, down = call(
        edge_back_kernel, "edge_back", (whole(PLANES, 4, PHI),) * 2,
        [half(512, SAMPLES)] * 2, local, child_shift, phi_high, phi_low, backs[2], backs[3],
    )
    from_below = shifted_ring(down, "theta", 1)
    from_above = shifted_ring(up, "theta", -1)
    own = call(
        own_back_kernel, "own_back", whole(PLANES * OWN, PHI),
        [half(1024, SAMPLES)] * 2, local, child_shift, phi_high, phi_low, backs[0], backs[1],
    ).reshape(planes.shape)
    result = own + jnp.pad(from_below, ((0, 0), (0, OWN - 4), (0, 0)))
    result = result + jnp.pad(from_above, ((0, 0), (OWN - 4, 0), (0, 0)))
    return result.reshape(children.shape)


def solution(mesh):
    return jax.shard_map(
        on_device,
        mesh=mesh,
        in_specs=(
            P("clus", None, None, "theta", None),
            P("theta", None),
            P(),
            P(None, None, "theta", None),
            P(None, None, ("theta", "clus"), None),
            P(),
            P(),
            P(),
        ),
        out_specs=P("clus", None, None, "theta", None),
        check_vma=False,
    )
```

time: 69.2 us -> 64.2 us (0.928)
  waiting for transfers between devices: 27.4 us -> 10.2 us
  blocking collectives: 0 us -> 16 us
  Pallas kernels: 4.07 us -> 10.9 us
  matrix products: 6.77 us -> 0 us
  starting transfers between devices: 17.7 us -> 16.3 us
  other arithmetic: 3.03 us -> 1.77 us
  local copies, waits for them, and re-layouts: 9.22 us -> 8.49 us
    all_to_all x0 -> x1, blocking collectives: none -> 16 us  [on_device(): local = lax.all_to_all(summed.reshape(packed.shape), 'clus', 0, 0)]
    all_to_all x1 -> x0, waiting for transfers between devices: 12.2 us -> none  [on_device(): local = lax.all_to_all(summed, 'clus', 0, 0)]
    pallas_call x1 -> x5, Pallas kernels: 4.07 us -> 10.9 us  [the longest x4 6.75 us: call(): pl.pallas_call(kernel, out_shape=outs, in_specs=[vmem] * len(operands), o...]
    dot_general x8 -> x0, matrix products: 6.77 us -> none  [the longest x1 1.65 us: on_device(): spread = jnp.einsum('rj,...jq->...rq', own_table, children, precision=HIGH)]
    ppermute x4, waiting for transfers between devices: 5.89 us -> 0.11 us  [shifted_ring(): lax.ppermute(value, axis, [(i, (i + step) % count) for i in range(count)])]
    unnamed x14 -> x36, local copies, waits for them, and re-layouts: 1.35 us -> 5.75 us
    all_to_all x1 -> x0, starting transfers between devices: 3.57 us -> none  [on_device(): local = lax.all_to_all(summed, 'clus', 0, 0)]
    ppermute x4, starting transfers between devices: 7.37 us -> 9.42 us  [shifted_ring(): lax.ppermute(value, axis, [(i, (i + step) % count) for i in range(count)])]
  transfers between devices with their start and end apart: 6 -> 5, of which waited for: 5 -> 2; matrix products, arithmetic and copies ran while one was open for 15% -> 4% of each run, Pallas kernels for 0% -> 6%
where the time goes in v2:
time: 64.2 us; the launch traced here: 63.9 us
  starting transfers between devices  16.3 us (25%)
  blocking collectives  16 us (25%)
  Pallas kernels  10.9 us (17%)
  waiting for transfers between devices  10.2 us (16%)
  local copies, waits for them, and re-layouts  8.49 us (13%)
  other arithmetic  1.77 us (3%)
    all_to_all x1, blocking collectives, on_device(): local = lax.all_to_all(summed.reshape(packed.shape), 'clus', 0, 0)  16 us
    all_to_all x1, waiting for transfers between devices, on_device(): field = lax.all_to_all(packed, 'clus', 0, 0)  10.1 us
    ppermute x4, starting transfers between devices, shifted_ring(): lax.ppermute(value, axis, [(i, (i + step) % count) for i in range(count)])  9.42 us
    all_to_all x1, starting transfers between devices, on_device(): field = lax.all_to_all(packed, 'clus', 0, 0)  6.89 us
    pallas_call x4, Pallas kernels, call(): pl.pallas_call(kernel, out_shape=outs, in_specs=[vmem] * len(operands), o...  6.75 us
    unnamed x36, local copies, waits for them, and re-layouts  5.75 us
    pallas_call x1, Pallas kernels, translate(): pl.pallas_call(translate_kernel, grid=(4,), out_shape=jax.ShapeDtypeStruc...  4.14 us
  transfers between devices with their start and end apart: 5, of which 2 were waited for; matrix products, arithmetic and copies ran while one was open for 4% of the time, Pallas kernels for 6%

profile of v2, /device:TPU:0, one launch (start us, length us, event | category | flops | bytes accessed | tf_op | source)
XLA Modules:
  0.0 63.9 jit_solution(17707599343654770625)
XLA Ops:
  0.0 1.1 %fusion = (f32[32,4,256]{2,1,0:T(4,128)S(1)}, f32[32,4,256]{2,1,0:T(4,128)S(1)}) fusion(f32[32,16,256]{2,1,0:T(8,128)} %bitcast.14), kind=kLoop, calls=%fused_computation.12 | loop fusion | bytes 524288 | tf_op jit(solution)/shard_map/slice | solution.py:293
  1.1 2.1 %collective-permute-start = (f32[32,4,256]{2,1,0:T(4,128)S(1)}, f32[32,4,256]{2,1,0:T(4,128)S(1)}, u32[]{:S(2)}, u32[]{:S(2)}) collective-permute-start(f32[32,4,256]{2,1,0:T(4,128)S(1)} %get-tuple-element.28), channel_id=1, source_target_pairs={{0,1},{1,2},{2,3},{3,4},{4,5},{5,6},{6,7},{7,0},{8,9},{9,10},{10,1... | collective-permute-start | bytes 393224 | tf_op jit(solution)/shard_map/ppermute | solution.py:22
  3.2 3.1 %collective-permute-start.1 = (f32[32,4,256]{2,1,0:T(4,128)S(1)}, f32[32,4,256]{2,1,0:T(4,128)S(1)}, u32[]{:S(2)}, u32[]{:S(2)}) collective-permute-start(f32[32,4,256]{2,1,0:T(4,128)S(1)} %get-tuple-element.27), channel_id=1, source_target_pairs={{0,7},{1,0},{2,1},{3,2},{4,3},{5,4},{6,5},{7,6},{8,15},{9,8},{10,9... | collective-permute-start | bytes 393224 | tf_op jit(solution)/shard_map/ppermute | solution.py:22
  6.4 0.7 %copy-done.14 = f32[32,8]{0,1:T(8,128)S(1)} copy-done((f32[32,8]{0,1:T(8,128)S(1)}, f32[32,8]{0,1:T(8,128)}, u32[]{:S(2)}) %copy-start.14) | copy-done | bytes 1048
  7.1 0.1 slice_multiply_fusion.1
  7.1 0.1 pad_maximum_fusion.1
  7.2 0.1 tile.21
  7.3 0.1 tile.9
  7.4 0.0 copy-done
  7.4 1.0 %copy-done.3 = f32[8,2,2,16,256]{4,3,2,1,0:T(8,128)S(1)} copy-done((f32[8,2,2,16,256]{4,3,2,1,0:T(8,128)S(1)}, f32[8,2,2,16,256]{4,3,2,1,0:T(8,128)}, u32[]{:S(2)}) %copy-start.3) | copy-done | bytes 524312
  8.4 1.0 %copy-done.4 = f32[256,512]{1,0:T(8,128)S(1)} copy-done((f32[256,512]{1,0:T(8,128)S(1)}, f32[256,512]{1,0:T(8,128)}, u32[]{:S(2)}) %copy-start.4) | copy-done | bytes 524312
  9.5 2.1 %own_forward.1 = (f32[16,2,4,8,128]{4,3,2,1,0:T(8,128)S(1)}, bf16[256,512]{1,0:T(8,128)(2,1)S(1)}, bf16[256,512]{1,0:T(8,128)(2,1)S(1)}, bf16[256,128]{1,0:T(8,1...) custom-call(f32[8,512]{1,0:T(8,128)S(1)} %pad_maximum_fusion.bands_r, ...), custom_call_target="tpu_custom_call" | custom-call | tf_op jit(solution)/shard_map/own_forward/pallas_call | solution.py:252
  11.6 0.0 copy-start.5
  11.6 0.8 %copy-done.5 = f32[16,2,4,8,128]{4,3,2,1,0:T(8,128)} copy-done((f32[16,2,4,8,128]{4,3,2,1,0:T(8,128)}, f32[16,2,4,8,128]{4,3,2,1,0:T(8,128)S(1)}, u32[]{:S(2)}) %copy-start.5) | copy-done | bytes 524312
  12.4 0.0 collective-permute-done.above_ref
  12.4 0.0 collective-permute-done.1.below_ref
  12.4 0.0 copy-start.6
  12.4 1.2 %copy-done.6 = f32[16,2,4,8,128]{4,3,2,1,0:T(8,128)S(1)} copy-done((f32[16,2,4,8,128]{4,3,2,1,0:T(8,128)S(1)}, f32[16,2,4,8,128]{4,3,2,1,0:T(8,128)}, u32[]{:S(2)}) %copy-start.6) | copy-done | bytes 524312
  13.6 1.8 %edge_forward.1 = f32[16,2,4,8,128]{4,3,2,1,0:T(8,128)} custom-call(f32[32,4,256]{2,1,0:T(4,128)S(1)} %collective-permute-done.above_ref, f32[32,4,256]{2,1,0:T(4,128)S(1)} %collective-permute-done.1.below_ref, bf16[256,512]{1,0:T(8,128)(2,1)S(1)} %get-tuple-element.16.phi_high_ref, bf16[256,512]{1,0:T(8,128)(2,1)S(1)} %get-tuple-element.17.phi_low_ref, ...), custom_call_target="tpu_custom_call" | custom-call | tf_op jit(solution)/shard_map/edge_forward/pallas_call | solution.py:252
  15.4 0.0 copy-done.7
  15.5 0.0 copy-done.9
  15.5 0.0 copy-done.11
  15.5 0.0 copy-start.15
  15.5 0.0 copy-start.13
  15.5 6.9 %all-to-all-start = ((f32[16,2,4,8,128]{4,3,2,1,0:T(8,128)}), f32[16,2,4,8,128]{4,3,2,1,0:T(8,128)S(1)}, u32[]{:S(2)}, u32[]{:S(2)}) async-start(f32[16,2,4,8,128]{4,3,2,1,0:T(8,128)} %edge_forward.1), calls=%async_computation | async-start | bytes 1048576 | tf_op jit(solution)/shard_map/all_to_all | solution.py:310
  22.4 0.0 copy-done.15
  22.4 0.0 copy-start.17
  22.4 0.0 copy-start.16
  22.4 0.7 %reshape.39.source_ref = s32[1024]{0:T(1024)} reshape(s32[32,32]{1,0:T(8,128)S(1)} %broadcast_multiply_fusion) | data formatting | bytes 8192 | tf_op jit(solution)/shard_map/reshape | solution.py:268
  23.1 0.1 reshape.41
  23.2 0.0 copy-done.16
  23.2 0.1 select_multiply_fusion
  23.3 0.7 %reshape.40.offset_ref = s32[1024]{0:T(1024)} reshape(s32[32,32]{1,0:T(8,128)S(1)} %select_multiply_fusion) | data formatting | bytes 8192 | tf_op jit(solution)/shard_map/reshape | solution.py:269
  24.0 0.1 reduce_max.9
  24.1 0.6 and_select_fusion.steps_ref
  24.6 10.1 %all-to-all-done = f32[16,2,4,8,128]{4,3,2,1,0:T(8,128)S(1)} async-done(((f32[16,2,4,8,128]{4,3,2,1,0:T(8,128)}), f32[16,2,4,8,128]{4,3,2,1,0:T(8,128)S(1)}, u32[]{:S(2)}, u32[]{:S(2)}) %all-to-all-start) | async-done | bytes 524320 | tf_op jit(solution)/shard_map/all_to_all | solution.py:310
  34.7 4.1 %translate.1 = f32[1024,128]{1,0:T(8,128)} custom-call(s32[1024]{0:T(1024)} %reshape.39.source_ref, s32[1024]{0:T(1024)} %reshape.40.offset_ref, s32[16]{0:T(128)} %and_select_fusion.steps_ref, f32[1024,128]{1,0:T(8,128)S(1)} %bitcast.12, f32[656,128]{1,0:T(8,128)S(1)} %pad.12.operator_ref), custom_call_target="tpu_custom_call" | custom-call | tf_op jit(solution)/shard_map/translate/pallas_call | solution.py:274
  38.9 16.0 %all_to_all.10.local_ref = f32[16,2,4,8,128]{4,3,2,1,0:T(8,128)S(1)} all-to-all(f32[16,2,4,8,128]{4,3,2,1,0:T(8,128)} %bitcast.16), channel_id=1, replica_groups=mesh['clus'=16,'theta'=8] {'clus'}, dimensions={0} | all-to-all | bytes 1048576 | tf_op jit(solution)/shard_map/all_to_all | solution.py:312
  54.9 0.0 copy-done.1
  54.9 1.0 %edge_back.1 = (f32[32,4,256]{2,1,0:T(4,128)S(1)}, f32[32,4,256]{2,1,0:T(4,128)S(1)}) custom-call(f32[16,2,4,8,128]{4,3,2,1,0:T(8,128)S(1)} %all_to_all.10.local_ref, f32[4,2,32,512]{3,2,1,0:T(8,128)S(1)} %copy-done, bf16[256,512]{1,0:T(8,128)(2,1)S(1)} %get-tuple-element.16.phi_high_ref, bf16[256,512]{1,0:T(8,128)(2,1)S(1)} %get-tuple-element.17.phi_low_ref, ...), custom_call_target="tpu_custom_call" | custom-call | tf_op jit(solution)/shard_map/edge_back/pallas_call | solution.py:252
  55.8 0.1 collective-permute-start.2
  55.9 4.1 %collective-permute-start.3 = (f32[32,4,256]{2,1,0:T(4,128)S(1)}, f32[32,4,256]{2,1,0:T(4,128)S(1)}, u32[]{:S(2)}, u32[]{:S(2)}) collective-permute-start(f32[32,4,256]{2,1,0:T(4,128)S(1)} %get-tuple-element.26), channel_id=1, source_target_pairs={{0,7},{1,0},{2,1},{3,2},{4,3},{5,4},{6,5},{7,6},{8,15},{9,8},{10,9... | collective-permute-start | bytes 393224 | tf_op jit(solution)/shard_map/ppermute | solution.py:22
  60.0 0.0 copy-done.10
  60.0 0.9 %copy-done.2 = bf16[256,512]{1,0:T(8,128)(2,1)S(1)} copy-done((bf16[256,512]{1,0:T(8,128)(2,1)S(1)}, bf16[256,512]{1,0:T(8,128)(2,1)}, u32[]{:S(2)}) %copy-start.2) | copy-done | bytes 262168
  61.0 1.9 %own_back.1 = f32[512,256]{1,0:T(8,128)S(1)} custom-call(f32[16,2,4,8,128]{4,3,2,1,0:T(8,128)S(1)} %all_to_all.10.local_ref, f32[4,2,32,512]{3,2,1,0:T(8,128)S(1)} %copy-done, bf16[256,512]{1,0:T(8,128)(2,1)S(1)} %copy-done.2, bf16[256,512]{1,0:T(8,128)(2,1)S(1)} %get-tuple-element.17.phi_low_ref, bf16[128,256]{1,0:T(8,128)(2,1)S(1)} %copy-done.8, ...), custom_call_target="tpu_custom_call" | custom-call | tf_op jit(solution)/shard_map/own_back/pallas_call | solution.py:252
  62.9 0.1 collective-permute-done.2
  63.0 0.0 collective-permute-done.3
  63.0 0.9 %pad_add_fusion = f32[32,16,256]{2,1,0:T(8,128)} fusion(f32[32,4,256]{2,1,0:T(4,128)S(1)} %collective-permute-done.3, f32[32,16,256]{2,1,0:T(8,128)S(1)} %bitcast.13, f32[32,4,256]{2,1,0:T(4,128)S(1)} %collective-permute-done.2), kind=kLoop, calls=%fused_computation | loop fusion | flops 262144 | bytes 1310720 | tf_op jit(solution)/shard_map/add | solution.py:324
  (21 shorter events, 0.1 us)
Async XLA Ops:
  0.0 7.4 %copy-start = (f32[4,2,32,512]{3,2,1,0:T(8,128)S(1)}, f32[4,2,32,512]{3,2,1,0:T(8,128)}, u32[]{:S(2)}) copy-start(f32[4,2,32,512]{3,2,1,0:T(8,128)} %shift_ref.7) | copy-start | bytes 1572868
  1.1 11.3 %collective-permute-start = (f32[32,4,256]{2,1,0:T(4,128)S(1)}, f32[32,4,256]{2,1,0:T(4,128)S(1)}, u32[]{:S(2)}, u32[]{:S(2)}) collective-permute-start(f32[32,4,256]{2,1,0:T(4,128)S(1)} %get-tuple-element.28), channel_id=1, source_target_pairs={{0,1},{1,2},{2,3},{3,4},{4,5},{5,6},{6,7},{7,0},{8,9},{9,10},{10,1... | collective-permute-start | bytes 393224 | tf_op jit(solution)/shard_map/ppermute | solution.py:22
  3.2 9.2 %collective-permute-start.1 = (f32[32,4,256]{2,1,0:T(4,128)S(1)}, f32[32,4,256]{2,1,0:T(4,128)S(1)}, u32[]{:S(2)}, u32[]{:S(2)}) collective-permute-start(f32[32,4,256]{2,1,0:T(4,128)S(1)} %get-tuple-element.27), channel_id=1, source_target_pairs={{0,7},{1,0},{2,1},{3,2},{4,3},{5,4},{6,5},{7,6},{8,15},{9,8},{10,9... | collective-permute-start | bytes 393224 | tf_op jit(solution)/shard_map/ppermute | solution.py:22
  6.4 0.7 %copy-start.14 = (f32[32,8]{0,1:T(8,128)S(1)}, f32[32,8]{0,1:T(8,128)}, u32[]{:S(2)}) copy-start(f32[32,8]{0,1:T(8,128)} %param.9) | copy-start | bytes 3076
  7.4 1.0 %copy-start.3 = (f32[8,2,2,16,256]{4,3,2,1,0:T(8,128)S(1)}, f32[8,2,2,16,256]{4,3,2,1,0:T(8,128)}, u32[]{:S(2)}) copy-start(f32[8,2,2,16,256]{4,3,2,1,0:T(8,128)} %param.8) | copy-start | bytes 1572868
  8.4 1.0 %copy-start.4 = (f32[256,512]{1,0:T(8,128)S(1)}, f32[256,512]{1,0:T(8,128)}, u32[]{:S(2)}) copy-start(f32[256,512]{1,0:T(8,128)} %phi_ref.1) | copy-start | bytes 1572868
  11.6 0.8 %copy-start.5 = (f32[16,2,4,8,128]{4,3,2,1,0:T(8,128)}, f32[16,2,4,8,128]{4,3,2,1,0:T(8,128)S(1)}, u32[]{:S(2)}) copy-start(f32[16,2,4,8,128]{4,3,2,1,0:T(8,128)S(1)} %get-tuple-element.20.packed_ref) | copy-start | bytes 1572868
  12.4 3.1 %copy-start.7 = (bf16[128,256]{1,0:T(8,128)(2,1)}, bf16[128,256]{1,0:T(8,128)(2,1)S(1)}, u32[]{:S(2)}) copy-start(bf16[128,256]{1,0:T(8,128)(2,1)S(1)} %get-tuple-element.21.table_high_ref) | copy-start | bytes 196612
  12.4 3.1 %copy-start.9 = (bf16[128,256]{1,0:T(8,128)(2,1)}, bf16[128,256]{1,0:T(8,128)(2,1)S(1)}, u32[]{:S(2)}) copy-start(bf16[128,256]{1,0:T(8,128)(2,1)S(1)} %get-tuple-element.22.table_low_ref) | copy-start | bytes 196612
  12.4 3.1 %copy-start.11 = (bf16[128,256]{1,0:T(8,128)(2,1)}, bf16[128,256]{1,0:T(8,128)(2,1)S(1)}, u32[]{:S(2)}) copy-start(bf16[128,256]{1,0:T(8,128)(2,1)S(1)} %get-tuple-element.24.table_low_ref) | copy-start | bytes 196612
  12.4 42.5 %copy-start.1 = (bf16[256,512]{1,0:T(8,128)(2,1)}, bf16[256,512]{1,0:T(8,128)(2,1)S(1)}, u32[]{:S(2)}) copy-start(bf16[256,512]{1,0:T(8,128)(2,1)S(1)} %get-tuple-element.16.phi_high_ref) | copy-start | bytes 786436
  12.4 1.2 %copy-start.6 = (f32[16,2,4,8,128]{4,3,2,1,0:T(8,128)S(1)}, f32[16,2,4,8,128]{4,3,2,1,0:T(8,128)}, u32[]{:S(2)}) copy-start(f32[16,2,4,8,128]{4,3,2,1,0:T(8,128)} %copy-done.5) | copy-start | bytes 1572868
  15.5 6.9 %copy-start.15 = (s32[32,32]{1,0:T(8,128)S(1)}, s32[32,32]{1,0:T(8,128)}, u32[]{:S(2)}) copy-start(s32[32,32]{1,0:T(8,128)} %param.13) | copy-start | bytes 12292
  15.5 8.5 %copy-start.13 = (f32[40,2,2,512]{3,2,1,0:T(2,128)S(1)}, f32[40,2,2,512]{3,2,1,0:T(2,128)}, u32[]{:S(2)}) copy-start(f32[40,2,2,512]{3,2,1,0:T(2,128)} %param.12) | copy-start | bytes 983044
  15.5 19.2 %all-to-all-start = ((f32[16,2,4,8,128]{4,3,2,1,0:T(8,128)}), f32[16,2,4,8,128]{4,3,2,1,0:T(8,128)S(1)}, u32[]{:S(2)}, u32[]{:S(2)}) async-start(f32[16,2,4,8,128]{4,3,2,1,0:T(8,128)} %edge_forward.1), calls=%async_computation | async-start | bytes 1048576 | tf_op jit(solution)/shard_map/all_to_all | solution.py:310
  22.4 0.7 %copy-start.17 = (s32[32]{0:T(128)S(1)}, s32[32]{0:T(128)}, u32[]{:S(2)}) copy-start(s32[32]{0:T(128)} %param.15) | copy-start | bytes 388
  22.4 0.8 %copy-start.16 = (s32[32,32]{1,0:T(8,128)S(1)}, s32[32,32]{1,0:T(8,128)}, u32[]{:S(2)}) copy-start(s32[32,32]{1,0:T(8,128)} %param.14) | copy-start | bytes 12292
  38.9 16.0 %copy-start.12 = (bf16[128,256]{1,0:T(8,128)(2,1)S(1)}, bf16[128,256]{1,0:T(8,128)(2,1)}, u32[]{:S(2)}) copy-start(bf16[128,256]{1,0:T(8,128)(2,1)} %copy-done.11) | copy-start | bytes 196612
  54.9 5.2 %copy-start.8 = (bf16[128,256]{1,0:T(8,128)(2,1)S(1)}, bf16[128,256]{1,0:T(8,128)(2,1)}, u32[]{:S(2)}) copy-start(bf16[128,256]{1,0:T(8,128)(2,1)} %copy-done.7) | copy-start | bytes 196612
  54.9 5.2 %copy-start.10 = (bf16[128,256]{1,0:T(8,128)(2,1)S(1)}, bf16[128,256]{1,0:T(8,128)(2,1)}, u32[]{:S(2)}) copy-start(bf16[128,256]{1,0:T(8,128)(2,1)} %copy-done.9) | copy-start | bytes 196612
  55.8 7.1 %collective-permute-start.2 = (f32[32,4,256]{2,1,0:T(4,128)S(1)}, f32[32,4,256]{2,1,0:T(4,128)S(1)}, u32[]{:S(2)}, u32[]{:S(2)}) collective-permute-start(f32[32,4,256]{2,1,0:T(4,128)S(1)} %get-tuple-element.25), channel_id=1, source_target_pairs={{0,1},{1,2},{2,3},{3,4},{4,5},{5,6},{6,7},{7,0},{8,9},{9,10},{10,1... | collective-permute-start | bytes 393224 | tf_op jit(solution)/shard_map/ppermute | solution.py:22
  55.9 7.1 %collective-permute-start.3 = (f32[32,4,256]{2,1,0:T(4,128)S(1)}, f32[32,4,256]{2,1,0:T(4,128)S(1)}, u32[]{:S(2)}, u32[]{:S(2)}) collective-permute-start(f32[32,4,256]{2,1,0:T(4,128)S(1)} %get-tuple-element.26), channel_id=1, source_target_pairs={{0,7},{1,0},{2,1},{3,2},{4,3},{5,4},{6,5},{7,6},{8,15},{9,8},{10,9... | collective-permute-start | bytes 393224 | tf_op jit(solution)/shard_map/ppermute | solution.py:22
  60.0 1.0 %copy-start.2 = (bf16[256,512]{1,0:T(8,128)(2,1)S(1)}, bf16[256,512]{1,0:T(8,128)(2,1)}, u32[]{:S(2)}) copy-start(bf16[256,512]{1,0:T(8,128)(2,1)} %copy-done.1) | copy-start | bytes 786436

commit v3 on v2

--- a/solution.py
+++ b/solution.py
@@ -13,6 +13,7 @@
 OWN = 16
 PHI = 256
 SAMPLES = 512
+GRANT = 12 * 2**20
 HALF = jnp.bfloat16
 WHOLE = jnp.float32
 
@@ -56,6 +57,13 @@
 
 def lane_blocks(value):
     return [value[:, 128 * i : 128 * (i + 1)] for i in range(4)]
+
+
+def tiled(bands, outer):
+    row = lax.broadcasted_iota(jnp.int32, (outer, 256), 0)
+    column = lax.broadcasted_iota(jnp.int32, (outer, 256), 1)
+    pick = (row == column % outer).astype(HALF)
+    return [jnp.dot(part, pick, preferred_element_type=WHOLE) for part in halves(bands)]
 
 
 def band_tables(bands, planes, inner, outer, edge):
@@ -69,25 +77,45 @@
         parent = jnp.where(parent < 8, parent, parent + 16)
     tap = child - parent // 2 + 3
     tap = jnp.where(row // inner == column // outer, tap, -1)
-    table = jnp.zeros(shape, WHOLE)
-    for t in range(8):
-        table = jnp.where(tap == t, jnp.broadcast_to(bands[t : t + 1], shape), table)
-    return table
+    tables = []
+    for part in tiled(bands, outer):
+        table = jnp.zeros(shape, WHOLE)
+        for t in range(8):
+            table = jnp.where(tap == t, jnp.broadcast_to(part[t : t + 1], shape), table)
+        tables.append(table)
+    return tables
 
 
 def own_forward_kernel(
-    bands_ref, children_ref, phi_ref, shift_ref,
+    taps_hbm, children_hbm, phi_hbm, shift_ref,
     packed_ref, phi_high_ref, phi_low_ref, edge_high_ref, edge_low_ref,
-    back_high_ref, back_low_ref, edge_back_high_ref, edge_back_low_ref, fine_ref,
-):
+    back_high_ref, back_low_ref, edge_back_high_ref, edge_back_low_ref,
+    fine_ref, taps_ref, phi_ref, children_ref, sems,
+):
+    pairs = ((taps_hbm, taps_ref), (phi_hbm, phi_ref), (children_hbm, children_ref))
+    copies = [pltpu.make_async_copy(*pair, sems.at[i]) for i, pair in enumerate(pairs)]
+    for copy in copies:
+        copy.start()
+    strip = lax.axis_index("theta")
+    first = (strip > 0).astype(WHOLE)
+    last = (strip < lax.axis_size("theta") - 1).astype(WHOLE)
+    copies[0].wait()
+    taps = taps_ref[...]
+    table = band_tables(taps, 8, 16, 32, False)
+    own = []
+    for part, ref in zip(table, (back_high_ref, back_low_ref)):
+        ref[...] = part.astype(HALF)
+        own.append(part.T.astype(HALF))
+    taps = jnp.concatenate([taps[:, :8] * first, taps[:, ROWS - 8 :] * last], axis=1)
+    table = band_tables(taps, 16, 8, 16, True)
+    refs = ((edge_back_high_ref, edge_high_ref), (edge_back_low_ref, edge_low_ref))
+    for part, (back_ref, ref) in zip(table, refs):
+        back_ref[...] = part.astype(HALF)
+        ref[...] = part.T.astype(HALF)
+    copies[1].wait()
     phi = halves(phi_ref[...])
     phi_high_ref[...], phi_low_ref[...] = phi
-    table = band_tables(bands_ref[:, :256], 8, 16, 32, False)
-    back_high_ref[...], back_low_ref[...] = halves(table)
-    own = halves(table.T)
-    table = band_tables(bands_ref[:, 256:], 16, 8, 16, True)
-    edge_back_high_ref[...], edge_back_low_ref[...] = halves(table)
-    edge_high_ref[...], edge_low_ref[...] = halves(table.T)
+    copies[2].wait()
     for group in range(4):
         rows = slice(128 * group, 128 * (group + 1))
         mixed = dot3(halves(children_ref[rows]), phi)
@@ -247,16 +275,22 @@
     return pltpu.with_memory_space_constraint(value, pltpu.VMEM)
 
 
-def call(kernel, name, outs, scratch, *operands, out_specs=None):
+def in_hbm(value):
+    return pltpu.with_memory_space_constraint(value, pltpu.HBM)
+
+
+def call(kernel, name, outs, scratch, *operands, raw=0, out_specs=None):
     vmem = pl.BlockSpec(memory_space=pltpu.VMEM)
+    hbm = pl.BlockSpec(memory_space=pltpu.HBM)
     return pl.pallas_call(
         kernel,
         out_shape=outs,
-        in_specs=[vmem] * len(operands),
+        in_specs=[hbm] * raw + [vmem] * (len(operands) - raw),
         out_specs=out_specs if out_specs is not None else jax.tree.map(lambda _: vmem, outs),
         scratch_shapes=scratch,
+        compiler_params=pltpu.CompilerParams(vmem_limit_bytes=GRANT),
         name=name,
-    )(*[in_vmem(operand) for operand in operands])
+    )(*map(in_hbm, operands[:raw]), *map(in_vmem, operands[raw:]))
 
 
 def translate(field, translators, far_source, far_offset, far_count):
@@ -277,6 +311,7 @@
         out_shape=jax.ShapeDtypeStruct((parents * 32, 128), jnp.float32),
         in_specs=[smem, smem, smem, vmem, vmem],
         out_specs=pl.BlockSpec((parents * 8, 128), lambda i: (i, 0)),
+        compiler_params=pltpu.CompilerParams(vmem_limit_bytes=GRANT),
         name="translate",
     )(source, offset, steps, in_vmem(field.reshape(parents * 32, 128)), in_vmem(operators))
 
@@ -284,22 +319,19 @@
 def on_device(
     children, theta_band, phi_interp, child_shift, translators, far_source, far_offset, far_count
 ):
-    strips = lax.axis_size("theta")
-    strip = lax.axis_index("theta")
-    first = (strip > 0).astype(jnp.float32)
-    last = (strip < strips - 1).astype(jnp.float32)
     planes = children.reshape(PLANES, OWN, PHI)
     above = shifted_ring(planes[:, OWN - 4 :], "theta", 1)
     below = shifted_ring(planes[:, :4], "theta", -1)
-    taps = theta_band.T
-    edge_taps = jnp.concatenate([taps[:, :8] * first, taps[:, -8:] * last], axis=1)
-    bands = jnp.concatenate([jnp.tile(taps, (1, 8)), jnp.tile(edge_taps, (1, 16))], axis=1)
     half = lambda *shape: pltpu.VMEM(shape, HALF)
     whole = lambda *shape: pltpu.VMEM(shape, WHOLE)
     tables = (half(256, 512),) * 2 + (half(256, 128),) * 2 + (half(128, 256),) * 4
     packed, phi_high, phi_low, edge_high, edge_low, *backs = call(
         own_forward_kernel, "own_forward", (whole(16, 2, 4, 8, 128),) + tables,
-        [whole(1024, SAMPLES)], bands, planes.reshape(-1, PHI), phi_interp, child_shift,
+        [
+            whole(1024, SAMPLES), whole(8, ROWS), whole(PHI, SAMPLES), whole(PLANES * OWN, PHI),
+            pltpu.SemaphoreType.DMA((3,)),
+        ],
+        theta_band.T, planes.reshape(-1, PHI), phi_interp, child_shift, raw=3,
     )
     packed = call(
         edge_forward_kernel, "edge_forward", jax.ShapeDtypeStruct((16, 2, 4, 8, 128), WHOLE),

time: 64.2 us -> 58 us (0.903)
  local copies, waits for them, and re-layouts: 8.49 us -> 1.97 us
  waiting for transfers between devices: 10.2 us -> 12.4 us
  blocking collectives: 16 us -> 15 us
  other arithmetic: 1.77 us -> 1.08 us
    unnamed x36 -> x10, local copies, waits for them, and re-layouts: 5.75 us -> 0.59 us
    pallas_call x1, Pallas kernels: 4.14 us -> 2.8 us  [translate(): pl.pallas_call(translate_kernel, grid=(4,), out_shape=jax.ShapeDtypeStruc...]
    pallas_call x4, Pallas kernels: 6.75 us -> 7.97 us  [call(): pl.pallas_call(kernel, out_shape=outs, in_specs=[hbm] * raw + [vmem] * (l...]
    all_to_all x1, waiting for transfers between devices: 10.1 us -> 11.2 us  [on_device(): field = lax.all_to_all(packed, 'clus', 0, 0)]
    ppermute x4, waiting for transfers between devices: 0.11 us -> 1.16 us  [shifted_ring(): lax.ppermute(value, axis, [(i, (i + step) % count) for i in range(count)])]
    all_to_all x1, blocking collectives: 16 us -> 15 us  [on_device(): local = lax.all_to_all(summed.reshape(packed.shape), 'clus', 0, 0)]
  transfers between devices with their start and end apart: 5 -> 5, of which waited for: 2 -> 3; matrix products, arithmetic and copies ran while one was open for 4% -> 1% of each run, Pallas kernels for 6% -> 9%
where the time goes in v3:
time: 58 us; the launch traced here: 57.6 us
  starting transfers between devices  16.3 us (28%)
  blocking collectives  15 us (26%)
  waiting for transfers between devices  12.4 us (21%)
  Pallas kernels  10.8 us (19%)
  local copies, waits for them, and re-layouts  1.97 us (3%)
  other arithmetic  1.08 us (2%)
    all_to_all x1, blocking collectives, on_device(): local = lax.all_to_all(summed.reshape(packed.shape), 'clus', 0, 0)  15 us
    all_to_all x1, waiting for transfers between devices, on_device(): field = lax.all_to_all(packed, 'clus', 0, 0)  11.2 us
    ppermute x4, starting transfers between devices, shifted_ring(): lax.ppermute(value, axis, [(i, (i + step) % count) for i in range(count)])  9.43 us
    pallas_call x4, Pallas kernels, call(): pl.pallas_call(kernel, out_shape=outs, in_specs=[hbm] * raw + [vmem] * (l...  7.97 us
    all_to_all x1, starting transfers between devices, on_device(): field = lax.all_to_all(packed, 'clus', 0, 0)  6.88 us
    pallas_call x1, Pallas kernels, translate(): pl.pallas_call(translate_kernel, grid=(4,), out_shape=jax.ShapeDtypeStruc...  2.8 us
  transfers between devices with their start and end apart: 5, of which 3 were waited for; matrix products, arithmetic and copies ran while one was open for 1% of the time, Pallas kernels for 9%

profile of v3, /device:TPU:0, one launch (start us, length us, event | category | flops | bytes accessed | tf_op | source)
XLA Modules:
  0.0 57.6 jit_solution(3302435650840412885)
XLA Ops:
  0.0 0.0 copy-start
  0.0 1.1 %fusion = (f32[32,4,256]{2,1,0:T(4,128)S(1)}, f32[32,4,256]{2,1,0:T(4,128)S(1)}) fusion(f32[32,16,256]{2,1,0:T(8,128)} %bitcast.15), kind=kLoop, calls=%fused_computation.8 | loop fusion | bytes 524288 | tf_op jit(solution)/shard_map/slice | solution.py:324
  1.1 2.1 %collective-permute-start = (f32[32,4,256]{2,1,0:T(4,128)S(1)}, f32[32,4,256]{2,1,0:T(4,128)S(1)}, u32[]{:S(2)}, u32[]{:S(2)}) collective-permute-start(f32[32,4,256]{2,1,0:T(4,128)S(1)} %get-tuple-element.28), channel_id=1, source_target_pairs={{0,1},{1,2},{2,3},{3,4},{4,5},{5,6},{6,7},{7,0},{8,9},{9,10},{10,1... | collective-permute-start | bytes 393224 | tf_op jit(solution)/shard_map/ppermute | solution.py:23
  3.2 3.1 %collective-permute-start.1 = (f32[32,4,256]{2,1,0:T(4,128)S(1)}, f32[32,4,256]{2,1,0:T(4,128)S(1)}, u32[]{:S(2)}, u32[]{:S(2)}) collective-permute-start(f32[32,4,256]{2,1,0:T(4,128)S(1)} %get-tuple-element.27), channel_id=1, source_target_pairs={{0,7},{1,0},{2,1},{3,2},{4,3},{5,4},{6,5},{7,6},{8,15},{9,8},{10,9... | collective-permute-start | bytes 393224 | tf_op jit(solution)/shard_map/ppermute | solution.py:23
  6.4 0.0 copy-done
  6.4 3.3 %own_forward.1 = (f32[16,2,4,8,128]{4,3,2,1,0:T(8,128)S(1)}, bf16[256,512]{1,0:T(8,128)(2,1)S(1)}, bf16[256,512]{1,0:T(8,128)(2,1)S(1)}, bf16[256,128]{1,0:T(8,1...) custom-call(f32[8,32]{1,0:T(8,128)} %bitcast.18, ...), custom_call_target="tpu_custom_call" | custom-call | tf_op jit(solution)/shard_map/own_forward/pallas_call | solution.py:285
  9.7 0.1 collective-permute-done.above_ref
  9.8 0.0 collective-permute-done.1.below_ref
  9.8 1.8 %edge_forward.1 = f32[16,2,4,8,128]{4,3,2,1,0:T(8,128)} custom-call(f32[32,4,256]{2,1,0:T(4,128)S(1)} %collective-permute-done.above_ref, f32[32,4,256]{2,1,0:T(4,128)S(1)} %collective-permute-done.1.below_ref, bf16[256,512]{1,0:T(8,128)(2,1)S(1)} %get-tuple-element.16.phi_high_ref, bf16[256,512]{1,0:T(8,128)(2,1)S(1)} %get-tuple-element.17.phi_low_ref, ...), custom_call_target="tpu_custom_call" | custom-call | tf_op jit(solution)/shard_map/edge_forward/pallas_call | solution.py:285
  11.6 0.0 copy-start.2
  11.6 0.0 copy-start.1
  11.6 6.9 %all-to-all-start = ((f32[16,2,4,8,128]{4,3,2,1,0:T(8,128)}), f32[16,2,4,8,128]{4,3,2,1,0:T(8,128)S(1)}, u32[]{:S(2)}, u32[]{:S(2)}) async-start(f32[16,2,4,8,128]{4,3,2,1,0:T(8,128)} %edge_forward.1), calls=%async_computation | async-start | bytes 1048576 | tf_op jit(solution)/shard_map/all_to_all | solution.py:342
  18.5 0.0 copy-done.2
  18.5 0.0 copy-start.4
  18.6 0.0 copy-start.3
  18.6 0.1 reshape.31.source_ref
  18.6 0.6 copy-done.4
  19.2 0.1 reshape.33
  19.3 0.0 copy-done.3
  19.3 0.1 select_multiply_fusion
  19.4 0.1 reshape.32.offset_ref
  19.4 0.0 copy-done.1
  19.5 0.1 reduce_max.9
  19.6 11.2 %all-to-all-done = f32[16,2,4,8,128]{4,3,2,1,0:T(8,128)S(1)} async-done(((f32[16,2,4,8,128]{4,3,2,1,0:T(8,128)}), f32[16,2,4,8,128]{4,3,2,1,0:T(8,128)S(1)}, u32[]{:S(2)}, u32[]{:S(2)}) %all-to-all-start) | async-done | bytes 524320 | tf_op jit(solution)/shard_map/all_to_all | solution.py:342
  30.8 2.8 %translate.1 = f32[1024,128]{1,0:T(8,128)S(1)} custom-call(s32[1024]{0:T(1024)S(1)} %reshape.31.source_ref, s32[1024]{0:T(1024)S(1)} %reshape.32.offset_ref, s32[16]{0:T(128)S(1)} %and_select_fusion.steps_ref, f32[1024,128]{1,0:T(8,128)S(1)} %bitcast.12, f32[656,128]{1,0:T(8,128)S(1)} %pad.12.operator_ref), custom_call_target="tpu_custom_call" | custom-call | tf_op jit(solution)/shard_map/translate/pallas_call | solution.py:308
  33.7 15.0 %all_to_all.10.local_ref = f32[16,2,4,8,128]{4,3,2,1,0:T(8,128)S(1)} all-to-all(f32[16,2,4,8,128]{4,3,2,1,0:T(8,128)S(1)} %bitcast.14), channel_id=1, replica_groups=mesh['clus'=16,'theta'=8] {'clus'}, dimensions={0} | all-to-all | bytes 1048576 | tf_op jit(solution)/shard_map/all_to_all | solution.py:344
  48.6 1.0 %edge_back.1 = (f32[32,4,256]{2,1,0:T(4,128)S(1)}, f32[32,4,256]{2,1,0:T(4,128)S(1)}) custom-call(f32[16,2,4,8,128]{4,3,2,1,0:T(8,128)S(1)} %all_to_all.10.local_ref, f32[4,2,32,512]{3,2,1,0:T(8,128)S(1)} %copy-done, bf16[256,512]{1,0:T(8,128)(2,1)S(1)} %get-tuple-element.16.phi_high_ref, bf16[256,512]{1,0:T(8,128)(2,1)S(1)} %get-tuple-element.17.phi_low_ref, ...), custom_call_target="tpu_custom_call" | custom-call | tf_op jit(solution)/shard_map/edge_back/pallas_call | solution.py:285
  49.6 0.7 %collective-permute-start.2 = (f32[32,4,256]{2,1,0:T(4,128)S(1)}, f32[32,4,256]{2,1,0:T(4,128)S(1)}, u32[]{:S(2)}, u32[]{:S(2)}) collective-permute-start(f32[32,4,256]{2,1,0:T(4,128)S(1)} %get-tuple-element.25), channel_id=1, source_target_pairs={{0,1},{1,2},{2,3},{3,4},{4,5},{5,6},{6,7},{7,0},{8,9},{9,10},{10,1... | collective-permute-start | bytes 393224 | tf_op jit(solution)/shard_map/ppermute | solution.py:23
  50.3 3.5 %collective-permute-start.3 = (f32[32,4,256]{2,1,0:T(4,128)S(1)}, f32[32,4,256]{2,1,0:T(4,128)S(1)}, u32[]{:S(2)}, u32[]{:S(2)}) collective-permute-start(f32[32,4,256]{2,1,0:T(4,128)S(1)} %get-tuple-element.26), channel_id=1, source_target_pairs={{0,7},{1,0},{2,1},{3,2},{4,3},{5,4},{6,5},{7,6},{8,15},{9,8},{10,9... | collective-permute-start | bytes 393224 | tf_op jit(solution)/shard_map/ppermute | solution.py:23
  53.8 1.9 %own_back.1 = f32[512,256]{1,0:T(8,128)S(1)} custom-call(f32[16,2,4,8,128]{4,3,2,1,0:T(8,128)S(1)} %all_to_all.10.local_ref, f32[4,2,32,512]{3,2,1,0:T(8,128)S(1)} %copy-done, bf16[256,512]{1,0:T(8,128)(2,1)S(1)} %get-tuple-element.16.phi_high_ref, bf16[256,512]{1,0:T(8,128)(2,1)S(1)} %get-tuple-element.17.phi_low_ref, ...), custom_call_target="tpu_custom_call" | custom-call | tf_op jit(solution)/shard_map/own_back/pallas_call | solution.py:285
  55.7 1.0 %collective-permute-done.2 = f32[32,4,256]{2,1,0:T(4,128)S(1)} collective-permute-done((f32[32,4,256]{2,1,0:T(4,128)S(1)}, f32[32,4,256]{2,1,0:T(4,128)S(1)}, u32[]{:S(2)}, u32[]{:S(2)}) %collective-permute-start.2) | collective-permute-done | bytes 131104 | tf_op jit(solution)/shard_map/ppermute | solution.py:23
  56.7 0.0 collective-permute-done.3
  56.7 0.9 %pad_add_fusion = f32[32,16,256]{2,1,0:T(8,128)} fusion(f32[32,4,256]{2,1,0:T(4,128)S(1)} %collective-permute-done.3, f32[32,16,256]{2,1,0:T(8,128)S(1)} %bitcast.13, f32[32,4,256]{2,1,0:T(4,128)S(1)} %collective-permute-done.2), kind=kLoop, calls=%fused_computation | loop fusion | flops 262144 | bytes 1310720 | tf_op jit(solution)/shard_map/add | solution.py:356
  (3 shorter events, 0.0 us)
Async XLA Ops:
  0.0 6.4 %copy-start = (f32[4,2,32,512]{3,2,1,0:T(8,128)S(1)}, f32[4,2,32,512]{3,2,1,0:T(8,128)}, u32[]{:S(2)}) copy-start(f32[4,2,32,512]{3,2,1,0:T(8,128)} %shift_ref.7) | copy-start | bytes 1572868
  1.1 8.6 %collective-permute-start = (f32[32,4,256]{2,1,0:T(4,128)S(1)}, f32[32,4,256]{2,1,0:T(4,128)S(1)}, u32[]{:S(2)}, u32[]{:S(2)}) collective-permute-start(f32[32,4,256]{2,1,0:T(4,128)S(1)} %get-tuple-element.28), channel_id=1, source_target_pairs={{0,1},{1,2},{2,3},{3,4},{4,5},{5,6},{6,7},{7,0},{8,9},{9,10},{10,1... | collective-permute-start | bytes 393224 | tf_op jit(solution)/shard_map/ppermute | solution.py:23
  3.2 6.5 %collective-permute-start.1 = (f32[32,4,256]{2,1,0:T(4,128)S(1)}, f32[32,4,256]{2,1,0:T(4,128)S(1)}, u32[]{:S(2)}, u32[]{:S(2)}) collective-permute-start(f32[32,4,256]{2,1,0:T(4,128)S(1)} %get-tuple-element.27), channel_id=1, source_target_pairs={{0,7},{1,0},{2,1},{3,2},{4,3},{5,4},{6,5},{7,6},{8,15},{9,8},{10,9... | collective-permute-start | bytes 393224 | tf_op jit(solution)/shard_map/ppermute | solution.py:23
  11.6 6.9 %copy-start.2 = (s32[32,32]{1,0:T(8,128)S(1)}, s32[32,32]{1,0:T(8,128)}, u32[]{:S(2)}) copy-start(s32[32,32]{1,0:T(8,128)} %param.13) | copy-start | bytes 12292
  11.6 7.8 %copy-start.1 = (f32[40,2,2,512]{3,2,1,0:T(2,128)S(1)}, f32[40,2,2,512]{3,2,1,0:T(2,128)}, u32[]{:S(2)}) copy-start(f32[40,2,2,512]{3,2,1,0:T(2,128)} %param.12) | copy-start | bytes 983044
  11.6 19.2 %all-to-all-start = ((f32[16,2,4,8,128]{4,3,2,1,0:T(8,128)}), f32[16,2,4,8,128]{4,3,2,1,0:T(8,128)S(1)}, u32[]{:S(2)}, u32[]{:S(2)}) async-start(f32[16,2,4,8,128]{4,3,2,1,0:T(8,128)} %edge_forward.1), calls=%async_computation | async-start | bytes 1048576 | tf_op jit(solution)/shard_map/all_to_all | solution.py:342
  18.5 0.7 %copy-start.4 = (s32[32]{0:T(128)S(1)}, s32[32]{0:T(128)}, u32[]{:S(2)}) copy-start(s32[32]{0:T(128)} %param.15) | copy-start | bytes 388
  18.6 0.7 %copy-start.3 = (s32[32,32]{1,0:T(8,128)S(1)}, s32[32,32]{1,0:T(8,128)}, u32[]{:S(2)}) copy-start(s32[32,32]{1,0:T(8,128)} %param.14) | copy-start | bytes 12292
  49.6 7.1 %collective-permute-start.2 = (f32[32,4,256]{2,1,0:T(4,128)S(1)}, f32[32,4,256]{2,1,0:T(4,128)S(1)}, u32[]{:S(2)}, u32[]{:S(2)}) collective-permute-start(f32[32,4,256]{2,1,0:T(4,128)S(1)} %get-tuple-element.25), channel_id=1, source_target_pairs={{0,1},{1,2},{2,3},{3,4},{4,5},{5,6},{6,7},{7,0},{8,9},{9,10},{10,1... | collective-permute-start | bytes 393224 | tf_op jit(solution)/shard_map/ppermute | solution.py:23
  50.3 6.4 %collective-permute-start.3 = (f32[32,4,256]{2,1,0:T(4,128)S(1)}, f32[32,4,256]{2,1,0:T(4,128)S(1)}, u32[]{:S(2)}, u32[]{:S(2)}) collective-permute-start(f32[32,4,256]{2,1,0:T(4,128)S(1)} %get-tuple-element.26), channel_id=1, source_target_pairs={{0,7},{1,0},{2,1},{3,2},{4,3},{5,4},{6,5},{7,6},{8,15},{9,8},{10,9... | collective-permute-start | bytes 393224 | tf_op jit(solution)/shard_map/ppermute | solution.py:23

commit v4 on v3

--- a/solution.py
+++ b/solution.py
@@ -8,6 +8,7 @@
 KIDS = 4
 LIST = 32
 GROUP = 4
+QUAD = 4
 PLANES = 32
 ROWS = 32
 OWN = 16
@@ -86,13 +87,27 @@
     return tables
 
 
+def cut_kernel(children_hbm, children_ref, upper_ref, lower_ref, sems):
+    chunks = [slice(8 * i, 8 * i + 8) for i in range(4)]
+    copies = [
+        pltpu.make_async_copy(children_hbm.at[chunk], children_ref.at[chunk], sems.at[i])
+        for i, chunk in enumerate(chunks)
+    ]
+    for copy in copies:
+        copy.start()
+    for copy, chunk in zip(copies, chunks):
+        copy.wait()
+        upper_ref[chunk] = children_ref[chunk, :4]
+        lower_ref[chunk] = children_ref[chunk, OWN - 4 :]
+
+
 def own_forward_kernel(
-    taps_hbm, children_hbm, phi_hbm, shift_ref,
+    taps_hbm, phi_hbm, children_ref, shift_ref,
     packed_ref, phi_high_ref, phi_low_ref, edge_high_ref, edge_low_ref,
     back_high_ref, back_low_ref, edge_back_high_ref, edge_back_low_ref,
-    fine_ref, taps_ref, phi_ref, children_ref, sems,
+    fine_ref, taps_ref, phi_ref, sems,
 ):
-    pairs = ((taps_hbm, taps_ref), (phi_hbm, phi_ref), (children_hbm, children_ref))
+    pairs = ((taps_hbm, taps_ref), (phi_hbm, phi_ref))
     copies = [pltpu.make_async_copy(*pair, sems.at[i]) for i, pair in enumerate(pairs)]
     for copy in copies:
         copy.start()
@@ -115,10 +130,9 @@
     copies[1].wait()
     phi = halves(phi_ref[...])
     phi_high_ref[...], phi_low_ref[...] = phi
-    copies[2].wait()
     for group in range(4):
-        rows = slice(128 * group, 128 * (group + 1))
-        mixed = dot3(halves(children_ref[rows]), phi)
+        own_rows = children_ref[8 * group : 8 * group + 8].reshape(8 * OWN, PHI)
+        mixed = dot3(halves(own_rows), phi)
         fine_ref[256 * group : 256 * (group + 1)] = dot3(own, halves(mixed))
     for parent in range(2):
         for pol in range(2):
@@ -145,11 +159,11 @@
 
 
 def edge_forward_kernel(
-    above_ref, below_ref, phi_high_ref, phi_low_ref, edge_high_ref, edge_low_ref, shift_ref,
-    packed_ref, out_ref, halo_ref, fine_ref, edge_ref, sems,
+    codes_hbm, above_ref, below_ref, phi_high_ref, phi_low_ref, edge_high_ref, edge_low_ref,
+    shift_ref, packed_ref, out_ref, codes_ref, halo_ref, fine_ref, sem,
 ):
-    middle = pltpu.make_async_copy(packed_ref.at[4:12], out_ref.at[4:12], sems.at[0])
-    middle.start()
+    copy = pltpu.make_async_copy(codes_hbm, codes_ref, sem)
+    copy.start()
     for plane in range(PLANES):
         halo_ref[8 * plane : 8 * plane + 4] = above_ref[plane]
         halo_ref[8 * plane + 4 : 8 * plane + 8] = below_ref[plane]
@@ -158,7 +172,7 @@
     for parent in range(2):
         mixed = dot3(halves(halo_ref[128 * parent : 128 * (parent + 1)]), phi)
         fine_ref[256 * parent : 256 * (parent + 1)] = dot3(edge, halves(mixed))
-    copies = []
+    out_ref[4:12] = packed_ref[4:12]
     for side in range(2):
         rows = slice(24 * side, 24 * side + 8)
         for parent in range(2):
@@ -166,15 +180,9 @@
                 real, imag = gathered(fine_ref, shift_ref, parent, pol, 16, 8 * side, rows)
                 for part, value in enumerate((real, imag)):
                     for pair, tile in enumerate(swap_blocks(lane_blocks(value))):
-                        own = packed_ref[12 * side + pair, parent, 2 * pol + part]
-                        edge_ref[4 * side + pair, parent, 2 * pol + part] = own + tile
-        target = out_ref.at[12 * side : 12 * side + 4]
-        copy = pltpu.make_async_copy(edge_ref.at[4 * side : 4 * side + 4], target, sems.at[1 + side])
-        copy.start()
-        copies.append(copy)
-    middle.wait()
-    for copy in copies:
-        copy.wait()
+                        at = (12 * side + pair, parent, 2 * pol + part)
+                        out_ref[at] = packed_ref[at] + tile
+    copy.wait()
 
 
 def spread_back(local_ref, shift_ref, parent, pol, blocks, store):
@@ -238,41 +246,52 @@
             own_ref[128 * group : 128 * (group + 1)] = dot3(halves(narrowed), phi, contract=1)
 
 
-def translate_kernel(source_ref, offset_ref, steps_ref, field_ref, operator_ref, out_ref):
-    pairs = out_ref.shape[0] // 64
-    start = pl.program_id(0) * pairs
-
-    def one_pair(index, carry):
-        pair = start + index
+def translate_kernel(codes_ref, field_ref, operator_ref, out_ref):
+    parents = out_ref.shape[0] // 32
+    slots = parents * LIST
+
+    def one_quad(quad, carry):
+        bases = [codes_ref[2 * slots + quad * QUAD + member] for member in range(QUAD)]
 
         def some_slots(step, sums):
             sums = list(sums)
-            for member in range(2):
+            for member in range(QUAD):
+                slot = bases[member] + step * GROUP
                 for lane in range(GROUP):
-                    slot = pair * (2 * LIST) + step * GROUP + (member * LIST + lane)
-                    source = pl.multiple_of(source_ref[slot], 8)
-                    offset = pl.multiple_of(offset_ref[slot], 8)
-                    real = operator_ref[pl.ds(offset, 8), :]
-                    imag = operator_ref[pl.ds(offset + 8, 8), :]
+                    source = pl.multiple_of(codes_ref[slot + lane], 8)
+                    offset = pl.multiple_of(codes_ref[slot + (slots + lane)], 8)
+                    c = operator_ref[pl.ds(offset, 8), :]
+                    less = operator_ref[pl.ds(offset + 8, 8), :]
+                    more = operator_ref[pl.ds(offset + 16, 8), :]
                     for pol in range(2):
-                        at = member * 4 + pol * 2
+                        at = member * 6 + pol * 3
                         a = field_ref[pl.ds(source + pol * 16, 8), :]
                         b = field_ref[pl.ds(source + (pol * 16 + 8), 8), :]
-                        sums[at] = sums[at] + (real * a - imag * b)
-                        sums[at + 1] = sums[at + 1] + (real * b + imag * a)
+                        sums[at] = sums[at] + c * (a + b)
+                        sums[at + 1] = sums[at + 1] + a * less
+                        sums[at + 2] = sums[at + 2] + b * more
             return tuple(sums)
 
         zero = jnp.zeros((8, 128), jnp.float32)
-        sums = lax.fori_loop(0, steps_ref[pair], some_slots, (zero,) * 8)
-        for part in range(8):
-            out_ref[pl.ds(pl.multiple_of(index * 64 + part * 8, 8), 8), :] = sums[part]
+        steps = codes_ref[2 * slots + parents + quad]
+        sums = lax.fori_loop(0, steps, some_slots, (zero,) * (6 * QUAD))
+        for member in range(QUAD):
+            for pol in range(2):
+                both, less, more = sums[member * 6 + pol * 3 : member * 6 + pol * 3 + 3]
+                at = pl.multiple_of(bases[member] + pol * 16, 8)
+                out_ref[pl.ds(at, 8), :] = both - more
+                out_ref[pl.ds(at + 8, 8), :] = both + less
         return carry
 
-    lax.fori_loop(0, pairs, one_pair, 0)
+    lax.fori_loop(0, parents // QUAD, one_quad, 0)
 
 
 def in_vmem(value):
     return pltpu.with_memory_space_constraint(value, pltpu.VMEM)
+
+
+def in_smem(value):
+    return pltpu.with_memory_space_constraint(value, pltpu.SMEM)
 
 
 def in_hbm(value):
@@ -293,54 +312,93 @@
     )(*map(in_hbm, operands[:raw]), *map(in_vmem, operands[raw:]))
 
 
-def translate(field, translators, far_source, far_offset, far_count):
+def slot_codes(far_source, far_offset, far_count, kinds):
     parents, slots = far_source.shape
-    kinds, _, rows, samples = translators.shape
-    operators = translators.reshape(kinds, 2, rows, samples // 128, 128).transpose(0, 1, 3, 2, 4)
-    operators = jnp.pad(operators.reshape(kinds * 16, 128), ((0, 16), (0, 0)))
     live = jnp.arange(slots, dtype=jnp.int32)[None, :] < far_count[:, None]
     source = (far_source * 32).reshape(-1)
-    offset = (jnp.where(live, far_offset, kinds) * 16).reshape(-1)
-    longest = jnp.max(far_count.reshape(parents // 2, 2), axis=1)
-    steps = (longest + (GROUP - 1)) // GROUP
+    offset = (jnp.where(live, far_offset, kinds) * 24).reshape(-1)
+    index = jnp.arange(parents, dtype=jnp.int32)
+    key = far_count * parents - index
+    rank = jnp.sum((key[None, :] > key[:, None]).astype(jnp.int32), axis=1)
+    chosen = rank[None, :] == index[:, None]
+    order = jnp.sum(jnp.where(chosen, index[None, :] * LIST, 0), axis=1)
+    counts = jnp.sum(jnp.where(chosen[::QUAD], far_count[None, :], 0), axis=1)
+    return jnp.concatenate([source, offset, order, (counts + (GROUP - 1)) // GROUP])
+
+
+def operator_table(translators):
+    kinds, _, rows, samples = translators.shape
+    table = translators.reshape(kinds, 2, rows, samples // 128, 128).transpose(0, 1, 3, 2, 4)
+    real, imag = table[:, 0], table[:, 1]
+    table = jnp.stack([real, imag - real, imag + real], axis=1)
+    return jnp.pad(table.reshape(kinds * 24, 128), ((0, 24), (0, 0)))
+
+
+def translate(field, codes, operators):
     smem = pl.BlockSpec(memory_space=pltpu.SMEM)
     vmem = pl.BlockSpec(memory_space=pltpu.VMEM)
+    field = field.reshape(-1, 128)
     return pl.pallas_call(
         translate_kernel,
-        grid=(4,),
-        out_shape=jax.ShapeDtypeStruct((parents * 32, 128), jnp.float32),
-        in_specs=[smem, smem, smem, vmem, vmem],
-        out_specs=pl.BlockSpec((parents * 8, 128), lambda i: (i, 0)),
+        out_shape=jax.ShapeDtypeStruct(field.shape, jnp.float32),
+        in_specs=[smem, vmem, vmem],
+        out_specs=vmem,
         compiler_params=pltpu.CompilerParams(vmem_limit_bytes=GRANT),
         name="translate",
-    )(source, offset, steps, in_vmem(field.reshape(parents * 32, 128)), in_vmem(operators))
+    )(in_smem(codes), in_vmem(field), in_vmem(operators))
+
+
+def merge_kernel(own_ref, top_ref, bottom_ref, out_hbm, out_ref, sems):
+    copies = []
+    for i in range(4):
+        chunk = slice(8 * i, 8 * i + 8)
+        own = own_ref[chunk]
+        middle = own[:, 4 : OWN - 4]
+        top = own[:, :4] + top_ref[chunk]
+        bottom = own[:, OWN - 4 :] + bottom_ref[chunk]
+        out_ref[chunk] = jnp.concatenate([top, middle, bottom], axis=1)
+        copies.append(pltpu.make_async_copy(out_ref.at[chunk], out_hbm.at[chunk], sems.at[i]))
+        copies[-1].start()
+    for copy in copies:
+        copy.wait()
 
 
 def on_device(
     children, theta_band, phi_interp, child_shift, translators, far_source, far_offset, far_count
 ):
     planes = children.reshape(PLANES, OWN, PHI)
-    above = shifted_ring(planes[:, OWN - 4 :], "theta", 1)
-    below = shifted_ring(planes[:, :4], "theta", -1)
     half = lambda *shape: pltpu.VMEM(shape, HALF)
     whole = lambda *shape: pltpu.VMEM(shape, WHOLE)
+    hbm = pl.BlockSpec(memory_space=pl.ANY)
+    vmem = pl.BlockSpec(memory_space=pltpu.VMEM)
+    smem = pl.BlockSpec(memory_space=pltpu.SMEM)
+    planes, upper, lower = call(
+        cut_kernel, "cut", (whole(PLANES, OWN, PHI),) + (whole(PLANES, 4, PHI),) * 2,
+        [pltpu.SemaphoreType.DMA((4,))], planes, raw=1,
+    )
+    above = shifted_ring(lower, "theta", 1)
+    below = shifted_ring(upper, "theta", -1)
     tables = (half(256, 512),) * 2 + (half(256, 128),) * 2 + (half(128, 256),) * 4
     packed, phi_high, phi_low, edge_high, edge_low, *backs = call(
         own_forward_kernel, "own_forward", (whole(16, 2, 4, 8, 128),) + tables,
         [
-            whole(1024, SAMPLES), whole(8, ROWS), whole(PHI, SAMPLES), whole(PLANES * OWN, PHI),
-            pltpu.SemaphoreType.DMA((3,)),
+            whole(1024, SAMPLES), whole(8, ROWS), whole(PHI, SAMPLES),
+            pltpu.SemaphoreType.DMA((2,)),
         ],
-        theta_band.T, planes.reshape(-1, PHI), phi_interp, child_shift, raw=3,
-    )
-    packed = call(
-        edge_forward_kernel, "edge_forward", jax.ShapeDtypeStruct((16, 2, 4, 8, 128), WHOLE),
-        [whole(256, PHI), whole(512, SAMPLES), whole(8, 2, 4, 8, 128), pltpu.SemaphoreType.DMA((3,))],
-        above, below, phi_high, phi_low, edge_high, edge_low, child_shift, packed,
-        out_specs=pl.BlockSpec(memory_space=pl.ANY),
-    )
+        theta_band.T, phi_interp, planes, child_shift, raw=2,
+    )
+    codes = slot_codes(far_source, far_offset, far_count, translators.shape[0])
+    operators = operator_table(translators)
+    packed, codes = call(
+        edge_forward_kernel, "edge_forward",
+        (whole(16, 2, 4, 8, 128), pltpu.SMEM(codes.shape, jnp.int32)),
+        [whole(256, PHI), whole(512, SAMPLES), pltpu.SemaphoreType.DMA],
+        codes, above, below, phi_high, phi_low, edge_high, edge_low, child_shift, packed,
+        raw=1, out_specs=(vmem, smem),
+    )
+    packed, operators = lax.optimization_barrier((packed, operators))
     field = lax.all_to_all(packed, "clus", 0, 0)
-    summed = translate(field, translators, far_source, far_offset, far_count)
+    summed = translate(field, codes, operators)
     local = lax.all_to_all(summed.reshape(packed.shape), "clus", 0, 0)
     up, down = call(
         edge_back_kernel, "edge_back", (whole(PLANES, 4, PHI),) * 2,
@@ -352,8 +410,11 @@
         own_back_kernel, "own_back", whole(PLANES * OWN, PHI),
         [half(1024, SAMPLES)] * 2, local, child_shift, phi_high, phi_low, backs[0], backs[1],
     ).reshape(planes.shape)
-    result = own + jnp.pad(from_below, ((0, 0), (0, OWN - 4), (0, 0)))
-    result = result + jnp.pad(from_above, ((0, 0), (OWN - 4, 0), (0, 0)))
+    result = call(
+        merge_kernel, "merge", jax.ShapeDtypeStruct(planes.shape, WHOLE),
+        [whole(PLANES, OWN, PHI), pltpu.SemaphoreType.DMA((4,))],
+        own, from_below, from_above, out_specs=hbm,
+    )
     return result.reshape(children.shape)
 
 

time: 58 us -> 57.7 us (level)
  blocking collectives: 15 us -> 33.8 us
  waiting for transfers between devices: 12.4 us -> 1.07 us
  starting transfers between devices: 16.3 us -> 9.44 us
  local copies, waits for them, and re-layouts: 1.97 us -> 1.04 us
    all_to_all x0 -> x1, blocking collectives: none -> 18.9 us  [on_device(): field = lax.all_to_all(packed, 'clus', 0, 0)]
    all_to_all x1 -> x0, waiting for transfers between devices: 11.2 us -> none  [on_device(): field = lax.all_to_all(packed, 'clus', 0, 0)]
    all_to_all x1 -> x0, starting transfers between devices: 6.88 us -> none  [on_device(): field = lax.all_to_all(packed, 'clus', 0, 0)]
    pallas_call x4 -> x6, Pallas kernels: 7.97 us -> 9.22 us  [call(): pl.pallas_call(kernel, out_shape=outs, in_specs=[hbm] * raw + [vmem] * (l...]
    pallas_call x1, Pallas kernels: 2.8 us -> 1.61 us  [translate(): pl.pallas_call(translate_kernel, out_shape=jax.ShapeDtypeStruct(field.sha...]
    slice x1, local copies, waits for them, and re-layouts: 1.13 us -> 0.03 us  [slot_codes(): counts = jnp.sum(jnp.where(chosen[::QUAD], far_count[None, :], 0), axis=1)]
    add x1 -> x0, other arithmetic: 0.87 us -> none  [on_device(): result = result + jnp.pad(from_above, ((0, 0), (OWN - 4, 0), (0, 0)))]
    concatenate x0 -> x1, local copies, waits for them, and re-layouts: none -> 0.68 us  [slot_codes(): jnp.concatenate([source, offset, order, (counts + (GROUP - 1)) // GROUP])]
  transfers between devices with their start and end apart: 5 -> 4, of which waited for: 3 -> 1; matrix products, arithmetic and copies ran while one was open for 1% -> 3% of each run, Pallas kernels for 9% -> 9%
where the time goes in v4:
time: 57.7 us; the launch traced here: 57.2 us
  blocking collectives  33.8 us (59%)
  Pallas kernels  10.8 us (19%)
  starting transfers between devices  9.44 us (16%)
  waiting for transfers between devices  1.07 us (2%)
  local copies, waits for them, and re-layouts  1.04 us (2%)
  other arithmetic  0.87 us (2%)
    all_to_all x1, blocking collectives, on_device(): field = lax.all_to_all(packed, 'clus', 0, 0)  18.9 us
    all_to_all x1, blocking collectives, on_device(): local = lax.all_to_all(summed.reshape(packed.shape), 'clus', 0, 0)  15 us
    ppermute x4, starting transfers between devices, shifted_ring(): lax.ppermute(value, axis, [(i, (i + step) % count) for i in range(count)])  9.44 us
    pallas_call x6, Pallas kernels, call(): pl.pallas_call(kernel, out_shape=outs, in_specs=[hbm] * raw + [vmem] * (l...  9.22 us
    pallas_call x1, Pallas kernels, translate(): pl.pallas_call(translate_kernel, out_shape=jax.ShapeDtypeStruct(field.sha...  1.61 us
  transfers between devices with their start and end apart: 4, of which 1 were waited for; matrix products, arithmetic and copies ran while one was open for 3% of the time, Pallas kernels for 9%

profile of v4, /device:TPU:0, one launch (start us, length us, event | category | flops | bytes accessed | tf_op | source)
XLA Modules:
  0.0 57.2 jit_solution(10635868081659793665)
XLA Ops:
  0.0 0.0 copy-start.1
  0.0 0.0 copy-start.2
  0.0 1.2 %cut.1 = (f32[32,16,256]{2,1,0:T(8,128)S(1)}, f32[32,4,256]{2,1,0:T(4,128)S(1)}, f32[32,4,256]{2,1,0:T(4,128)S(1)}) custom-call(f32[32,16,256]{2,1,0:T(8,128)} %bitcast.14), custom_call_target="tpu_custom_call" | custom-call | tf_op jit(solution)/shard_map/cut/pallas_call | solution.py:304
  1.2 2.1 %collective-permute-start = (f32[32,4,256]{2,1,0:T(4,128)S(1)}, f32[32,4,256]{2,1,0:T(4,128)S(1)}, u32[]{:S(2)}, u32[]{:S(2)}) collective-permute-start(f32[32,4,256]{2,1,0:T(4,128)S(1)} %get-tuple-element.23), channel_id=1, source_target_pairs={{0,1},{1,2},{2,3},{3,4},{4,5},{5,6},{6,7},{7,0},{8,9},{9,10},{10,1... | collective-permute-start | bytes 393224 | tf_op jit(solution)/shard_map/ppermute | solution.py:24
  3.3 0.0 copy-start.4
  3.3 0.0 copy-start.3
  3.3 3.1 %collective-permute-start.1 = (f32[32,4,256]{2,1,0:T(4,128)S(1)}, f32[32,4,256]{2,1,0:T(4,128)S(1)}, u32[]{:S(2)}, u32[]{:S(2)}) collective-permute-start(f32[32,4,256]{2,1,0:T(4,128)S(1)} %get-tuple-element.24), channel_id=1, source_target_pairs={{0,7},{1,0},{2,1},{3,2},{4,3},{5,4},{6,5},{7,6},{8,15},{9,8},{10,9... | collective-permute-start | bytes 393224 | tf_op jit(solution)/shard_map/ppermute | solution.py:24
  6.5 0.0 copy-done.2
  6.5 0.0 copy-done.4
  6.5 0.0 copy-done.3
  6.5 0.1 select_multiply_fusion
  6.6 0.2 convert_reduce_fusion
  6.8 0.1 select_reduce_fusion.1
  6.9 0.0 copy-done.1
  6.9 0.1 fusion
  7.1 0.2 pad_maximum_fusion
  7.3 0.1 reshape.37
  7.4 0.0 copy-start
  7.4 0.1 reshape.38
  7.5 0.1 select_reduce_fusion
  7.6 0.7 %concatenate.3.codes_hbm = s32[2088]{0:T(1024)} concatenate(s32[1024]{0:T(1024)S(1)} %reshape.37, s32[1024]{0:T(1024)S(1)} %reshape.38, s32[32]{0:T(128)S(1)} %select_reduce_fusion, s32[8]{0:T(128)S(1)} %and_select_fusion), dimensions={0} | concatenate | bytes 16704 | tf_op jit(solution)/shard_map/concatenate | solution.py:326
  8.3 0.1 copy-done
  8.4 3.2 %own_forward.1 = (f32[16,2,4,8,128]{4,3,2,1,0:T(8,128)S(1)}, bf16[256,512]{1,0:T(8,128)(2,1)S(1)}, bf16[256,512]{1,0:T(8,128)(2,1)S(1)}, bf16[256,128]{1,0:T(8,1...) custom-call(f32[8,32]{1,0:T(8,128)} %bitcast.16, ...), custom_call_target="tpu_custom_call" | custom-call | tf_op jit(solution)/shard_map/own_forward/pallas_call | solution.py:304
  11.7 0.0 collective-permute-done.above_ref
  11.7 0.0 collective-permute-done.1.below_ref
  11.7 1.1 %edge_forward.1 = (f32[16,2,4,8,128]{4,3,2,1,0:T(8,128)S(1)}, s32[2088]{0:T(1024)S(4)}) custom-call(s32[2088]{0:T(1024)} %concatenate.3.codes_hbm, f32[32,4,256]{2,1,0:T(4,128)S(1)} %collective-permute-done.above_ref, f32[32,4,256]{2,1,0:T(4,128)S(1)} %collective-permute-done.1.below_ref, bf16[256,512]{1,0:T(8,128)(2,1)S(1)} %get-tuple-element.26.phi_high_ref, ...), custom_call_target="tpu_custom_call" | custom-call | tf_op jit(solution)/shard_map/edge_forward/pallas_call | solution.py:304
  12.8 18.9 %all_to_all.10 = f32[16,2,4,8,128]{4,3,2,1,0:T(8,128)S(1)} all-to-all(f32[16,2,4,8,128]{4,3,2,1,0:T(8,128)S(1)} %get-tuple-element.33), channel_id=1, replica_groups=mesh['clus'=16,'theta'=8] {'clus'}, dimensions={0} | all-to-all | bytes 1048576 | tf_op jit(solution)/shard_map/all_to_all | solution.py:400
  31.7 1.6 %translate.1 = f32[1024,128]{1,0:T(8,128)S(1)} custom-call(s32[2088]{0:T(1024)S(4)} %get-tuple-element.31.codes_ref, f32[1024,128]{1,0:T(8,128)S(1)} %bitcast.11, f32[984,128]{1,0:T(8,128)S(1)} %pad.4.operator_ref), custom_call_target="tpu_custom_call" | custom-call | tf_op jit(solution)/shard_map/translate/pallas_call | solution.py:341
  33.3 15.0 %all_to_all.11.local_ref = f32[16,2,4,8,128]{4,3,2,1,0:T(8,128)S(1)} all-to-all(f32[16,2,4,8,128]{4,3,2,1,0:T(8,128)S(1)} %bitcast.12), channel_id=1, replica_groups=mesh['clus'=16,'theta'=8] {'clus'}, dimensions={0} | all-to-all | bytes 1048576 | tf_op jit(solution)/shard_map/all_to_all | solution.py:402
  48.3 1.0 %edge_back.1 = (f32[32,4,256]{2,1,0:T(4,128)S(1)}, f32[32,4,256]{2,1,0:T(4,128)S(1)}) custom-call(f32[16,2,4,8,128]{4,3,2,1,0:T(8,128)S(1)} %all_to_all.11.local_ref, f32[4,2,32,512]{3,2,1,0:T(8,128)S(1)} %copy-done, bf16[256,512]{1,0:T(8,128)(2,1)S(1)} %get-tuple-element.26.phi_high_ref, bf16[256,512]{1,0:T(8,128)(2,1)S(1)} %get-tuple-element.27.phi_low_ref, ...), custom_call_target="tpu_custom_call" | custom-call | tf_op jit(solution)/shard_map/edge_back/pallas_call | solution.py:304
  49.2 0.1 collective-permute-start.2
  49.3 4.1 %collective-permute-start.3 = (f32[32,4,256]{2,1,0:T(4,128)S(1)}, f32[32,4,256]{2,1,0:T(4,128)S(1)}, u32[]{:S(2)}, u32[]{:S(2)}) collective-permute-start(f32[32,4,256]{2,1,0:T(4,128)S(1)} %get-tuple-element.40), channel_id=1, source_target_pairs={{0,7},{1,0},{2,1},{3,2},{4,3},{5,4},{6,5},{7,6},{8,15},{9,8},{10,9... | collective-permute-start | bytes 393224 | tf_op jit(solution)/shard_map/ppermute | solution.py:24
  53.4 1.9 %own_back.1 = f32[512,256]{1,0:T(8,128)S(1)} custom-call(f32[16,2,4,8,128]{4,3,2,1,0:T(8,128)S(1)} %all_to_all.11.local_ref, f32[4,2,32,512]{3,2,1,0:T(8,128)S(1)} %copy-done, bf16[256,512]{1,0:T(8,128)(2,1)S(1)} %get-tuple-element.26.phi_high_ref, bf16[256,512]{1,0:T(8,128)(2,1)S(1)} %get-tuple-element.27.phi_low_ref, ...), custom_call_target="tpu_custom_call" | custom-call | tf_op jit(solution)/shard_map/own_back/pallas_call | solution.py:304
  55.3 1.1 %collective-permute-done.2.top_ref = f32[32,4,256]{2,1,0:T(4,128)S(1)} collective-permute-done((f32[32,4,256]{2,1,0:T(4,128)S(1)}, f32[32,4,256]{2,1,0:T(4,128)S(1)}, u32[]{:S(2)}, u32[]{:S(2)}) %collective-permute-start.2) | collective-permute-done | bytes 131104 | tf_op jit(solution)/shard_map/ppermute | solution.py:24
  56.4 0.0 collective-permute-done.3.bottom_ref
  56.4 0.8 %merge.1 = f32[32,16,256]{2,1,0:T(8,128)} custom-call(f32[32,16,256]{2,1,0:T(8,128)S(1)} %bitcast.10, f32[32,4,256]{2,1,0:T(4,128)S(1)} %collective-permute-done.2.top_ref, f32[32,4,256]{2,1,0:T(4,128)S(1)} %collective-permute-done.3.bottom_ref), custom_call_target="tpu_custom_call" | custom-call | tf_op jit(solution)/shard_map/merge/pallas_call | solution.py:304
  (7 shorter events, 0.1 us)
Async XLA Ops:
  0.0 6.9 %copy-start.1 = (f32[40,2,2,512]{3,2,1,0:T(2,128)S(1)}, f32[40,2,2,512]{3,2,1,0:T(2,128)}, u32[]{:S(2)}) copy-start(f32[40,2,2,512]{3,2,1,0:T(2,128)} %param.12) | copy-start | bytes 983044
  0.0 6.5 %copy-start.2 = (s32[32,32]{1,0:T(8,128)S(1)}, s32[32,32]{1,0:T(8,128)}, u32[]{:S(2)}) copy-start(s32[32,32]{1,0:T(8,128)} %param.13) | copy-start | bytes 12292
  1.2 10.5 %collective-permute-start = (f32[32,4,256]{2,1,0:T(4,128)S(1)}, f32[32,4,256]{2,1,0:T(4,128)S(1)}, u32[]{:S(2)}, u32[]{:S(2)}) collective-permute-start(f32[32,4,256]{2,1,0:T(4,128)S(1)} %get-tuple-element.23), channel_id=1, source_target_pairs={{0,1},{1,2},{2,3},{3,4},{4,5},{5,6},{6,7},{7,0},{8,9},{9,10},{10,1... | collective-permute-start | bytes 393224 | tf_op jit(solution)/shard_map/ppermute | solution.py:24
  3.3 3.2 %copy-start.4 = (s32[32]{0:T(128)S(1)}, s32[32]{0:T(128)}, u32[]{:S(2)}) copy-start(s32[32]{0:T(128)} %param.15) | copy-start | bytes 388
  3.3 3.2 %copy-start.3 = (s32[32,32]{1,0:T(8,128)S(1)}, s32[32,32]{1,0:T(8,128)}, u32[]{:S(2)}) copy-start(s32[32,32]{1,0:T(8,128)} %param.14) | copy-start | bytes 12292
  3.3 8.4 %collective-permute-start.1 = (f32[32,4,256]{2,1,0:T(4,128)S(1)}, f32[32,4,256]{2,1,0:T(4,128)S(1)}, u32[]{:S(2)}, u32[]{:S(2)}) collective-permute-start(f32[32,4,256]{2,1,0:T(4,128)S(1)} %get-tuple-element.24), channel_id=1, source_target_pairs={{0,7},{1,0},{2,1},{3,2},{4,3},{5,4},{6,5},{7,6},{8,15},{9,8},{10,9... | collective-permute-start | bytes 393224 | tf_op jit(solution)/shard_map/ppermute | solution.py:24
  7.4 1.0 %copy-start = (f32[4,2,32,512]{3,2,1,0:T(8,128)S(1)}, f32[4,2,32,512]{3,2,1,0:T(8,128)}, u32[]{:S(2)}) copy-start(f32[4,2,32,512]{3,2,1,0:T(8,128)} %shift_ref.7) | copy-start | bytes 1572868
  49.2 7.1 %collective-permute-start.2 = (f32[32,4,256]{2,1,0:T(4,128)S(1)}, f32[32,4,256]{2,1,0:T(4,128)S(1)}, u32[]{:S(2)}, u32[]{:S(2)}) collective-permute-start(f32[32,4,256]{2,1,0:T(4,128)S(1)} %get-tuple-element.39), channel_id=1, source_target_pairs={{0,1},{1,2},{2,3},{3,4},{4,5},{5,6},{6,7},{7,0},{8,9},{9,10},{10,1... | collective-permute-start | bytes 393224 | tf_op jit(solution)/shard_map/ppermute | solution.py:24
  49.3 7.1 %collective-permute-start.3 = (f32[32,4,256]{2,1,0:T(4,128)S(1)}, f32[32,4,256]{2,1,0:T(4,128)S(1)}, u32[]{:S(2)}, u32[]{:S(2)}) collective-permute-start(f32[32,4,256]{2,1,0:T(4,128)S(1)} %get-tuple-element.40), channel_id=1, source_target_pairs={{0,7},{1,0},{2,1},{3,2},{4,3},{5,4},{6,5},{7,6},{8,15},{9,8},{10,9... | collective-permute-start | bytes 393224 | tf_op jit(solution)/shard_map/ppermute | solution.py:24

commit v5 on v4

v5 whole, which is shorter than its diff:
```python
import functools

import jax
import jax.numpy as jnp
from jax import lax
from jax.experimental import pallas as pl
from jax.experimental.pallas import tpu as pltpu
from jax.sharding import PartitionSpec as P

KIDS = 4
LIST = 32
GROUP = 8
PAIR = 2
PLANES = 32
ROWS = 32
OWN = 16
PHI = 256
SAMPLES = 512
GRANT = 12 * 2**20
HALF = jnp.bfloat16
WHOLE = jnp.float32


def shifted_ring(value, axis, step):
    count = lax.axis_size(axis)
    return lax.ppermute(value, axis, [(i, (i + step) % count) for i in range(count)])


def halves(value):
    high = value.astype(HALF)
    return high, (value - high.astype(WHOLE)).astype(HALF)


def dot3(left, right, contract=0):
    dims = (((1,), (contract,)), ((), ()))
    total = None
    for a, b in ((0, 0), (0, 1), (1, 0)):
        part = lax.dot_general(left[a], right[b], dims, preferred_element_type=WHOLE)
        total = part if total is None else total + part
    return total


def swap_blocks(tiles):
    sub = lax.broadcasted_iota(jnp.int32, (8, 128), 0)
    even = (sub // 2) % 2 == 0
    low = sub < 4
    a, b, c, d = tiles

    def step(first, second, shift, mask):
        one = jnp.where(mask, first, pltpu.roll(second, shift, 0))
        two = jnp.where(mask, pltpu.roll(first, 8 - shift, 0), second)
        return one, two

    a, b = step(a, b, 2, even)
    c, d = step(c, d, 2, even)
    a, c = step(a, c, 4, low)
    b, d = step(b, d, 4, low)
    return a, b, c, d


def lane_blocks(value):
    return [value[:, 128 * i : 128 * (i + 1)] for i in range(4)]


def tiled(bands, outer, width):
    row = lax.broadcasted_iota(jnp.int32, (outer, width), 0)
    column = lax.broadcasted_iota(jnp.int32, (outer, width), 1)
    pick = (row == column % outer).astype(HALF)
    return [jnp.dot(part, pick, preferred_element_type=WHOLE) for part in halves(bands)]


def band_tables(bands, planes, inner, outer, place):
    shape = (planes * inner, planes * outer)
    row = lax.broadcasted_iota(jnp.int32, shape, 0)
    column = lax.broadcasted_iota(jnp.int32, shape, 1)
    child, parent = place(row % inner, column % outer)
    tap = child - parent // 2 + 3
    tap = jnp.where(row // inner == column // outer, tap, -1)
    tables = []
    for part in tiled(bands, outer, shape[1]):
        table = jnp.zeros(shape, WHOLE)
        for t in range(8):
            table = jnp.where(tap == t, jnp.broadcast_to(part[t : t + 1], shape), table)
        tables.append(table)
    return tables


def edge_rows(child, parent):
    child = jnp.where(child < 4, child - 4, child + 12)
    return child, jnp.where(parent < 8, parent, parent + 16)


def cut_kernel(children_hbm, taps_hbm, children_ref, taps_ref, upper_ref, lower_ref, sems):
    chunks = [slice(128 * i, 128 * i + 128) for i in range(4)]
    copies = [
        pltpu.make_async_copy(
            children_hbm.at[chunk, 128 * side : 128 * side + 128],
            children_ref.at[side, chunk],
            sems.at[2 * i + side],
        )
        for i, chunk in enumerate(chunks)
        for side in range(2)
    ]
    for copy in copies:
        copy.start()
    taps = pltpu.make_async_copy(taps_hbm, taps_ref, sems.at[8])
    taps.start()
    for at, copy in enumerate(copies):
        copy.wait()
        i, side = divmod(at, 2)
        for ref, first, count in ((upper_ref, 0, 4), (lower_ref, OWN - 3, 3)):
            for row in range(count):
                rows = pl.ds(128 * i + first + row, 8, stride=OWN)
                value = children_ref[side, rows, :]
                ref[row, 8 * i : 8 * i + 8, 128 * side : 128 * side + 128] = value
    taps.wait()


def both_sides(ref, first, count):
    return jnp.concatenate([ref[side, first : first + count] for side in range(2)], axis=1)


def own_forward_kernel(
    phi_hbm, source_hbm, offset_hbm, counts_hbm, taps_ref, children_ref, shift_ref,
    packed_ref, phi_high_ref, phi_low_ref, edge_high_ref, edge_low_ref, back_high_ref, back_low_ref,
    up_high_ref, up_low_ref, down_high_ref, down_low_ref, codes_ref, counts_ref,
    fine_ref, phi_ref, source_ref, offset_ref, sems, *, kinds,
):
    pairs = (
        (phi_hbm, phi_ref), (source_hbm, source_ref), (offset_hbm, offset_ref),
        (counts_hbm, counts_ref),
    )
    copies = [pltpu.make_async_copy(*pair, sems.at[i]) for i, pair in enumerate(pairs)]
    for copy in copies:
        copy.start()
    strip = lax.axis_index("theta")
    first = (strip > 0).astype(WHOLE)
    last = (strip < lax.axis_size("theta") - 1).astype(WHOLE)
    taps = taps_ref[...]
    table = band_tables(taps, 8, 16, 32, lambda child, parent: (child, parent))
    own = []
    for part, ref in zip(table, (back_high_ref, back_low_ref)):
        ref[...] = part.astype(HALF)
        own.append(part.T.astype(HALF))
    for copy in copies:
        copy.wait()
    phi = halves(phi_ref[...])
    phi_high_ref[...], phi_low_ref[...] = phi
    lane = lax.broadcasted_iota(jnp.int32, (1, LIST), 1)
    for parent in range(source_ref.shape[0]):
        live = lane < counts_ref[parent]
        offset = jnp.where(live, offset_ref[parent : parent + 1], kinds)
        codes_ref[parent : parent + 1] = source_ref[parent : parent + 1] * 32 + offset * (24 * 65536)
    for group in range(4):
        mixed = dot3(halves(both_sides(children_ref, 128 * group, 128)), phi)
        fine_ref[256 * group : 256 * (group + 1)] = dot3(own, halves(mixed))
    upper, lower = taps[:, :8] * first, taps[:, ROWS - 8 :] * last
    table = band_tables(jnp.concatenate([upper, lower], axis=1), 16, 8, 16, edge_rows)
    for part, ref in zip(table, (edge_high_ref, edge_low_ref)):
        ref[...] = part.T.astype(HALF)
    table = band_tables(upper, 16, 4, 8, lambda child, parent: (child - 4, parent))
    for part, ref in zip(table, (up_high_ref, up_low_ref)):
        ref[...] = part.astype(HALF)
    table = band_tables(lower, 16, 4, 8, lambda child, parent: (child + 16, parent + 24))
    for part, ref in zip(table, (down_high_ref, down_low_ref)):
        ref[...] = part.astype(HALF)
    for parent in range(2):
        for pol in range(2):
            for block in range(4):
                rows = slice(8 * block, 8 * (block + 1))
                real, imag = gathered(fine_ref, shift_ref, parent, pol, 32, 8 * block, rows)
                for part, value in enumerate((real, imag)):
                    for pair, tile in enumerate(swap_blocks(lane_blocks(value))):
                        packed_ref[4 * block + pair, parent, 2 * pol + part] = tile


def gathered(fine_ref, shift_ref, parent, pol, per_plane, first, rows):
    real = imag = None
    for kid in range(KIDS):
        at = ((parent * KIDS + kid) * 4 + pol * 2) * per_plane + first
        a = fine_ref[at : at + 8]
        b = fine_ref[at + per_plane : at + per_plane + 8]
        c = shift_ref[kid, 0, rows]
        d = shift_ref[kid, 1, rows]
        one, two = c * a - d * b, c * b + d * a
        real = one if real is None else real + one
        imag = two if imag is None else imag + two
    return real, imag


def edge_forward_kernel(
    codes_src, above_ref, below_ref, phi_high_ref, phi_low_ref, edge_high_ref, edge_low_ref,
    shift_ref, packed_ref, out_ref, codes_ref, halo_ref, fine_ref, sem,
):
    codes = pltpu.make_async_copy(codes_src, codes_ref, sem)
    codes.start()
    for side in range(2):
        lanes = slice(128 * side, 128 * side + 128)
        halo_ref[side, pl.ds(0, PLANES, stride=8), :] = jnp.zeros((PLANES, 128), WHOLE)
        for row in range(3):
            halo_ref[side, pl.ds(row + 1, PLANES, stride=8), :] = above_ref[row, :, lanes]
        for row in range(4):
            halo_ref[side, pl.ds(row + 4, PLANES, stride=8), :] = below_ref[row, :, lanes]
    phi = (phi_high_ref[...], phi_low_ref[...])
    edge = (edge_high_ref[...], edge_low_ref[...])
    for parent in range(2):
        mixed = dot3(halves(both_sides(halo_ref, 128 * parent, 128)), phi)
        fine_ref[256 * parent : 256 * (parent + 1)] = dot3(edge, halves(mixed))
    out_ref[4:12] = packed_ref[4:12]
    for side in range(2):
        rows = slice(24 * side, 24 * side + 8)
        for parent in range(2):
            for pol in range(2):
                real, imag = gathered(fine_ref, shift_ref, parent, pol, 16, 8 * side, rows)
                for part, value in enumerate((real, imag)):
                    for pair, tile in enumerate(swap_blocks(lane_blocks(value))):
                        at = (12 * side + pair, parent, 2 * pol + part)
                        out_ref[at] = packed_ref[at] + tile
    codes.wait()


def spread_back(local_ref, shift_ref, parent, pol, blocks, high_ref, low_ref):
    parts = []
    for part in range(2):
        pieces = []
        for first in blocks:
            tiles = [local_ref[first + pair, parent, 2 * pol + part] for pair in range(4)]
            pieces.append(jnp.concatenate(swap_blocks(tiles), axis=1))
        parts.append(pieces)
    for kid in range(KIDS):
        real, imag = [], []
        for index, first in enumerate(blocks):
            a, b = parts[0][index], parts[1][index]
            c = shift_ref[kid, 0, 2 * first : 2 * first + 8]
            d = shift_ref[kid, 1, 2 * first : 2 * first + 8]
            real.append(c * a + d * b)
            imag.append(c * b - d * a)
        height = 16 * len(blocks)
        at = ((parent * KIDS + kid) * 2 + pol) * height
        value = halves(jnp.concatenate(real + imag, axis=0))
        high_ref[at : at + height], low_ref[at : at + height] = value


def edge_back_kernel(first, skipped):
    def kernel(
        local_ref, shift_ref, phi_high_ref, phi_low_ref, table_high_ref, table_low_ref,
        out_ref, high_ref, low_ref, narrow_ref, result_ref,
    ):
        phi = (phi_high_ref[...], phi_low_ref[...])
        table = (table_high_ref[...], table_low_ref[...])
        for parent in range(2):
            for pol in range(2):
                spread_back(local_ref, shift_ref, parent, pol, (first,), high_ref, low_ref)
            rows = slice(128 * parent, 128 * (parent + 1))
            narrow = dot3(table, (high_ref[rows], low_ref[rows]))
            narrow_ref[64 * parent : 64 * (parent + 1)] = narrow
        result = dot3(halves(narrow_ref[...]), phi, contract=1)
        for side in range(2):
            lanes = slice(128 * side, 128 * side + 128)
            result_ref[side] = result[:, lanes]
            for row in range(4 - skipped):
                rows = pl.ds(row + skipped, PLANES, stride=4)
                out_ref[row, :, lanes] = result_ref[side, rows, :]

    return kernel


def own_back_kernel(
    local_ref, shift_ref, phi_high_ref, phi_low_ref, table_high_ref, table_low_ref,
    own_ref, high_ref, low_ref,
):
    phi = (phi_high_ref[...], phi_low_ref[...])
    table = (table_high_ref[...], table_low_ref[...])

    for parent in range(2):
        for pol in range(2):
            spread_back(local_ref, shift_ref, parent, pol, (0, 4, 8, 12), high_ref, low_ref)
        for group in (2 * parent, 2 * parent + 1):
            rows = slice(256 * group, 256 * (group + 1))
            narrowed = dot3(table, (high_ref[rows], low_ref[rows]))
            result = dot3(halves(narrowed), phi, contract=1)
            for side in range(2):
                lanes = slice(128 * side, 128 * side + 128)
                own_ref[side, 128 * group : 128 * (group + 1)] = result[:, lanes]


def translate_kernel(codes_ref, counts_ref, field_ref, operator_ref, out_ref, table_ref):
    parents = counts_ref.shape[0]
    kinds = operator_ref.shape[0] // 16
    for kind in range(kinds):
        c = operator_ref[16 * kind : 16 * kind + 8]
        d = operator_ref[16 * kind + 8 : 16 * kind + 16]
        for at, value in enumerate((c, d - c, c + d)):
            table_ref[24 * kind + 8 * at : 24 * kind + 8 * at + 8] = value
    table_ref[24 * kinds : 24 * kinds + 24] = jnp.zeros((24, 128), WHOLE)

    def one_pair(pair, carry):
        def some_slots(step, sums):
            sums = list(sums)
            for member in range(PAIR):
                for lane in range(GROUP):
                    slot = pair * (PAIR * LIST) + step * GROUP + (member * LIST + lane)
                    code = codes_ref[slot]
                    source = pl.multiple_of(code & 0xFFFF, 8)
                    offset = pl.multiple_of(code >> 16, 8)
                    c = table_ref[pl.ds(offset, 8), :]
                    less = table_ref[pl.ds(offset + 8, 8), :]
                    more = table_ref[pl.ds(offset + 16, 8), :]
                    for pol in range(2):
                        at = member * 6 + pol * 3
                        a = field_ref[pl.ds(source + pol * 16, 8), :]
                        b = field_ref[pl.ds(source + (pol * 16 + 8), 8), :]
                        sums[at] = sums[at] + c * (a + b)
                        sums[at + 1] = sums[at + 1] + a * less
                        sums[at + 2] = sums[at + 2] + b * more
            return tuple(sums)

        zero = jnp.zeros((8, 128), WHOLE)
        longest = jnp.maximum(counts_ref[pair * PAIR], counts_ref[pair * PAIR + 1])
        steps = lax.shift_right_logical(longest + (GROUP - 1), 3)
        sums = lax.fori_loop(0, steps, some_slots, (zero,) * (6 * PAIR))
        for member in range(PAIR):
            for pol in range(2):
                both, less, more = sums[member * 6 + pol * 3 : member * 6 + pol * 3 + 3]
                at = pl.multiple_of(pair * 64 + member * 32 + pol * 16, 8)
                out_ref[pl.ds(at, 8), :] = both - more
                out_ref[pl.ds(at + 8, 8), :] = both + less
        return carry

    lax.fori_loop(0, parents // PAIR, one_pair, 0)


def in_vmem(value):
    return pltpu.with_memory_space_constraint(value, pltpu.VMEM)


def in_smem(value):
    return pltpu.with_memory_space_constraint(value, pltpu.SMEM)


def in_hbm(value):
    return pltpu.with_memory_space_constraint(value, pltpu.HBM)


def call(kernel, name, outs, scratch, *operands, raw=0, out_specs=None):
    vmem = pl.BlockSpec(memory_space=pltpu.VMEM)
    hbm = pl.BlockSpec(memory_space=pltpu.HBM)
    return pl.pallas_call(
        kernel,
        out_shape=outs,
        in_specs=[hbm] * raw + [vmem] * (len(operands) - raw),
        out_specs=out_specs if out_specs is not None else jax.tree.map(lambda _: vmem, outs),
        scratch_shapes=scratch,
        compiler_params=pltpu.CompilerParams(vmem_limit_bytes=GRANT),
        name=name,
    )(*map(in_hbm, operands[:raw]), *map(in_vmem, operands[raw:]))


def operator_rows(translators):
    kinds, _, rows, samples = translators.shape
    table = translators.reshape(kinds, 2, rows, samples // 128, 128).transpose(0, 1, 3, 2, 4)
    return table.reshape(kinds * 16, 128)


def translate(field, codes, counts, operators):
    smem = pl.BlockSpec(memory_space=pltpu.SMEM)
    vmem = pl.BlockSpec(memory_space=pltpu.VMEM)
    field = field.reshape(-1, 128)
    return pl.pallas_call(
        translate_kernel,
        out_shape=jax.ShapeDtypeStruct(field.shape, WHOLE),
        in_specs=[smem, smem, vmem, vmem],
        out_specs=vmem,
        scratch_shapes=[pltpu.VMEM((operators.shape[0] * 3 // 2 + 24, 128), WHOLE)],
        compiler_params=pltpu.CompilerParams(vmem_limit_bytes=GRANT),
        name="translate",
    )(in_smem(codes), in_smem(counts), in_vmem(field), in_vmem(operators))


def merge_kernel(own_ref, top_ref, bottom_ref, out_hbm, out_ref, sems):
    copies = []
    for i in range(4):
        chunk = slice(128 * i, 128 * i + 128)
        for side in range(2):
            lanes = slice(128 * side, 128 * side + 128)
            out_ref[side, chunk] = own_ref[side, chunk]
            for ref, first, count in ((top_ref, 0, 4), (bottom_ref, OWN - 3, 3)):
                for row in range(count):
                    rows = pl.ds(128 * i + first + row, 8, stride=OWN)
                    value = own_ref[side, rows, :] + ref[row, 8 * i : 8 * i + 8, lanes]
                    out_ref[side, rows, :] = value
            target = out_hbm.at[chunk, lanes]
            copy = pltpu.make_async_copy(out_ref.at[side, chunk], target, sems.at[2 * i + side])
            copy.start()
            copies.append(copy)
    for copy in copies:
        copy.wait()


def on_device(
    children, theta_band, phi_interp, child_shift, translators, far_source, far_offset, far_count
):
    half = lambda *shape: pltpu.VMEM(shape, HALF)
    whole = lambda *shape: pltpu.VMEM(shape, WHOLE)
    hbm = pl.BlockSpec(memory_space=pl.ANY)
    vmem = pl.BlockSpec(memory_space=pltpu.VMEM)
    smem = pl.BlockSpec(memory_space=pltpu.SMEM)
    dma = pltpu.SemaphoreType.DMA
    planes, taps, upper, lower = call(
        cut_kernel, "cut",
        (whole(2, PLANES * OWN, 128), whole(8, ROWS), whole(4, PLANES, PHI), whole(3, PLANES, PHI)),
        [dma((9,))], children.reshape(-1, PHI), theta_band.T, raw=2,
    )
    below = shifted_ring(upper, "theta", -1)
    above = shifted_ring(lower, "theta", 1)
    tables = (half(256, 512),) * 2 + (half(256, 128),) * 2 + (half(128, 256),) * 2
    packed, *tables, codes, counts = call(
        functools.partial(own_forward_kernel, kinds=translators.shape[0]), "own_forward",
        (whole(16, 2, 4, 8, 128),) + tables + (half(64, 128),) * 4
        + (pltpu.VMEM(far_source.shape, jnp.int32), pltpu.SMEM(far_count.shape, jnp.int32)),
        [
            whole(1024, SAMPLES), whole(PHI, SAMPLES), pltpu.VMEM(far_source.shape, jnp.int32),
            pltpu.VMEM(far_source.shape, jnp.int32), dma((4,)),
        ],
        phi_interp, far_source, far_offset, far_count, taps, planes, child_shift,
        raw=4, out_specs=(vmem,) * 12 + (smem,),
    )
    phi, edge, back, up_table, down_table = (tables[i : i + 2] for i in range(0, 10, 2))
    operators = in_vmem(operator_rows(translators))
    packed, codes = call(
        edge_forward_kernel, "edge_forward",
        (whole(16, 2, 4, 8, 128), pltpu.SMEM((codes.size,), jnp.int32)),
        [whole(2, 256, 128), whole(512, SAMPLES), dma],
        codes.reshape(-1), above, below, *phi, *edge, child_shift, packed, out_specs=(vmem, smem),
    )
    packed, operators = lax.optimization_barrier((packed, operators))
    field = lax.all_to_all(packed, "clus", 0, 0)
    summed = translate(field, codes, counts, operators)
    local = lax.all_to_all(summed.reshape(packed.shape), "clus", 0, 0)
    scratch = [half(256, SAMPLES)] * 2 + [whole(128, SAMPLES), whole(2, 128, 128)]
    down = call(
        edge_back_kernel(12, 0), "down_back", whole(4, PLANES, PHI), scratch,
        local, child_shift, *phi, *down_table,
    )
    from_below = shifted_ring(down, "theta", 1)
    up = call(
        edge_back_kernel(0, 1), "up_back", whole(3, PLANES, PHI), scratch,
        local, child_shift, *phi, *up_table,
    )
    from_above = shifted_ring(up, "theta", -1)
    own = call(
        own_back_kernel, "own_back", whole(2, PLANES * OWN, 128), [half(1024, SAMPLES)] * 2,
        local, child_shift, *phi, *back,
    )
    result = call(
        merge_kernel, "merge", jax.ShapeDtypeStruct((PLANES * OWN, PHI), WHOLE),
        [whole(2, PLANES * OWN, 128), dma((8,))], own, from_below, from_above, out_specs=hbm,
    )
    return result.reshape(children.shape)


def solution(mesh):
    return jax.shard_map(
        on_device,
        mesh=mesh,
        in_specs=(
            P("clus", None, None, "theta", None),
            P("theta", None),
            P(),
            P(None, None, "theta", None),
            P(None, None, ("theta", "clus"), None),
            P(),
            P(),
            P(),
        ),
        out_specs=P("clus", None, None, "theta", None),
        check_vma=False,
    )
```

time: 57.7 us -> 59 us (1.023)
  waiting for transfers between devices: 1.07 us -> 3.56 us
  local copies, waits for them, and re-layouts: 1.04 us -> 0.08 us
  other arithmetic: 0.87 us -> 0 us
  Pallas kernels: 10.8 us -> 11.4 us
    ppermute x4, waiting for transfers between devices: 1.07 us -> 3.56 us  [shifted_ring(): lax.ppermute(value, axis, [(i, (i + step) % count) for i in range(count)])]
    concatenate x1 -> x0, local copies, waits for them, and re-layouts: 0.68 us -> none  [slot_codes(): jnp.concatenate([source, offset, order, (counts + (GROUP - 1)) // GROUP])]
    pallas_call x6 -> x7, Pallas kernels: 9.22 us -> 9.76 us  [call(): pl.pallas_call(kernel, out_shape=outs, in_specs=[hbm] * raw + [vmem] * (l...]
  transfers between devices with their start and end apart: 4 -> 4, of which waited for: 1 -> 2; matrix products, arithmetic and copies ran while one was open for 3% -> 0% of each run, Pallas kernels for 9% -> 10%
where the time goes in v5:
time: 59 us; the launch traced here: 58.5 us
  blocking collectives  34 us (58%)
  Pallas kernels  11.4 us (19%)
  starting transfers between devices  9.42 us (16%)
  waiting for transfers between devices  3.56 us (6%)
    all_to_all x1, blocking collectives, on_device(): field = lax.all_to_all(packed, 'clus', 0, 0)  19 us
    all_to_all x1, blocking collectives, on_device(): local = lax.all_to_all(summed.reshape(packed.shape), 'clus', 0, 0)  15 us
    pallas_call x7, Pallas kernels, call(): pl.pallas_call(kernel, out_shape=outs, in_specs=[hbm] * raw + [vmem] * (l...  9.76 us
    ppermute x4, starting transfers between devices, shifted_ring(): lax.ppermute(value, axis, [(i, (i + step) % count) for i in range(count)])  9.42 us
    ppermute x4, waiting for transfers between devices, shifted_ring(): lax.ppermute(value, axis, [(i, (i + step) % count) for i in range(count)])  3.56 us
    pallas_call x1, Pallas kernels, translate(): pl.pallas_call(translate_kernel, out_shape=jax.ShapeDtypeStruct(field.sha...  1.67 us
  transfers between devices with their start and end apart: 4, of which 2 were waited for; matrix products, arithmetic and copies ran while one was open for 0% of the time, Pallas kernels for 10%

profile of v5, /device:TPU:0, one launch (start us, length us, event | category | flops | bytes accessed | tf_op | source)
XLA Modules:
  0.0 58.5 jit_solution(840132594220969669)
XLA Ops:
  0.0 0.0 copy-start
  0.0 1.2 %cut.1 = (f32[2,512,128]{2,1,0:T(8,128)S(1)}, f32[8,32]{1,0:T(8,128)S(1)}, f32[4,32,256]{2,1,0:T(8,128)S(1)}, f32[3,32,256]{2,1,0:T(8,128)S(1)}) custom-call(f32[512,256]{1,0:T(8,128)} %bitcast.13, f32[8,32]{1,0:T(8,128)} %bitcast.14), custom_call_target="tpu_custom_call" | custom-call | tf_op jit(solution)/shard_map/cut/pallas_call | solution.py:348
  1.2 5.1 %collective-permute-start.1 = (f32[4,32,256]{2,1,0:T(8,128)S(1)}, f32[4,32,256]{2,1,0:T(8,128)S(1)}, u32[]{:S(2)}, u32[]{:S(2)}) collective-permute-start(f32[4,32,256]{2,1,0:T(8,128)S(1)} %get-tuple-element.30), channel_id=1, source_target_pairs={{0,7},{1,0},{2,1},{3,2},{4,3},{5,4},{6,5},{7,6},{8,15},{9,8},{10,9... | collective-permute-start | bytes 393224 | tf_op jit(solution)/shard_map/ppermute | solution.py:26
  6.4 0.0 collective-permute-start
  6.4 0.0 copy-done
  6.4 3.5 %own_forward.1 = (f32[16,2,4,8,128]{4,3,2,1,0:T(8,128)S(1)}, bf16[256,512]{1,0:T(8,128)(2,1)S(1)}, bf16[256,512]{1,0:T(8,128)(2,1)S(1)}, bf16[256,128]{1,0:T(8,1...) custom-call(f32[256,512]{1,0:T(8,128)} %phi_hbm.1, ...), custom_call_target="tpu_custom_call" | custom-call | tf_op jit(solution)/shard_map/own_forward/pallas_call | solution.py:348
  9.8 0.1 reshape.22.codes_src
  9.9 3.2 %collective-permute-done.above_ref = f32[3,32,256]{2,1,0:T(8,128)S(1)} collective-permute-done((f32[3,32,256]{2,1,0:T(8,128)S(1)}, f32[3,32,256]{2,1,0:T(8,128)S(1)}, u32[]{:S(2)}, u32[]{:S(2)}) %collective-permute-start) | collective-permute-done | bytes 98336 | tf_op jit(solution)/shard_map/ppermute | solution.py:26
  13.1 0.0 collective-permute-done.1.below_ref
  13.1 1.1 %edge_forward.1 = (f32[16,2,4,8,128]{4,3,2,1,0:T(8,128)S(1)}, s32[1024]{0:T(1024)S(4)}) custom-call(s32[1024]{0:T(1024)S(1)} %reshape.22.codes_src, f32[3,32,256]{2,1,0:T(8,128)S(1)} %collective-permute-done.above_ref, f32[4,32,256]{2,1,0:T(8,128)S(1)} %collective-permute-done.1.below_ref, bf16[256,512]{1,0:T(8,128)(2,1)S(1)} %get-tuple-element.31.phi_high_ref, ...), custom_call_target="tpu_custom_call" | custom-call | tf_op jit(solution)/shard_map/edge_forward/pallas_call | solution.py:348
  14.2 0.0 copy-start.1
  14.2 19.0 %all_to_all.10 = f32[16,2,4,8,128]{4,3,2,1,0:T(8,128)S(1)} all-to-all(f32[16,2,4,8,128]{4,3,2,1,0:T(8,128)S(1)} %get-tuple-element.39), channel_id=1, replica_groups=mesh['clus'=16,'theta'=8] {'clus'}, dimensions={0} | all-to-all | bytes 1048576 | tf_op jit(solution)/shard_map/all_to_all | solution.py:437
  33.2 0.0 copy-done.1
  33.2 1.7 %translate.1 = f32[1024,128]{1,0:T(8,128)S(1)} custom-call(s32[1024]{0:T(1024)S(4)} %get-tuple-element.36.codes_ref, s32[32]{0:T(128)S(4)} %get-tuple-element.37.counts_ref, f32[1024,128]{1,0:T(8,128)S(1)} %bitcast.10, f32[640,128]{1,0:T(8,128)S(1)} %bitcast.12), custom_call_target="tpu_custom_call" | custom-call | tf_op jit(solution)/shard_map/translate/pallas_call | solution.py:369
  34.9 15.0 %all_to_all.11.local_ref = f32[16,2,4,8,128]{4,3,2,1,0:T(8,128)S(1)} all-to-all(f32[16,2,4,8,128]{4,3,2,1,0:T(8,128)S(1)} %bitcast.11), channel_id=1, replica_groups=mesh['clus'=16,'theta'=8] {'clus'}, dimensions={0} | all-to-all | bytes 1048576 | tf_op jit(solution)/shard_map/all_to_all | solution.py:439
  49.9 0.6 %down_back.1 = f32[4,32,256]{2,1,0:T(8,128)S(1)} custom-call(f32[16,2,4,8,128]{4,3,2,1,0:T(8,128)S(1)} %all_to_all.11.local_ref, f32[4,2,32,512]{3,2,1,0:T(8,128)S(1)} %copy-done, bf16[256,512]{1,0:T(8,128)(2,1)S(1)} %get-tuple-element.31.phi_high_ref, bf16[256,512]{1,0:T(8,128)(2,1)S(1)} %get-tuple-element.32.phi_low_ref, ...), custom_call_target="tpu_custom_call" | custom-call | tf_op jit(solution)/shard_map/down_back/pallas_call | solution.py:348
  50.5 0.1 collective-permute-start.2
  50.6 0.6 %up_back.1 = f32[3,32,256]{2,1,0:T(8,128)S(1)} custom-call(f32[16,2,4,8,128]{4,3,2,1,0:T(8,128)S(1)} %all_to_all.11.local_ref, f32[4,2,32,512]{3,2,1,0:T(8,128)S(1)} %copy-done, bf16[256,512]{1,0:T(8,128)(2,1)S(1)} %get-tuple-element.31.phi_high_ref, bf16[256,512]{1,0:T(8,128)(2,1)S(1)} %get-tuple-element.32.phi_low_ref, ...), custom_call_target="tpu_custom_call" | custom-call | tf_op jit(solution)/shard_map/up_back/pallas_call | solution.py:348
  51.2 4.2 %collective-permute-start.3 = (f32[3,32,256]{2,1,0:T(8,128)S(1)}, f32[3,32,256]{2,1,0:T(8,128)S(1)}, u32[]{:S(2)}, u32[]{:S(2)}) collective-permute-start(f32[3,32,256]{2,1,0:T(8,128)S(1)} %up_back.1), channel_id=1, source_target_pairs={{0,7},{1,0},{2,1},{3,2},{4,3},{5,4},{6,5},{7,6},{8,15},{9,8},{10,9... | collective-permute-start | bytes 294920 | tf_op jit(solution)/shard_map/ppermute | solution.py:26
  55.4 1.9 %own_back.1.own_ref = f32[2,512,128]{2,1,0:T(8,128)S(1)} custom-call(f32[16,2,4,8,128]{4,3,2,1,0:T(8,128)S(1)} %all_to_all.11.local_ref, f32[4,2,32,512]{3,2,1,0:T(8,128)S(1)} %copy-done, bf16[256,512]{1,0:T(8,128)(2,1)S(1)} %get-tuple-element.31.phi_high_ref, bf16[256,512]{1,0:T(8,128)(2,1)S(1)} %get-tuple-element.32.phi_low_ref, ...), custom_call_target="tpu_custom_call" | custom-call | tf_op jit(solution)/shard_map/own_back/pallas_call | solution.py:348
  57.3 0.3 collective-permute-done.3.bottom_ref
  57.6 0.0 collective-permute-done.2.top_ref
  57.6 0.9 %merge.1 = f32[512,256]{1,0:T(8,128)} custom-call(f32[2,512,128]{2,1,0:T(8,128)S(1)} %own_back.1.own_ref, f32[4,32,256]{2,1,0:T(8,128)S(1)} %collective-permute-done.2.top_ref, f32[3,32,256]{2,1,0:T(8,128)S(1)} %collective-permute-done.3.bottom_ref), custom_call_target="tpu_custom_call" | custom-call | tf_op jit(solution)/shard_map/merge/pallas_call | solution.py:348
Async XLA Ops:
  0.0 6.4 %copy-start = (f32[4,2,32,512]{3,2,1,0:T(8,128)S(1)}, f32[4,2,32,512]{3,2,1,0:T(8,128)}, u32[]{:S(2)}) copy-start(f32[4,2,32,512]{3,2,1,0:T(8,128)} %shift_ref.9) | copy-start | bytes 1572868
  1.2 11.9 %collective-permute-start.1 = (f32[4,32,256]{2,1,0:T(8,128)S(1)}, f32[4,32,256]{2,1,0:T(8,128)S(1)}, u32[]{:S(2)}, u32[]{:S(2)}) collective-permute-start(f32[4,32,256]{2,1,0:T(8,128)S(1)} %get-tuple-element.30), channel_id=1, source_target_pairs={{0,7},{1,0},{2,1},{3,2},{4,3},{5,4},{6,5},{7,6},{8,15},{9,8},{10,9... | collective-permute-start | bytes 393224 | tf_op jit(solution)/shard_map/ppermute | solution.py:26
  6.4 6.7 %collective-permute-start = (f32[3,32,256]{2,1,0:T(8,128)S(1)}, f32[3,32,256]{2,1,0:T(8,128)S(1)}, u32[]{:S(2)}, u32[]{:S(2)}) collective-permute-start(f32[3,32,256]{2,1,0:T(8,128)S(1)} %get-tuple-element.29), channel_id=1, source_target_pairs={{0,1},{1,2},{2,3},{3,4},{4,5},{5,6},{6,7},{7,0},{8,9},{9,10},{10,1... | collective-permute-start | bytes 294920 | tf_op jit(solution)/shard_map/ppermute | solution.py:26
  14.2 19.0 %copy-start.1 = (f32[40,2,2,512]{3,2,1,0:T(2,128)S(1)}, f32[40,2,2,512]{3,2,1,0:T(2,128)}, u32[]{:S(2)}) copy-start(f32[40,2,2,512]{3,2,1,0:T(2,128)} %param.12) | copy-start | bytes 983044
  50.5 7.1 %collective-permute-start.2 = (f32[4,32,256]{2,1,0:T(8,128)S(1)}, f32[4,32,256]{2,1,0:T(8,128)S(1)}, u32[]{:S(2)}, u32[]{:S(2)}) collective-permute-start(f32[4,32,256]{2,1,0:T(8,128)S(1)} %down_back.1), channel_id=1, source_target_pairs={{0,1},{1,2},{2,3},{3,4},{4,5},{5,6},{6,7},{7,0},{8,9},{9,10},{10,1... | collective-permute-start | bytes 393224 | tf_op jit(solution)/shard_map/ppermute | solution.py:26
  51.2 6.4 %collective-permute-start.3 = (f32[3,32,256]{2,1,0:T(8,128)S(1)}, f32[3,32,256]{2,1,0:T(8,128)S(1)}, u32[]{:S(2)}, u32[]{:S(2)}) collective-permute-start(f32[3,32,256]{2,1,0:T(8,128)S(1)} %up_back.1), channel_id=1, source_target_pairs={{0,7},{1,0},{2,1},{3,2},{4,3},{5,4},{6,5},{7,6},{8,15},{9,8},{10,9... | collective-permute-start | bytes 294920 | tf_op jit(solution)/shard_map/ppermute | solution.py:26

commit v6 on v5

--- a/solution.py
+++ b/solution.py
@@ -21,9 +21,14 @@
 WHOLE = jnp.float32
 
 
-def shifted_ring(value, axis, step):
-    count = lax.axis_size(axis)
-    return lax.ppermute(value, axis, [(i, (i + step) % count) for i in range(count)])
+def swapped(value, far):
+    count = lax.axis_size("theta")
+    pairs = [(i, (i - 1 if (i % 2 == 0) == far else i + 1) % count) for i in range(count)]
+    return lax.ppermute(value, "theta", pairs)
+
+
+def even_strip():
+    return lax.rem(lax.axis_index("theta"), 2) == 0
 
 
 def halves(value):
@@ -90,7 +95,8 @@
     return child, jnp.where(parent < 8, parent, parent + 16)
 
 
-def cut_kernel(children_hbm, taps_hbm, children_ref, taps_ref, upper_ref, lower_ref, sems):
+def cut_kernel(children_hbm, taps_hbm, children_ref, taps_ref, far_ref, near_ref, sems):
+    even = even_strip()
     chunks = [slice(128 * i, 128 * i + 128) for i in range(4)]
     copies = [
         pltpu.make_async_copy(
@@ -108,11 +114,12 @@
     for at, copy in enumerate(copies):
         copy.wait()
         i, side = divmod(at, 2)
-        for ref, first, count in ((upper_ref, 0, 4), (lower_ref, OWN - 3, 3)):
-            for row in range(count):
-                rows = pl.ds(128 * i + first + row, 8, stride=OWN)
-                value = children_ref[side, rows, :]
-                ref[row, 8 * i : 8 * i + 8, 128 * side : 128 * side + 128] = value
+        lanes = slice(128 * side, 128 * side + 128)
+        for row in range(4):
+            upper = children_ref[side, pl.ds(128 * i + row, 8, stride=OWN), :]
+            lower = children_ref[side, pl.ds(128 * i + OWN - 4 + row, 8, stride=OWN), :]
+            far_ref[row, 8 * i : 8 * i + 8, lanes] = jnp.where(even, upper, lower)
+            near_ref[row, 8 * i : 8 * i + 8, lanes] = jnp.where(even, lower, upper)
     taps.wait()
 
 
@@ -123,7 +130,7 @@
 def own_forward_kernel(
     phi_hbm, source_hbm, offset_hbm, counts_hbm, taps_ref, children_ref, shift_ref,
     packed_ref, phi_high_ref, phi_low_ref, edge_high_ref, edge_low_ref, back_high_ref, back_low_ref,
-    up_high_ref, up_low_ref, down_high_ref, down_low_ref, codes_ref, counts_ref,
+    side_high_ref, side_low_ref, codes_ref, counts_ref,
     fine_ref, phi_ref, source_ref, offset_ref, sems, *, kinds,
 ):
     pairs = (
@@ -159,11 +166,11 @@
     for part, ref in zip(table, (edge_high_ref, edge_low_ref)):
         ref[...] = part.T.astype(HALF)
     table = band_tables(upper, 16, 4, 8, lambda child, parent: (child - 4, parent))
-    for part, ref in zip(table, (up_high_ref, up_low_ref)):
-        ref[...] = part.astype(HALF)
+    for part, ref in zip(table, (side_high_ref, side_low_ref)):
+        ref[0] = part.astype(HALF)
     table = band_tables(lower, 16, 4, 8, lambda child, parent: (child + 16, parent + 24))
-    for part, ref in zip(table, (down_high_ref, down_low_ref)):
-        ref[...] = part.astype(HALF)
+    for part, ref in zip(table, (side_high_ref, side_low_ref)):
+        ref[1] = part.astype(HALF)
     for parent in range(2):
         for pol in range(2):
             for block in range(4):
@@ -189,18 +196,18 @@
 
 
 def edge_forward_kernel(
-    codes_src, above_ref, below_ref, phi_high_ref, phi_low_ref, edge_high_ref, edge_low_ref,
+    codes_src, far_ref, near_ref, phi_high_ref, phi_low_ref, edge_high_ref, edge_low_ref,
     shift_ref, packed_ref, out_ref, codes_ref, halo_ref, fine_ref, sem,
 ):
     codes = pltpu.make_async_copy(codes_src, codes_ref, sem)
     codes.start()
+    even = even_strip()
     for side in range(2):
         lanes = slice(128 * side, 128 * side + 128)
-        halo_ref[side, pl.ds(0, PLANES, stride=8), :] = jnp.zeros((PLANES, 128), WHOLE)
-        for row in range(3):
-            halo_ref[side, pl.ds(row + 1, PLANES, stride=8), :] = above_ref[row, :, lanes]
         for row in range(4):
-            halo_ref[side, pl.ds(row + 4, PLANES, stride=8), :] = below_ref[row, :, lanes]
+            far, near = far_ref[row, :, lanes], near_ref[row, :, lanes]
+            halo_ref[side, pl.ds(row, PLANES, stride=8), :] = jnp.where(even, far, near)
+            halo_ref[side, pl.ds(row + 4, PLANES, stride=8), :] = jnp.where(even, near, far)
     phi = (phi_high_ref[...], phi_low_ref[...])
     edge = (edge_high_ref[...], edge_low_ref[...])
     for parent in range(2):
@@ -231,8 +238,8 @@
         real, imag = [], []
         for index, first in enumerate(blocks):
             a, b = parts[0][index], parts[1][index]
-            c = shift_ref[kid, 0, 2 * first : 2 * first + 8]
-            d = shift_ref[kid, 1, 2 * first : 2 * first + 8]
+            rows = pl.ds(pl.multiple_of(2 * first, 8), 8)
+            c, d = shift_ref[kid, 0, rows], shift_ref[kid, 1, rows]
             real.append(c * a + d * b)
             imag.append(c * b - d * a)
         height = 16 * len(blocks)
@@ -241,13 +248,15 @@
         high_ref[at : at + height], low_ref[at : at + height] = value
 
 
-def edge_back_kernel(first, skipped):
+def edge_back_kernel(far):
     def kernel(
         local_ref, shift_ref, phi_high_ref, phi_low_ref, table_high_ref, table_low_ref,
         out_ref, high_ref, low_ref, narrow_ref, result_ref,
     ):
         phi = (phi_high_ref[...], phi_low_ref[...])
-        table = (table_high_ref[...], table_low_ref[...])
+        side = lax.rem(lax.axis_index("theta") + (0 if far else 1), 2)
+        table = (table_high_ref[side], table_low_ref[side])
+        first = side * 12
         for parent in range(2):
             for pol in range(2):
                 spread_back(local_ref, shift_ref, parent, pol, (first,), high_ref, low_ref)
@@ -255,12 +264,12 @@
             narrow = dot3(table, (high_ref[rows], low_ref[rows]))
             narrow_ref[64 * parent : 64 * (parent + 1)] = narrow
         result = dot3(halves(narrow_ref[...]), phi, contract=1)
-        for side in range(2):
-            lanes = slice(128 * side, 128 * side + 128)
-            result_ref[side] = result[:, lanes]
-            for row in range(4 - skipped):
-                rows = pl.ds(row + skipped, PLANES, stride=4)
-                out_ref[row, :, lanes] = result_ref[side, rows, :]
+        for half in range(2):
+            lanes = slice(128 * half, 128 * half + 128)
+            result_ref[half] = result[:, lanes]
+            for row in range(4):
+                rows = pl.ds(row, PLANES, stride=4)
+                out_ref[row, :, lanes] = result_ref[half, rows, :]
 
     return kernel
 
@@ -377,18 +386,21 @@
     )(in_smem(codes), in_smem(counts), in_vmem(field), in_vmem(operators))
 
 
-def merge_kernel(own_ref, top_ref, bottom_ref, out_hbm, out_ref, sems):
+def merge_kernel(own_ref, far_ref, near_ref, out_hbm, out_ref, sems):
+    even = even_strip()
     copies = []
     for i in range(4):
         chunk = slice(128 * i, 128 * i + 128)
         for side in range(2):
             lanes = slice(128 * side, 128 * side + 128)
             out_ref[side, chunk] = own_ref[side, chunk]
-            for ref, first, count in ((top_ref, 0, 4), (bottom_ref, OWN - 3, 3)):
-                for row in range(count):
-                    rows = pl.ds(128 * i + first + row, 8, stride=OWN)
-                    value = own_ref[side, rows, :] + ref[row, 8 * i : 8 * i + 8, lanes]
-                    out_ref[side, rows, :] = value
+            for row in range(4):
+                far = far_ref[row, 8 * i : 8 * i + 8, lanes]
+                near = near_ref[row, 8 * i : 8 * i + 8, lanes]
+                top = pl.ds(128 * i + row, 8, stride=OWN)
+                bottom = pl.ds(128 * i + OWN - 4 + row, 8, stride=OWN)
+                out_ref[side, top, :] = own_ref[side, top, :] + jnp.where(even, far, near)
+                out_ref[side, bottom, :] = own_ref[side, bottom, :] + jnp.where(even, near, far)
             target = out_hbm.at[chunk, lanes]
             copy = pltpu.make_async_copy(out_ref.at[side, chunk], target, sems.at[2 * i + side])
             copy.start()
@@ -406,55 +418,55 @@
     vmem = pl.BlockSpec(memory_space=pltpu.VMEM)
     smem = pl.BlockSpec(memory_space=pltpu.SMEM)
     dma = pltpu.SemaphoreType.DMA
-    planes, taps, upper, lower = call(
+    planes, taps, far, near = call(
         cut_kernel, "cut",
-        (whole(2, PLANES * OWN, 128), whole(8, ROWS), whole(4, PLANES, PHI), whole(3, PLANES, PHI)),
+        (whole(2, PLANES * OWN, 128), whole(8, ROWS)) + (whole(4, PLANES, PHI),) * 2,
         [dma((9,))], children.reshape(-1, PHI), theta_band.T, raw=2,
     )
-    below = shifted_ring(upper, "theta", -1)
-    above = shifted_ring(lower, "theta", 1)
+    far = swapped(far, True)
+    near = swapped(near, False)
     tables = (half(256, 512),) * 2 + (half(256, 128),) * 2 + (half(128, 256),) * 2
     packed, *tables, codes, counts = call(
         functools.partial(own_forward_kernel, kinds=translators.shape[0]), "own_forward",
-        (whole(16, 2, 4, 8, 128),) + tables + (half(64, 128),) * 4
+        (whole(16, 2, 4, 8, 128),) + tables + (half(2, 64, 128),) * 2
         + (pltpu.VMEM(far_source.shape, jnp.int32), pltpu.SMEM(far_count.shape, jnp.int32)),
         [
             whole(1024, SAMPLES), whole(PHI, SAMPLES), pltpu.VMEM(far_source.shape, jnp.int32),
             pltpu.VMEM(far_source.shape, jnp.int32), dma((4,)),
         ],
         phi_interp, far_source, far_offset, far_count, taps, planes, child_shift,
-        raw=4, out_specs=(vmem,) * 12 + (smem,),
-    )
-    phi, edge, back, up_table, down_table = (tables[i : i + 2] for i in range(0, 10, 2))
+        raw=4, out_specs=(vmem,) * 10 + (smem,),
+    )
+    phi, edge, back, sides = (tables[i : i + 2] for i in range(0, 8, 2))
     operators = in_vmem(operator_rows(translators))
     packed, codes = call(
         edge_forward_kernel, "edge_forward",
         (whole(16, 2, 4, 8, 128), pltpu.SMEM((codes.size,), jnp.int32)),
         [whole(2, 256, 128), whole(512, SAMPLES), dma],
-        codes.reshape(-1), above, below, *phi, *edge, child_shift, packed, out_specs=(vmem, smem),
+        codes.reshape(-1), far, near, *phi, *edge, child_shift, packed, out_specs=(vmem, smem),
     )
     packed, operators = lax.optimization_barrier((packed, operators))
     field = lax.all_to_all(packed, "clus", 0, 0)
     summed = translate(field, codes, counts, operators)
     local = lax.all_to_all(summed.reshape(packed.shape), "clus", 0, 0)
     scratch = [half(256, SAMPLES)] * 2 + [whole(128, SAMPLES), whole(2, 128, 128)]
-    down = call(
-        edge_back_kernel(12, 0), "down_back", whole(4, PLANES, PHI), scratch,
-        local, child_shift, *phi, *down_table,
-    )
-    from_below = shifted_ring(down, "theta", 1)
-    up = call(
-        edge_back_kernel(0, 1), "up_back", whole(3, PLANES, PHI), scratch,
-        local, child_shift, *phi, *up_table,
-    )
-    from_above = shifted_ring(up, "theta", -1)
+    far, near = (
+        swapped(
+            call(
+                edge_back_kernel(side), "edge_back", whole(4, PLANES, PHI), scratch,
+                local, child_shift, *phi, *sides,
+            ),
+            side,
+        )
+        for side in (True, False)
+    )
     own = call(
         own_back_kernel, "own_back", whole(2, PLANES * OWN, 128), [half(1024, SAMPLES)] * 2,
         local, child_shift, *phi, *back,
     )
     result = call(
         merge_kernel, "merge", jax.ShapeDtypeStruct((PLANES * OWN, PHI), WHOLE),
-        [whole(2, PLANES * OWN, 128), dma((8,))], own, from_below, from_above, out_specs=hbm,
+        [whole(2, PLANES * OWN, 128), dma((8,))], own, far, near, out_specs=hbm,
     )
     return result.reshape(children.shape)
 

time: 59 us -> 57.8 us (0.980)
  starting transfers between devices: 9.42 us -> 7.1 us
  waiting for transfers between devices: 3.56 us -> 4.5 us
    ppermute x4, starting transfers between devices: 9.42 us -> 7.1 us  [swapped(): return lax.ppermute(value, 'theta', pairs)]
    ppermute x4, waiting for transfers between devices: 3.56 us -> 4.5 us  [swapped(): return lax.ppermute(value, 'theta', pairs)]
  transfers between devices with their start and end apart: 4 -> 4, of which waited for: 2 -> 3; matrix products, arithmetic and copies ran while one was open for 0% -> 0% of each run, Pallas kernels for 10% -> 10%
where the time goes in v6:
time: 57.8 us; the launch traced here: 57.4 us
  blocking collectives  34 us (59%)
  Pallas kernels  11.7 us (20%)
  starting transfers between devices  7.1 us (12%)
  waiting for transfers between devices  4.5 us (8%)
    all_to_all x1, blocking collectives, on_device(): field = lax.all_to_all(packed, 'clus', 0, 0)  19 us
    all_to_all x1, blocking collectives, on_device(): local = lax.all_to_all(summed.reshape(packed.shape), 'clus', 0, 0)  15 us
    pallas_call x7, Pallas kernels, call(): pl.pallas_call(kernel, out_shape=outs, in_specs=[hbm] * raw + [vmem] * (l...  9.75 us
    ppermute x4, starting transfers between devices, swapped(): return lax.ppermute(value, 'theta', pairs)  7.1 us
    ppermute x4, waiting for transfers between devices, swapped(): return lax.ppermute(value, 'theta', pairs)  4.5 us
    pallas_call x1, Pallas kernels, translate(): pl.pallas_call(translate_kernel, out_shape=jax.ShapeDtypeStruct(field.sha...  1.91 us
  transfers between devices with their start and end apart: 4, of which 3 were waited for; matrix products, arithmetic and copies ran while one was open for 0% of the time, Pallas kernels for 10%

profile of v6, /device:TPU:0, one launch (start us, length us, event | category | flops | bytes accessed | tf_op | source)
XLA Modules:
  0.0 57.4 jit_solution(14297630136051026275)
XLA Ops:
  0.0 0.0 copy-start
  0.0 1.2 %cut.1 = (f32[2,512,128]{2,1,0:T(8,128)S(1)}, f32[8,32]{1,0:T(8,128)S(1)}, f32[4,32,256]{2,1,0:T(8,128)S(1)}, f32[4,32,256]{2,1,0:T(8,128)S(1)}) custom-call(f32[512,256]{1,0:T(8,128)} %bitcast.13, f32[8,32]{1,0:T(8,128)} %bitcast.14), custom_call_target="tpu_custom_call" | custom-call | tf_op jit(solution)/shard_map/cut/pallas_call | solution.py:357
  1.2 5.2 %collective-permute-start = (f32[4,32,256]{2,1,0:T(8,128)S(1)}, f32[4,32,256]{2,1,0:T(8,128)S(1)}, u32[]{:S(2)}, u32[]{:S(2)}) collective-permute-start(f32[4,32,256]{2,1,0:T(8,128)S(1)} %get-tuple-element.27), channel_id=1, source_target_pairs={{0,7},{1,2},{2,1},{3,4},{4,3},{5,6},{6,5},{7,0},{8,15},{9,10},{10,... | collective-permute-start | bytes 393224 | tf_op jit(solution)/shard_map/ppermute | solution.py:27
  6.4 0.0 collective-permute-start.1
  6.4 0.0 copy-done
  6.4 3.5 %own_forward.1 = (f32[16,2,4,8,128]{4,3,2,1,0:T(8,128)S(1)}, bf16[256,512]{1,0:T(8,128)(2,1)S(1)}, bf16[256,512]{1,0:T(8,128)(2,1)S(1)}, bf16[256,128]{1,0:T(8,1...) custom-call(f32[256,512]{1,0:T(8,128)} %phi_hbm.1, ...), custom_call_target="tpu_custom_call" | custom-call | tf_op jit(solution)/shard_map/own_forward/pallas_call | solution.py:357
  9.8 0.1 reshape.22.codes_src
  9.9 0.0 collective-permute-done.far_ref
  9.9 1.4 %collective-permute-done.1.near_ref = f32[4,32,256]{2,1,0:T(8,128)S(1)} collective-permute-done((f32[4,32,256]{2,1,0:T(8,128)S(1)}, f32[4,32,256]{2,1,0:T(8,128)S(1)}, u32[]{:S(2)}, u32[]{:S(2)}) %collective-permute-start.1) | collective-permute-done | bytes 131104 | tf_op jit(solution)/shard_map/ppermute | solution.py:27
  11.3 1.1 %edge_forward.1 = (f32[16,2,4,8,128]{4,3,2,1,0:T(8,128)S(1)}, s32[1024]{0:T(1024)S(4)}) custom-call(s32[1024]{0:T(1024)S(1)} %reshape.22.codes_src, f32[4,32,256]{2,1,0:T(8,128)S(1)} %collective-permute-done.far_ref, f32[4,32,256]{2,1,0:T(8,128)S(1)} %collective-permute-done.1.near_ref, bf16[256,512]{1,0:T(8,128)(2,1)S(1)} %get-tuple-element.29.phi_high_ref, ...), custom_call_target="tpu_custom_call" | custom-call | tf_op jit(solution)/shard_map/edge_forward/pallas_call | solution.py:357
  12.5 0.0 copy-start.1
  12.5 19.0 %all_to_all.10 = f32[16,2,4,8,128]{4,3,2,1,0:T(8,128)S(1)} all-to-all(f32[16,2,4,8,128]{4,3,2,1,0:T(8,128)S(1)} %get-tuple-element.37), channel_id=1, replica_groups=mesh['clus'=16,'theta'=8] {'clus'}, dimensions={0} | all-to-all | bytes 1048576 | tf_op jit(solution)/shard_map/all_to_all | solution.py:449
  31.5 0.0 copy-done.1
  31.5 1.9 %translate.1 = f32[1024,128]{1,0:T(8,128)S(1)} custom-call(s32[1024]{0:T(1024)S(4)} %get-tuple-element.34.codes_ref, s32[32]{0:T(128)S(4)} %get-tuple-element.35.counts_ref, f32[1024,128]{1,0:T(8,128)S(1)} %bitcast.10, f32[640,128]{1,0:T(8,128)S(1)} %bitcast.12), custom_call_target="tpu_custom_call" | custom-call | tf_op jit(solution)/shard_map/translate/pallas_call | solution.py:378
  33.4 15.0 %all_to_all.11.local_ref = f32[16,2,4,8,128]{4,3,2,1,0:T(8,128)S(1)} all-to-all(f32[16,2,4,8,128]{4,3,2,1,0:T(8,128)S(1)} %bitcast.11), channel_id=1, replica_groups=mesh['clus'=16,'theta'=8] {'clus'}, dimensions={0} | all-to-all | bytes 1048576 | tf_op jit(solution)/shard_map/all_to_all | solution.py:451
  48.4 0.6 %edge_back.2 = f32[4,32,256]{2,1,0:T(8,128)S(1)} custom-call(f32[16,2,4,8,128]{4,3,2,1,0:T(8,128)S(1)} %all_to_all.11.local_ref, f32[4,2,32,512]{3,2,1,0:T(8,128)S(1)} %copy-done, bf16[256,512]{1,0:T(8,128)(2,1)S(1)} %get-tuple-element.29.phi_high_ref, bf16[256,512]{1,0:T(8,128)(2,1)S(1)} %get-tuple-element.30.phi_low_ref, ...), custom_call_target="tpu_custom_call" | custom-call | tf_op jit(solution)/shard_map/edge_back/pallas_call | solution.py:357
  49.0 1.9 %collective-permute-start.2 = (f32[4,32,256]{2,1,0:T(8,128)S(1)}, f32[4,32,256]{2,1,0:T(8,128)S(1)}, u32[]{:S(2)}, u32[]{:S(2)}) collective-permute-start(f32[4,32,256]{2,1,0:T(8,128)S(1)} %edge_back.2), channel_id=1, source_target_pairs={{0,7},{1,2},{2,1},{3,4},{4,3},{5,6},{6,5},{7,0},{8,15},{9,10},{10,... | collective-permute-start | bytes 393224 | tf_op jit(solution)/shard_map/ppermute | solution.py:27
  50.8 0.6 %edge_back.3 = f32[4,32,256]{2,1,0:T(8,128)S(1)} custom-call(f32[16,2,4,8,128]{4,3,2,1,0:T(8,128)S(1)} %all_to_all.11.local_ref, f32[4,2,32,512]{3,2,1,0:T(8,128)S(1)} %copy-done, bf16[256,512]{1,0:T(8,128)(2,1)S(1)} %get-tuple-element.29.phi_high_ref, bf16[256,512]{1,0:T(8,128)(2,1)S(1)} %get-tuple-element.30.phi_low_ref, ...), custom_call_target="tpu_custom_call" | custom-call | tf_op jit(solution)/shard_map/edge_back/pallas_call | solution.py:357
  51.4 0.1 collective-permute-start.3
  51.5 1.9 %own_back.1.own_ref = f32[2,512,128]{2,1,0:T(8,128)S(1)} custom-call(f32[16,2,4,8,128]{4,3,2,1,0:T(8,128)S(1)} %all_to_all.11.local_ref, f32[4,2,32,512]{3,2,1,0:T(8,128)S(1)} %copy-done, bf16[256,512]{1,0:T(8,128)(2,1)S(1)} %get-tuple-element.29.phi_high_ref, bf16[256,512]{1,0:T(8,128)(2,1)S(1)} %get-tuple-element.30.phi_low_ref, ...), custom_call_target="tpu_custom_call" | custom-call | tf_op jit(solution)/shard_map/own_back/pallas_call | solution.py:357
  53.4 2.7 %collective-permute-done.2.far_ref = f32[4,32,256]{2,1,0:T(8,128)S(1)} collective-permute-done((f32[4,32,256]{2,1,0:T(8,128)S(1)}, f32[4,32,256]{2,1,0:T(8,128)S(1)}, u32[]{:S(2)}, u32[]{:S(2)}) %collective-permute-start.2) | collective-permute-done | bytes 131104 | tf_op jit(solution)/shard_map/ppermute | solution.py:27
  56.1 0.4 collective-permute-done.3.near_ref
  56.5 0.9 %merge.1 = f32[512,256]{1,0:T(8,128)} custom-call(f32[2,512,128]{2,1,0:T(8,128)S(1)} %own_back.1.own_ref, f32[4,32,256]{2,1,0:T(8,128)S(1)} %collective-permute-done.2.far_ref, f32[4,32,256]{2,1,0:T(8,128)S(1)} %collective-permute-done.3.near_ref), custom_call_target="tpu_custom_call" | custom-call | tf_op jit(solution)/shard_map/merge/pallas_call | solution.py:357
Async XLA Ops:
  0.0 6.4 %copy-start = (f32[4,2,32,512]{3,2,1,0:T(8,128)S(1)}, f32[4,2,32,512]{3,2,1,0:T(8,128)}, u32[]{:S(2)}) copy-start(f32[4,2,32,512]{3,2,1,0:T(8,128)} %shift_ref.9) | copy-start | bytes 1572868
  1.2 8.7 %collective-permute-start = (f32[4,32,256]{2,1,0:T(8,128)S(1)}, f32[4,32,256]{2,1,0:T(8,128)S(1)}, u32[]{:S(2)}, u32[]{:S(2)}) collective-permute-start(f32[4,32,256]{2,1,0:T(8,128)S(1)} %get-tuple-element.27), channel_id=1, source_target_pairs={{0,7},{1,2},{2,1},{3,4},{4,3},{5,6},{6,5},{7,0},{8,15},{9,10},{10,... | collective-permute-start | bytes 393224 | tf_op jit(solution)/shard_map/ppermute | solution.py:27
  6.4 5.0 %collective-permute-start.1 = (f32[4,32,256]{2,1,0:T(8,128)S(1)}, f32[4,32,256]{2,1,0:T(8,128)S(1)}, u32[]{:S(2)}, u32[]{:S(2)}) collective-permute-start(f32[4,32,256]{2,1,0:T(8,128)S(1)} %get-tuple-element.28), channel_id=1, source_target_pairs={{0,1},{1,0},{2,3},{3,2},{4,5},{5,4},{6,7},{7,6},{8,9},{9,8},{10,11... | collective-permute-start | bytes 393224 | tf_op jit(solution)/shard_map/ppermute | solution.py:27
  12.5 19.0 %copy-start.1 = (f32[40,2,2,512]{3,2,1,0:T(2,128)S(1)}, f32[40,2,2,512]{3,2,1,0:T(2,128)}, u32[]{:S(2)}) copy-start(f32[40,2,2,512]{3,2,1,0:T(2,128)} %param.12) | copy-start | bytes 983044
  49.0 7.2 %collective-permute-start.2 = (f32[4,32,256]{2,1,0:T(8,128)S(1)}, f32[4,32,256]{2,1,0:T(8,128)S(1)}, u32[]{:S(2)}, u32[]{:S(2)}) collective-permute-start(f32[4,32,256]{2,1,0:T(8,128)S(1)} %edge_back.2), channel_id=1, source_target_pairs={{0,7},{1,2},{2,1},{3,4},{4,3},{5,6},{6,5},{7,0},{8,15},{9,10},{10,... | collective-permute-start | bytes 393224 | tf_op jit(solution)/shard_map/ppermute | solution.py:27
  51.4 5.0 %collective-permute-start.3 = (f32[4,32,256]{2,1,0:T(8,128)S(1)}, f32[4,32,256]{2,1,0:T(8,128)S(1)}, u32[]{:S(2)}, u32[]{:S(2)}) collective-permute-start(f32[4,32,256]{2,1,0:T(8,128)S(1)} %edge_back.3), channel_id=1, source_target_pairs={{0,1},{1,0},{2,3},{3,2},{4,5},{5,4},{6,7},{7,6},{8,9},{9,8},{10,11... | collective-permute-start | bytes 393224 | tf_op jit(solution)/shard_map/ppermute | solution.py:27

commit v7 on v5

--- a/solution.py
+++ b/solution.py
@@ -6,6 +6,7 @@
 from jax.experimental import pallas as pl
 from jax.experimental.pallas import tpu as pltpu
 from jax.sharding import PartitionSpec as P
+
 
 KIDS = 4
 LIST = 32
@@ -90,7 +91,9 @@
     return child, jnp.where(parent < 8, parent, parent + 16)
 
 
-def cut_kernel(children_hbm, taps_hbm, children_ref, taps_ref, upper_ref, lower_ref, sems):
+def cut_kernel(
+    children_hbm, taps_hbm, phi_hbm, children_ref, taps_ref, phi_ref, upper_ref, lower_ref, sems
+):
     chunks = [slice(128 * i, 128 * i + 128) for i in range(4)]
     copies = [
         pltpu.make_async_copy(
@@ -105,6 +108,8 @@
         copy.start()
     taps = pltpu.make_async_copy(taps_hbm, taps_ref, sems.at[8])
     taps.start()
+    phi = pltpu.make_async_copy(phi_hbm, phi_ref, sems.at[9])
+    phi.start()
     for at, copy in enumerate(copies):
         copy.wait()
         i, side = divmod(at, 2)
@@ -114,6 +119,7 @@
                 value = children_ref[side, rows, :]
                 ref[row, 8 * i : 8 * i + 8, 128 * side : 128 * side + 128] = value
     taps.wait()
+    phi.wait()
 
 
 def both_sides(ref, first, count):
@@ -121,15 +127,12 @@
 
 
 def own_forward_kernel(
-    phi_hbm, source_hbm, offset_hbm, counts_hbm, taps_ref, children_ref, shift_ref,
+    source_hbm, offset_hbm, counts_hbm, phi_ref, taps_ref, children_ref, shift_ref,
     packed_ref, phi_high_ref, phi_low_ref, edge_high_ref, edge_low_ref, back_high_ref, back_low_ref,
     up_high_ref, up_low_ref, down_high_ref, down_low_ref, codes_ref, counts_ref,
-    fine_ref, phi_ref, source_ref, offset_ref, sems, *, kinds,
+    fine_ref, source_ref, offset_ref, sems, *, kinds,
 ):
-    pairs = (
-        (phi_hbm, phi_ref), (source_hbm, source_ref), (offset_hbm, offset_ref),
-        (counts_hbm, counts_ref),
-    )
+    pairs = ((source_hbm, source_ref), (offset_hbm, offset_ref), (counts_hbm, counts_ref))
     copies = [pltpu.make_async_copy(*pair, sems.at[i]) for i, pair in enumerate(pairs)]
     for copy in copies:
         copy.start()
@@ -142,18 +145,18 @@
     for part, ref in zip(table, (back_high_ref, back_low_ref)):
         ref[...] = part.astype(HALF)
         own.append(part.T.astype(HALF))
+    phi = halves(phi_ref[...])
+    phi_high_ref[...], phi_low_ref[...] = phi
+    for group in range(4):
+        mixed = dot3(halves(both_sides(children_ref, 128 * group, 128)), phi)
+        fine_ref[256 * group : 256 * (group + 1)] = dot3(own, halves(mixed))
     for copy in copies:
         copy.wait()
-    phi = halves(phi_ref[...])
-    phi_high_ref[...], phi_low_ref[...] = phi
     lane = lax.broadcasted_iota(jnp.int32, (1, LIST), 1)
     for parent in range(source_ref.shape[0]):
         live = lane < counts_ref[parent]
         offset = jnp.where(live, offset_ref[parent : parent + 1], kinds)
         codes_ref[parent : parent + 1] = source_ref[parent : parent + 1] * 32 + offset * (24 * 65536)
-    for group in range(4):
-        mixed = dot3(halves(both_sides(children_ref, 128 * group, 128)), phi)
-        fine_ref[256 * group : 256 * (group + 1)] = dot3(own, halves(mixed))
     upper, lower = taps[:, :8] * first, taps[:, ROWS - 8 :] * last
     table = band_tables(jnp.concatenate([upper, lower], axis=1), 16, 8, 16, edge_rows)
     for part, ref in zip(table, (edge_high_ref, edge_low_ref)):
@@ -342,7 +345,7 @@
     return pltpu.with_memory_space_constraint(value, pltpu.HBM)
 
 
-def call(kernel, name, outs, scratch, *operands, raw=0, out_specs=None):
+def call(kernel, outs, scratch, *operands, raw=0, out_specs=None):
     vmem = pl.BlockSpec(memory_space=pltpu.VMEM)
     hbm = pl.BlockSpec(memory_space=pltpu.HBM)
     return pl.pallas_call(
@@ -352,7 +355,6 @@
         out_specs=out_specs if out_specs is not None else jax.tree.map(lambda _: vmem, outs),
         scratch_shapes=scratch,
         compiler_params=pltpu.CompilerParams(vmem_limit_bytes=GRANT),
-        name=name,
     )(*map(in_hbm, operands[:raw]), *map(in_vmem, operands[raw:]))
 
 
@@ -406,29 +408,32 @@
     vmem = pl.BlockSpec(memory_space=pltpu.VMEM)
     smem = pl.BlockSpec(memory_space=pltpu.SMEM)
     dma = pltpu.SemaphoreType.DMA
-    planes, taps, upper, lower = call(
-        cut_kernel, "cut",
-        (whole(2, PLANES * OWN, 128), whole(8, ROWS), whole(4, PLANES, PHI), whole(3, PLANES, PHI)),
-        [dma((9,))], children.reshape(-1, PHI), theta_band.T, raw=2,
-    )
+    planes, taps, phi, upper, lower = call(
+        cut_kernel,
+        (
+            whole(2, PLANES * OWN, 128), whole(8, ROWS), whole(*phi_interp.shape),
+            whole(4, PLANES, PHI), whole(3, PLANES, PHI),
+        ),
+        [dma((10,))], children.reshape(-1, PHI), theta_band.T, phi_interp, raw=3,
+    )
+    above = shifted_ring(lower, "theta", 1)
     below = shifted_ring(upper, "theta", -1)
-    above = shifted_ring(lower, "theta", 1)
     tables = (half(256, 512),) * 2 + (half(256, 128),) * 2 + (half(128, 256),) * 2
     packed, *tables, codes, counts = call(
-        functools.partial(own_forward_kernel, kinds=translators.shape[0]), "own_forward",
+        functools.partial(own_forward_kernel, kinds=translators.shape[0]),
         (whole(16, 2, 4, 8, 128),) + tables + (half(64, 128),) * 4
         + (pltpu.VMEM(far_source.shape, jnp.int32), pltpu.SMEM(far_count.shape, jnp.int32)),
         [
-            whole(1024, SAMPLES), whole(PHI, SAMPLES), pltpu.VMEM(far_source.shape, jnp.int32),
-            pltpu.VMEM(far_source.shape, jnp.int32), dma((4,)),
+            whole(1024, SAMPLES), pltpu.VMEM(far_source.shape, jnp.int32),
+            pltpu.VMEM(far_source.shape, jnp.int32), dma((3,)),
         ],
-        phi_interp, far_source, far_offset, far_count, taps, planes, child_shift,
-        raw=4, out_specs=(vmem,) * 12 + (smem,),
+        far_source, far_offset, far_count, phi, taps, planes, child_shift,
+        raw=3, out_specs=(vmem,) * 12 + (smem,),
     )
     phi, edge, back, up_table, down_table = (tables[i : i + 2] for i in range(0, 10, 2))
     operators = in_vmem(operator_rows(translators))
     packed, codes = call(
-        edge_forward_kernel, "edge_forward",
+        edge_forward_kernel,
         (whole(16, 2, 4, 8, 128), pltpu.SMEM((codes.size,), jnp.int32)),
         [whole(2, 256, 128), whole(512, SAMPLES), dma],
         codes.reshape(-1), above, below, *phi, *edge, child_shift, packed, out_specs=(vmem, smem),
@@ -439,21 +444,21 @@
     local = lax.all_to_all(summed.reshape(packed.shape), "clus", 0, 0)
     scratch = [half(256, SAMPLES)] * 2 + [whole(128, SAMPLES), whole(2, 128, 128)]
     down = call(
-        edge_back_kernel(12, 0), "down_back", whole(4, PLANES, PHI), scratch,
+        edge_back_kernel(12, 0), whole(4, PLANES, PHI), scratch,
         local, child_shift, *phi, *down_table,
     )
     from_below = shifted_ring(down, "theta", 1)
     up = call(
-        edge_back_kernel(0, 1), "up_back", whole(3, PLANES, PHI), scratch,
+        edge_back_kernel(0, 1), whole(3, PLANES, PHI), scratch,
         local, child_shift, *phi, *up_table,
     )
     from_above = shifted_ring(up, "theta", -1)
     own = call(
-        own_back_kernel, "own_back", whole(2, PLANES * OWN, 128), [half(1024, SAMPLES)] * 2,
+        own_back_kernel, whole(2, PLANES * OWN, 128), [half(1024, SAMPLES)] * 2,
         local, child_shift, *phi, *back,
     )
     result = call(
-        merge_kernel, "merge", jax.ShapeDtypeStruct((PLANES * OWN, PHI), WHOLE),
+        merge_kernel, jax.ShapeDtypeStruct((PLANES * OWN, PHI), WHOLE),
         [whole(2, PLANES * OWN, 128), dma((8,))], own, from_below, from_above, out_specs=hbm,
     )
     return result.reshape(children.shape)

time: 59 us -> 59.4 us (level)
  transfers between devices with their start and end apart: 4 -> 4, of which waited for: 2 -> 2; matrix products, arithmetic and copies ran while one was open for 0% -> 0% of each run, Pallas kernels for 10% -> 9%
where the time goes in v7:
time: 59.4 us; the launch traced here: 59.1 us
  blocking collectives  34 us (57%)
  Pallas kernels  11.6 us (20%)
  starting transfers between devices  9.42 us (16%)
  waiting for transfers between devices  4.01 us (7%)
    all_to_all x1, blocking collectives, on_device(): field = lax.all_to_all(packed, 'clus', 0, 0)  19 us
    all_to_all x1, blocking collectives, on_device(): local = lax.all_to_all(summed.reshape(packed.shape), 'clus', 0, 0)  15 us
    pallas_call x7, Pallas kernels, call(): pl.pallas_call(kernel, out_shape=outs, in_specs=[hbm] * raw + [vmem] * (l...  9.54 us
    ppermute x4, starting transfers between devices, shifted_ring(): lax.ppermute(value, axis, [(i, (i + step) % count) for i in range(count)])  9.42 us
    ppermute x4, waiting for transfers between devices, shifted_ring(): lax.ppermute(value, axis, [(i, (i + step) % count) for i in range(count)])  4.01 us
    pallas_call x1, Pallas kernels, translate(): pl.pallas_call(translate_kernel, out_shape=jax.ShapeDtypeStruct(field.sha...  2.06 us
  transfers between devices with their start and end apart: 4, of which 2 were waited for; matrix products, arithmetic and copies ran while one was open for 0% of the time, Pallas kernels for 9%

profile of v7, /device:TPU:0, one launch (start us, length us, event | category | flops | bytes accessed | tf_op | source)
XLA Modules:
  0.0 59.1 jit_solution(1126326988341136884)
XLA Ops:
  0.0 0.0 copy-start
  0.0 1.4 %shard_map.82 = (f32[2,512,128]{2,1,0:T(8,128)S(1)}, f32[8,32]{1,0:T(8,128)S(1)}, f32[256,512]{1,0:T(8,128)S(1)}, f32[4,32,256]{2,1,0:T(8,128)S(1)}, f32[3,32,256]{2,1,0:T(8,128)S(1)}) custom-call(f32[512,256]{1,0:T(8,128)} %bitcast.13, f32[8,32]{1,0:T(8,128)} %bitcast.14, f32[256,512]{1,0:T(8,128)} %phi_hbm.1), custom_call_target="tpu_custom_call" | custom-call | tf_op jit(solution)/shard_map/pallas_call | solution.py:351
  1.5 5.1 %collective-permute-start.1 = (f32[4,32,256]{2,1,0:T(8,128)S(1)}, f32[4,32,256]{2,1,0:T(8,128)S(1)}, u32[]{:S(2)}, u32[]{:S(2)}) collective-permute-start(f32[4,32,256]{2,1,0:T(8,128)S(1)} %get-tuple-element.32), channel_id=1, source_target_pairs={{0,7},{1,0},{2,1},{3,2},{4,3},{5,4},{6,5},{7,6},{8,15},{9,8},{10,9... | collective-permute-start | bytes 393224 | tf_op jit(solution)/shard_map/ppermute | solution.py:27
  6.6 0.0 collective-permute-start
  6.6 0.0 copy-done
  6.6 3.0 %shard_map.83 = (f32[16,2,4,8,128]{4,3,2,1,0:T(8,128)S(1)}, bf16[256,512]{1,0:T(8,128)(2,1)S(1)}, bf16[256,512]{1,0:T(8,128)(2,1)S(1)}, bf16[256,128]{1,0:T(8,12...) custom-call(s32[32,32]{1,0:T(8,128)} %source_hbm.1, ...), custom_call_target="tpu_custom_call" | custom-call | tf_op jit(solution)/shard_map/pallas_call | solution.py:351
  9.6 0.1 reshape.22.codes_src
  9.7 3.6 %collective-permute-done.above_ref = f32[3,32,256]{2,1,0:T(8,128)S(1)} collective-permute-done((f32[3,32,256]{2,1,0:T(8,128)S(1)}, f32[3,32,256]{2,1,0:T(8,128)S(1)}, u32[]{:S(2)}, u32[]{:S(2)}) %collective-permute-start) | collective-permute-done | bytes 98336 | tf_op jit(solution)/shard_map/ppermute | solution.py:27
  13.3 0.0 collective-permute-done.1.below_ref
  13.3 1.1 %shard_map.84 = (f32[16,2,4,8,128]{4,3,2,1,0:T(8,128)S(1)}, s32[1024]{0:T(1024)S(4)}) custom-call(s32[1024]{0:T(1024)S(1)} %reshape.22.codes_src, f32[3,32,256]{2,1,0:T(8,128)S(1)} %collective-permute-done.above_ref, f32[4,32,256]{2,1,0:T(8,128)S(1)} %collective-permute-done.1.below_ref, bf16[256,512]{1,0:T(8,128)(2,1)S(1)} %get-tuple-element.33.phi_high_ref, ...), custom_call_target="tpu_custom_call" | custom-call | tf_op jit(solution)/shard_map/pallas_call | solution.py:351
  14.5 0.0 copy-start.1
  14.5 19.0 %all_to_all.10 = f32[16,2,4,8,128]{4,3,2,1,0:T(8,128)S(1)} all-to-all(f32[16,2,4,8,128]{4,3,2,1,0:T(8,128)S(1)} %get-tuple-element.41), channel_id=1, replica_groups=mesh['clus'=16,'theta'=8] {'clus'}, dimensions={0} | all-to-all | bytes 1048576 | tf_op jit(solution)/shard_map/all_to_all | solution.py:442
  33.5 0.0 copy-done.1
  33.5 2.1 %translate.1 = f32[1024,128]{1,0:T(8,128)S(1)} custom-call(s32[1024]{0:T(1024)S(4)} %get-tuple-element.38.codes_ref, s32[32]{0:T(128)S(4)} %get-tuple-element.39.counts_ref, f32[1024,128]{1,0:T(8,128)S(1)} %bitcast.10, f32[640,128]{1,0:T(8,128)S(1)} %bitcast.12), custom_call_target="tpu_custom_call" | custom-call | tf_op jit(solution)/shard_map/translate/pallas_call | solution.py:371
  35.6 15.0 %all_to_all.11.local_ref = f32[16,2,4,8,128]{4,3,2,1,0:T(8,128)S(1)} all-to-all(f32[16,2,4,8,128]{4,3,2,1,0:T(8,128)S(1)} %bitcast.11), channel_id=1, replica_groups=mesh['clus'=16,'theta'=8] {'clus'}, dimensions={0} | all-to-all | bytes 1048576 | tf_op jit(solution)/shard_map/all_to_all | solution.py:444
  50.5 0.6 %shard_map.86 = f32[4,32,256]{2,1,0:T(8,128)S(1)} custom-call(f32[16,2,4,8,128]{4,3,2,1,0:T(8,128)S(1)} %all_to_all.11.local_ref, f32[4,2,32,512]{3,2,1,0:T(8,128)S(1)} %copy-done, bf16[256,512]{1,0:T(8,128)(2,1)S(1)} %get-tuple-element.33.phi_high_ref, bf16[256,512]{1,0:T(8,128)(2,1)S(1)} %get-tuple-element.34.phi_low_ref, ...), custom_call_target="tpu_custom_call" | custom-call | tf_op jit(solution)/shard_map/pallas_call | solution.py:351
  51.1 0.1 collective-permute-start.2
  51.2 0.6 %shard_map.87 = f32[3,32,256]{2,1,0:T(8,128)S(1)} custom-call(f32[16,2,4,8,128]{4,3,2,1,0:T(8,128)S(1)} %all_to_all.11.local_ref, f32[4,2,32,512]{3,2,1,0:T(8,128)S(1)} %copy-done, bf16[256,512]{1,0:T(8,128)(2,1)S(1)} %get-tuple-element.33.phi_high_ref, bf16[256,512]{1,0:T(8,128)(2,1)S(1)} %get-tuple-element.34.phi_low_ref, ...), custom_call_target="tpu_custom_call" | custom-call | tf_op jit(solution)/shard_map/pallas_call | solution.py:351
  51.8 4.2 %collective-permute-start.3 = (f32[3,32,256]{2,1,0:T(8,128)S(1)}, f32[3,32,256]{2,1,0:T(8,128)S(1)}, u32[]{:S(2)}, u32[]{:S(2)}) collective-permute-start(f32[3,32,256]{2,1,0:T(8,128)S(1)} %shard_map.87), channel_id=1, source_target_pairs={{0,7},{1,0},{2,1},{3,2},{4,3},{5,4},{6,5},{7,6},{8,15},{9,8},{10,9... | collective-permute-start | bytes 294920 | tf_op jit(solution)/shard_map/ppermute | solution.py:27
  56.0 1.9 %shard_map.85.own_ref = f32[2,512,128]{2,1,0:T(8,128)S(1)} custom-call(f32[16,2,4,8,128]{4,3,2,1,0:T(8,128)S(1)} %all_to_all.11.local_ref, f32[4,2,32,512]{3,2,1,0:T(8,128)S(1)} %copy-done, bf16[256,512]{1,0:T(8,128)(2,1)S(1)} %get-tuple-element.33.phi_high_ref, bf16[256,512]{1,0:T(8,128)(2,1)S(1)} %get-tuple-element.34.phi_low_ref, ...), custom_call_target="tpu_custom_call" | custom-call | tf_op jit(solution)/shard_map/pallas_call | solution.py:351
  57.9 0.3 collective-permute-done.3.bottom_ref
  58.2 0.0 collective-permute-done.2.top_ref
  58.3 0.9 %shard_map.88 = f32[512,256]{1,0:T(8,128)} custom-call(f32[2,512,128]{2,1,0:T(8,128)S(1)} %shard_map.85.own_ref, f32[4,32,256]{2,1,0:T(8,128)S(1)} %collective-permute-done.2.top_ref, f32[3,32,256]{2,1,0:T(8,128)S(1)} %collective-permute-done.3.bottom_ref), custom_call_target="tpu_custom_call" | custom-call | tf_op jit(solution)/shard_map/pallas_call | solution.py:351
Async XLA Ops:
  0.0 6.6 %copy-start = (f32[4,2,32,512]{3,2,1,0:T(8,128)S(1)}, f32[4,2,32,512]{3,2,1,0:T(8,128)}, u32[]{:S(2)}) copy-start(f32[4,2,32,512]{3,2,1,0:T(8,128)} %shift_ref.9) | copy-start | bytes 1572868
  1.5 11.9 %collective-permute-start.1 = (f32[4,32,256]{2,1,0:T(8,128)S(1)}, f32[4,32,256]{2,1,0:T(8,128)S(1)}, u32[]{:S(2)}, u32[]{:S(2)}) collective-permute-start(f32[4,32,256]{2,1,0:T(8,128)S(1)} %get-tuple-element.32), channel_id=1, source_target_pairs={{0,7},{1,0},{2,1},{3,2},{4,3},{5,4},{6,5},{7,6},{8,15},{9,8},{10,9... | collective-permute-start | bytes 393224 | tf_op jit(solution)/shard_map/ppermute | solution.py:27
  6.6 6.7 %collective-permute-start = (f32[3,32,256]{2,1,0:T(8,128)S(1)}, f32[3,32,256]{2,1,0:T(8,128)S(1)}, u32[]{:S(2)}, u32[]{:S(2)}) collective-permute-start(f32[3,32,256]{2,1,0:T(8,128)S(1)} %get-tuple-element.31), channel_id=1, source_target_pairs={{0,1},{1,2},{2,3},{3,4},{4,5},{5,6},{6,7},{7,0},{8,9},{9,10},{10,1... | collective-permute-start | bytes 294920 | tf_op jit(solution)/shard_map/ppermute | solution.py:27
  14.5 19.0 %copy-start.1 = (f32[40,2,2,512]{3,2,1,0:T(2,128)S(1)}, f32[40,2,2,512]{3,2,1,0:T(2,128)}, u32[]{:S(2)}) copy-start(f32[40,2,2,512]{3,2,1,0:T(2,128)} %param.12) | copy-start | bytes 983044
  51.1 7.1 %collective-permute-start.2 = (f32[4,32,256]{2,1,0:T(8,128)S(1)}, f32[4,32,256]{2,1,0:T(8,128)S(1)}, u32[]{:S(2)}, u32[]{:S(2)}) collective-permute-start(f32[4,32,256]{2,1,0:T(8,128)S(1)} %shard_map.86), channel_id=1, source_target_pairs={{0,1},{1,2},{2,3},{3,4},{4,5},{5,6},{6,7},{7,0},{8,9},{9,10},{10,1... | collective-permute-start | bytes 393224 | tf_op jit(solution)/shard_map/ppermute | solution.py:27
  51.8 6.4 %collective-permute-start.3 = (f32[3,32,256]{2,1,0:T(8,128)S(1)}, f32[3,32,256]{2,1,0:T(8,128)S(1)}, u32[]{:S(2)}, u32[]{:S(2)}) collective-permute-start(f32[3,32,256]{2,1,0:T(8,128)S(1)} %shard_map.87), channel_id=1, source_target_pairs={{0,7},{1,0},{2,1},{3,2},{4,3},{5,4},{6,5},{7,6},{8,15},{9,8},{10,9... | collective-permute-start | bytes 294920 | tf_op jit(solution)/shard_map/ppermute | solution.py:27

commit v8 on v7

--- a/solution.py
+++ b/solution.py
@@ -63,32 +63,60 @@
     return [value[:, 128 * i : 128 * (i + 1)] for i in range(4)]
 
 
-def tiled(bands, outer, width):
-    row = lax.broadcasted_iota(jnp.int32, (outer, width), 0)
-    column = lax.broadcasted_iota(jnp.int32, (outer, width), 1)
-    pick = (row == column % outer).astype(HALF)
-    return [jnp.dot(part, pick, preferred_element_type=WHOLE) for part in halves(bands)]
-
-
-def band_tables(bands, planes, inner, outer, place):
-    shape = (planes * inner, planes * outer)
-    row = lax.broadcasted_iota(jnp.int32, shape, 0)
-    column = lax.broadcasted_iota(jnp.int32, shape, 1)
-    child, parent = place(row % inner, column % outer)
-    tap = child - parent // 2 + 3
-    tap = jnp.where(row // inner == column // outer, tap, -1)
-    tables = []
-    for part in tiled(bands, outer, shape[1]):
-        table = jnp.zeros(shape, WHOLE)
-        for t in range(8):
-            table = jnp.where(tap == t, jnp.broadcast_to(part[t : t + 1], shape), table)
-        tables.append(table)
-    return tables
+def table_times(table, value):
+    wide = jnp.dot(table, jnp.concatenate([value[0], value[0]], axis=0), preferred_element_type=WHOLE)
+    depth = table.shape[1] // 2
+    return wide + jnp.dot(table[:, :depth], value[1], preferred_element_type=WHOLE)
+
+
+def same(child, parent):
+    return child, parent
 
 
 def edge_rows(child, parent):
     child = jnp.where(child < 4, child - 4, child + 12)
     return child, jnp.where(parent < 8, parent, parent + 16)
+
+
+def tap_of(child, parent, place):
+    child, parent = place(child, parent)
+    return child - parent // 2 + 3
+
+
+def forward_table(bands, planes, inner, place):
+    outer = bands.shape[0]
+    width = planes * inner
+    row = lax.broadcasted_iota(jnp.int32, (outer, width), 0)
+    column = lax.broadcasted_iota(jnp.int32, (outer, width), 1)
+    tap = tap_of(column % inner, row, place)
+    block = jnp.zeros((outer, width), WHOLE)
+    for t in range(8):
+        block = jnp.where(tap == t, jnp.broadcast_to(bands[:, t : t + 1], block.shape), block)
+    owner = column // inner
+    blocks = [jnp.where(owner == plane, block, 0.0) for plane in range(planes)]
+    return jnp.concatenate(blocks, axis=0)
+
+
+def backward_table(bands, planes, inner, place):
+    outer = bands.shape[1]
+    width = planes * outer
+    high = max(inner, 8)
+    pick = lax.broadcasted_iota(jnp.int32, (outer, width), 1) % outer
+    pick = (lax.broadcasted_iota(jnp.int32, (outer, width), 0) == pick).astype(HALF)
+    row = lax.broadcasted_iota(jnp.int32, (high, width), 0)
+    column = lax.broadcasted_iota(jnp.int32, (high, width), 1)
+    tap = tap_of(row % inner, column % outer, place)
+    tables = []
+    for part in halves(bands):
+        tiled = jnp.dot(part, pick, preferred_element_type=WHOLE)
+        block = jnp.zeros((high, width), WHOLE)
+        for t in range(8):
+            block = jnp.where(tap == t, jnp.broadcast_to(tiled[t : t + 1], block.shape), block)
+        owner = column // outer - row // inner
+        step = high // inner
+        blocks = [jnp.where(owner == plane, block, 0.0) for plane in range(0, planes, step)]
+        tables.append(jnp.concatenate(blocks, axis=0).astype(HALF))
+    return tables
 
 
 def cut_kernel(
@@ -128,8 +156,8 @@
 
 def own_forward_kernel(
     source_hbm, offset_hbm, counts_hbm, phi_ref, taps_ref, children_ref, shift_ref,
-    packed_ref, phi_high_ref, phi_low_ref, edge_high_ref, edge_low_ref, back_high_ref, back_low_ref,
-    up_high_ref, up_low_ref, down_high_ref, down_low_ref, codes_ref, counts_ref,
+    packed_ref, phi_high_ref, phi_low_ref, edge_ref, back_high_ref, back_low_ref,
+    up_ref, down_ref, codes_ref, counts_ref,
     fine_ref, source_ref, offset_ref, sems, *, kinds,
 ):
     pairs = ((source_hbm, source_ref), (offset_hbm, offset_ref), (counts_hbm, counts_ref))
@@ -140,16 +168,36 @@
     first = (strip > 0).astype(WHOLE)
     last = (strip < lax.axis_size("theta") - 1).astype(WHOLE)
     taps = taps_ref[...]
-    table = band_tables(taps, 8, 16, 32, lambda child, parent: (child, parent))
-    own = []
-    for part, ref in zip(table, (back_high_ref, back_low_ref)):
-        ref[...] = part.astype(HALF)
-        own.append(part.T.astype(HALF))
+    bands = jnp.concatenate([taps] * 16, axis=0).T[:, :8]
+    own = jnp.concatenate(halves(forward_table(bands, 8, 16, same)), axis=1)
     phi = halves(phi_ref[...])
     phi_high_ref[...], phi_low_ref[...] = phi
+
+    def spread(group):
+        mixed = dot3(halves(both_sides(children_ref, 128 * group, 128)), phi)
+        fine_ref[256 * group : 256 * (group + 1)] = table_times(own, halves(mixed))
+
+    def collect(parent):
+        for pol in range(2):
+            for block in range(4):
+                rows = slice(8 * block, 8 * (block + 1))
+                real, imag = gathered(fine_ref, shift_ref, parent, pol, 32, 8 * block, rows)
+                for part, value in enumerate((real, imag)):
+                    for pair, tile in enumerate(swap_blocks(lane_blocks(value))):
+                        packed_ref[4 * block + pair, parent, 2 * pol + part] = tile
+
     for group in range(4):
-        mixed = dot3(halves(both_sides(children_ref, 128 * group, 128)), phi)
-        fine_ref[256 * group : 256 * (group + 1)] = dot3(own, halves(mixed))
+        spread(group)
+        if group == 2:
+            collect(0)
+    edge = jnp.concatenate([bands[:8] * first, bands[ROWS - 8 :] * last], axis=0)
+    edge_ref[...] = jnp.concatenate(halves(forward_table(edge, 16, 8, edge_rows)), axis=1)
+    back_high_ref[...], back_low_ref[...] = backward_table(taps, 8, 16, same)
+    upper, lower = taps[:, :8] * first, taps[:, ROWS - 8 :] * last
+    table = backward_table(upper, 16, 4, lambda child, parent: (child - 4, parent))
+    up_ref[...] = jnp.concatenate(table, axis=1)
+    table = backward_table(lower, 16, 4, lambda child, parent: (child + 16, parent + 24))
+    down_ref[...] = jnp.concatenate(table, axis=1)
     for copy in copies:
         copy.wait()
     lane = lax.broadcasted_iota(jnp.int32, (1, LIST), 1)
@@ -157,24 +205,7 @@
         live = lane < counts_ref[parent]
         offset = jnp.where(live, offset_ref[parent : parent + 1], kinds)
         codes_ref[parent : parent + 1] = source_ref[parent : parent + 1] * 32 + offset * (24 * 65536)
-    upper, lower = taps[:, :8] * first, taps[:, ROWS - 8 :] * last
-    table = band_tables(jnp.concatenate([upper, lower], axis=1), 16, 8, 16, edge_rows)
-    for part, ref in zip(table, (edge_high_ref, edge_low_ref)):
-        ref[...] = part.T.astype(HALF)
-    table = band_tables(upper, 16, 4, 8, lambda child, parent: (child - 4, parent))
-    for part, ref in zip(table, (up_high_ref, up_low_ref)):
-        ref[...] = part.astype(HALF)
-    table = band_tables(lower, 16, 4, 8, lambda child, parent: (child + 16, parent + 24))
-    for part, ref in zip(table, (down_high_ref, down_low_ref)):
-        ref[...] = part.astype(HALF)
-    for parent in range(2):
-        for pol in range(2):
-            for block in range(4):
-                rows = slice(8 * block, 8 * (block + 1))
-                real, imag = gathered(fine_ref, shift_ref, parent, pol, 32, 8 * block, rows)
-                for part, value in enumerate((real, imag)):
-                    for pair, tile in enumerate(swap_blocks(lane_blocks(value))):
-                        packed_ref[4 * block + pair, parent, 2 * pol + part] = tile
+    collect(1)
 
 
 def gathered(fine_ref, shift_ref, parent, pol, per_plane, first, rows):
@@ -192,7 +223,7 @@
 
 
 def edge_forward_kernel(
-    codes_src, above_ref, below_ref, phi_high_ref, phi_low_ref, edge_high_ref, edge_low_ref,
+    codes_src, above_ref, below_ref, phi_high_ref, phi_low_ref, edge_ref,
     shift_ref, packed_ref, out_ref, codes_ref, halo_ref, fine_ref, sem,
 ):
     codes = pltpu.make_async_copy(codes_src, codes_ref, sem)
@@ -205,10 +236,10 @@
         for row in range(4):
             halo_ref[side, pl.ds(row + 4, PLANES, stride=8), :] = below_ref[row, :, lanes]
     phi = (phi_high_ref[...], phi_low_ref[...])
-    edge = (edge_high_ref[...], edge_low_ref[...])
+    edge = edge_ref[...]
     for parent in range(2):
         mixed = dot3(halves(both_sides(halo_ref, 128 * parent, 128)), phi)
-        fine_ref[256 * parent : 256 * (parent + 1)] = dot3(edge, halves(mixed))
+        fine_ref[256 * parent : 256 * (parent + 1)] = table_times(edge, halves(mixed))
     out_ref[4:12] = packed_ref[4:12]
     for side in range(2):
         rows = slice(24 * side, 24 * side + 8)
@@ -246,16 +277,16 @@
 
 def edge_back_kernel(first, skipped):
     def kernel(
-        local_ref, shift_ref, phi_high_ref, phi_low_ref, table_high_ref, table_low_ref,
+        local_ref, shift_ref, phi_high_ref, phi_low_ref, table_ref,
         out_ref, high_ref, low_ref, narrow_ref, result_ref,
     ):
         phi = (phi_high_ref[...], phi_low_ref[...])
-        table = (table_high_ref[...], table_low_ref[...])
+        table = table_ref[...]
         for parent in range(2):
             for pol in range(2):
                 spread_back(local_ref, shift_ref, parent, pol, (first,), high_ref, low_ref)
             rows = slice(128 * parent, 128 * (parent + 1))
-            narrow = dot3(table, (high_ref[rows], low_ref[rows]))
+            narrow = table_times(table, (high_ref[rows], low_ref[rows]))
             narrow_ref[64 * parent : 64 * (parent + 1)] = narrow
         result = dot3(halves(narrow_ref[...]), phi, contract=1)
         for side in range(2):
@@ -418,25 +449,25 @@
     )
     above = shifted_ring(lower, "theta", 1)
     below = shifted_ring(upper, "theta", -1)
-    tables = (half(256, 512),) * 2 + (half(256, 128),) * 2 + (half(128, 256),) * 2
+    tables = (half(256, 512),) * 2 + (half(256, 256),) + (half(128, 256),) * 2
     packed, *tables, codes, counts = call(
         functools.partial(own_forward_kernel, kinds=translators.shape[0]),
-        (whole(16, 2, 4, 8, 128),) + tables + (half(64, 128),) * 4
+        (whole(16, 2, 4, 8, 128),) + tables + (half(64, 256),) * 2
         + (pltpu.VMEM(far_source.shape, jnp.int32), pltpu.SMEM(far_count.shape, jnp.int32)),
         [
             whole(1024, SAMPLES), pltpu.VMEM(far_source.shape, jnp.int32),
             pltpu.VMEM(far_source.shape, jnp.int32), dma((3,)),
         ],
         far_source, far_offset, far_count, phi, taps, planes, child_shift,
-        raw=3, out_specs=(vmem,) * 12 + (smem,),
-    )
-    phi, edge, back, up_table, down_table = (tables[i : i + 2] for i in range(0, 10, 2))
+        raw=3, out_specs=(vmem,) * 9 + (smem,),
+    )
+    *phi, edge, back_high, back_low, up_table, down_table = tables
     operators = in_vmem(operator_rows(translators))
     packed, codes = call(
         edge_forward_kernel,
         (whole(16, 2, 4, 8, 128), pltpu.SMEM((codes.size,), jnp.int32)),
         [whole(2, 256, 128), whole(512, SAMPLES), dma],
-        codes.reshape(-1), above, below, *phi, *edge, child_shift, packed, out_specs=(vmem, smem),
+        codes.reshape(-1), above, below, *phi, edge, child_shift, packed, out_specs=(vmem, smem),
     )
     packed, operators = lax.optimization_barrier((packed, operators))
     field = lax.all_to_all(packed, "clus", 0, 0)
@@ -445,17 +476,17 @@
     scratch = [half(256, SAMPLES)] * 2 + [whole(128, SAMPLES), whole(2, 128, 128)]
     down = call(
         edge_back_kernel(12, 0), whole(4, PLANES, PHI), scratch,
-        local, child_shift, *phi, *down_table,
+        local, child_shift, *phi, down_table,
     )
     from_below = shifted_ring(down, "theta", 1)
     up = call(
         edge_back_kernel(0, 1), whole(3, PLANES, PHI), scratch,
-        local, child_shift, *phi, *up_table,
+        local, child_shift, *phi, up_table,
     )
     from_above = shifted_ring(up, "theta", -1)
     own = call(
         own_back_kernel, whole(2, PLANES * OWN, 128), [half(1024, SAMPLES)] * 2,
-        local, child_shift, *phi, *back,
+        local, child_shift, *phi, back_high, back_low,
     )
     result = call(
         merge_kernel, jax.ShapeDtypeStruct((PLANES * OWN, PHI), WHOLE),

time: 59.4 us -> 59.3 us (level)
  no operation moved by 1% of the time
where the time goes in v8:
time: 59.3 us; the launch traced here: 59 us
  blocking collectives  34 us (57%)
  Pallas kernels  11.1 us (19%)
  starting transfers between devices  9.41 us (16%)
  waiting for transfers between devices  4.42 us (7%)
    all_to_all x1, blocking collectives, on_device(): field = lax.all_to_all(packed, 'clus', 0, 0)  19 us
    all_to_all x1, blocking collectives, on_device(): local = lax.all_to_all(summed.reshape(packed.shape), 'clus', 0, 0)  15 us
    ppermute x4, starting transfers between devices, shifted_ring(): lax.ppermute(value, axis, [(i, (i + step) % count) for i in range(count)])  9.41 us
    pallas_call x7, Pallas kernels, call(): pl.pallas_call(kernel, out_shape=outs, in_specs=[hbm] * raw + [vmem] * (l...  9.02 us
    ppermute x4, waiting for transfers between devices, shifted_ring(): lax.ppermute(value, axis, [(i, (i + step) % count) for i in range(count)])  4.42 us
    pallas_call x1, Pallas kernels, translate(): pl.pallas_call(translate_kernel, out_shape=jax.ShapeDtypeStruct(field.sha...  2.06 us
  transfers between devices with their start and end apart: 4, of which 2 were waited for; matrix products, arithmetic and copies ran while one was open for 0% of the time, Pallas kernels for 9%

profile of v8, /device:TPU:0, one launch (start us, length us, event | category | flops | bytes accessed | tf_op | source)
XLA Modules:
  0.0 59.0 jit_solution(12697439141321909745)
XLA Ops:
  0.0 0.0 copy-start
  0.0 1.4 %shard_map.82 = (f32[2,512,128]{2,1,0:T(8,128)S(1)}, f32[8,32]{1,0:T(8,128)S(1)}, f32[256,512]{1,0:T(8,128)S(1)}, f32[4,32,256]{2,1,0:T(8,128)S(1)}, f32[3,32,256]{2,1,0:T(8,128)S(1)}) custom-call(f32[512,256]{1,0:T(8,128)} %bitcast.13, f32[8,32]{1,0:T(8,128)} %bitcast.14, f32[256,512]{1,0:T(8,128)} %phi_hbm.1), custom_call_target="tpu_custom_call" | custom-call | tf_op jit(solution)/shard_map/pallas_call | solution.py:382
  1.5 5.1 %collective-permute-start.1 = (f32[4,32,256]{2,1,0:T(8,128)S(1)}, f32[4,32,256]{2,1,0:T(8,128)S(1)}, u32[]{:S(2)}, u32[]{:S(2)}) collective-permute-start(f32[4,32,256]{2,1,0:T(8,128)S(1)} %get-tuple-element.29), channel_id=1, source_target_pairs={{0,7},{1,0},{2,1},{3,2},{4,3},{5,4},{6,5},{7,6},{8,15},{9,8},{10,9... | collective-permute-start | bytes 393224 | tf_op jit(solution)/shard_map/ppermute | solution.py:27
  6.6 0.0 collective-permute-start
  6.6 0.0 copy-done
  6.6 2.6 %shard_map.83 = (f32[16,2,4,8,128]{4,3,2,1,0:T(8,128)S(1)}, bf16[256,512]{1,0:T(8,128)(2,1)S(1)}, bf16[256,512]{1,0:T(8,128)(2,1)S(1)}, bf16[256,256]{1,0:T(8,12...) custom-call(s32[32,32]{1,0:T(8,128)} %source_hbm.1, ...), custom_call_target="tpu_custom_call" | custom-call | tf_op jit(solution)/shard_map/pallas_call | solution.py:382
  9.2 0.1 reshape.22.codes_src
  9.3 4.0 %collective-permute-done.above_ref = f32[3,32,256]{2,1,0:T(8,128)S(1)} collective-permute-done((f32[3,32,256]{2,1,0:T(8,128)S(1)}, f32[3,32,256]{2,1,0:T(8,128)S(1)}, u32[]{:S(2)}, u32[]{:S(2)}) %collective-permute-start) | collective-permute-done | bytes 98336 | tf_op jit(solution)/shard_map/ppermute | solution.py:27
  13.3 0.0 collective-permute-done.1.below_ref
  13.3 1.0 %shard_map.84 = (f32[16,2,4,8,128]{4,3,2,1,0:T(8,128)S(1)}, s32[1024]{0:T(1024)S(4)}) custom-call(s32[1024]{0:T(1024)S(1)} %reshape.22.codes_src, f32[3,32,256]{2,1,0:T(8,128)S(1)} %collective-permute-done.above_ref, f32[4,32,256]{2,1,0:T(8,128)S(1)} %collective-permute-done.1.below_ref, bf16[256,512]{1,0:T(8,128)(2,1)S(1)} %get-tuple-element.30.phi_high_ref, ...), custom_call_target="tpu_custom_call" | custom-call | tf_op jit(solution)/shard_map/pallas_call | solution.py:382
  14.3 0.0 copy-start.1
  14.4 19.0 %all_to_all.10 = f32[16,2,4,8,128]{4,3,2,1,0:T(8,128)S(1)} all-to-all(f32[16,2,4,8,128]{4,3,2,1,0:T(8,128)S(1)} %get-tuple-element.37), channel_id=1, replica_groups=mesh['clus'=16,'theta'=8] {'clus'}, dimensions={0} | all-to-all | bytes 1048576 | tf_op jit(solution)/shard_map/all_to_all | solution.py:473
  33.4 0.0 copy-done.1
  33.4 2.1 %translate.1 = f32[1024,128]{1,0:T(8,128)S(1)} custom-call(s32[1024]{0:T(1024)S(4)} %get-tuple-element.34.codes_ref, s32[32]{0:T(128)S(4)} %get-tuple-element.35.counts_ref, f32[1024,128]{1,0:T(8,128)S(1)} %bitcast.10, f32[640,128]{1,0:T(8,128)S(1)} %bitcast.12), custom_call_target="tpu_custom_call" | custom-call | tf_op jit(solution)/shard_map/translate/pallas_call | solution.py:402
  35.4 15.0 %all_to_all.11.local_ref = f32[16,2,4,8,128]{4,3,2,1,0:T(8,128)S(1)} all-to-all(f32[16,2,4,8,128]{4,3,2,1,0:T(8,128)S(1)} %bitcast.11), channel_id=1, replica_groups=mesh['clus'=16,'theta'=8] {'clus'}, dimensions={0} | all-to-all | bytes 1048576 | tf_op jit(solution)/shard_map/all_to_all | solution.py:475
  50.4 0.6 %shard_map.86 = f32[4,32,256]{2,1,0:T(8,128)S(1)} custom-call(f32[16,2,4,8,128]{4,3,2,1,0:T(8,128)S(1)} %all_to_all.11.local_ref, f32[4,2,32,512]{3,2,1,0:T(8,128)S(1)} %copy-done, bf16[256,512]{1,0:T(8,128)(2,1)S(1)} %get-tuple-element.30.phi_high_ref, bf16[256,512]{1,0:T(8,128)(2,1)S(1)} %get-tuple-element.31.phi_low_ref, ...), custom_call_target="tpu_custom_call" | custom-call | tf_op jit(solution)/shard_map/pallas_call | solution.py:382
  51.0 0.1 collective-permute-start.2
  51.1 0.6 %shard_map.87 = f32[3,32,256]{2,1,0:T(8,128)S(1)} custom-call(f32[16,2,4,8,128]{4,3,2,1,0:T(8,128)S(1)} %all_to_all.11.local_ref, f32[4,2,32,512]{3,2,1,0:T(8,128)S(1)} %copy-done, bf16[256,512]{1,0:T(8,128)(2,1)S(1)} %get-tuple-element.30.phi_high_ref, bf16[256,512]{1,0:T(8,128)(2,1)S(1)} %get-tuple-element.31.phi_low_ref, ...), custom_call_target="tpu_custom_call" | custom-call | tf_op jit(solution)/shard_map/pallas_call | solution.py:382
  51.7 4.2 %collective-permute-start.3 = (f32[3,32,256]{2,1,0:T(8,128)S(1)}, f32[3,32,256]{2,1,0:T(8,128)S(1)}, u32[]{:S(2)}, u32[]{:S(2)}) collective-permute-start(f32[3,32,256]{2,1,0:T(8,128)S(1)} %shard_map.87), channel_id=1, source_target_pairs={{0,7},{1,0},{2,1},{3,2},{4,3},{5,4},{6,5},{7,6},{8,15},{9,8},{10,9... | collective-permute-start | bytes 294920 | tf_op jit(solution)/shard_map/ppermute | solution.py:27
  55.9 1.9 %shard_map.85.own_ref = f32[2,512,128]{2,1,0:T(8,128)S(1)} custom-call(f32[16,2,4,8,128]{4,3,2,1,0:T(8,128)S(1)} %all_to_all.11.local_ref, f32[4,2,32,512]{3,2,1,0:T(8,128)S(1)} %copy-done, bf16[256,512]{1,0:T(8,128)(2,1)S(1)} %get-tuple-element.30.phi_high_ref, bf16[256,512]{1,0:T(8,128)(2,1)S(1)} %get-tuple-element.31.phi_low_ref, ...), custom_call_target="tpu_custom_call" | custom-call | tf_op jit(solution)/shard_map/pallas_call | solution.py:382
  57.8 0.3 collective-permute-done.3.bottom_ref
  58.1 0.0 collective-permute-done.2.top_ref
  58.2 0.9 %shard_map.88 = f32[512,256]{1,0:T(8,128)} custom-call(f32[2,512,128]{2,1,0:T(8,128)S(1)} %shard_map.85.own_ref, f32[4,32,256]{2,1,0:T(8,128)S(1)} %collective-permute-done.2.top_ref, f32[3,32,256]{2,1,0:T(8,128)S(1)} %collective-permute-done.3.bottom_ref), custom_call_target="tpu_custom_call" | custom-call | tf_op jit(solution)/shard_map/pallas_call | solution.py:382
Async XLA Ops:
  0.0 6.6 %copy-start = (f32[4,2,32,512]{3,2,1,0:T(8,128)S(1)}, f32[4,2,32,512]{3,2,1,0:T(8,128)}, u32[]{:S(2)}) copy-start(f32[4,2,32,512]{3,2,1,0:T(8,128)} %shift_ref.9) | copy-start | bytes 1572868
  1.5 11.9 %collective-permute-start.1 = (f32[4,32,256]{2,1,0:T(8,128)S(1)}, f32[4,32,256]{2,1,0:T(8,128)S(1)}, u32[]{:S(2)}, u32[]{:S(2)}) collective-permute-start(f32[4,32,256]{2,1,0:T(8,128)S(1)} %get-tuple-element.29), channel_id=1, source_target_pairs={{0,7},{1,0},{2,1},{3,2},{4,3},{5,4},{6,5},{7,6},{8,15},{9,8},{10,9... | collective-permute-start | bytes 393224 | tf_op jit(solution)/shard_map/ppermute | solution.py:27
  6.6 6.7 %collective-permute-start = (f32[3,32,256]{2,1,0:T(8,128)S(1)}, f32[3,32,256]{2,1,0:T(8,128)S(1)}, u32[]{:S(2)}, u32[]{:S(2)}) collective-permute-start(f32[3,32,256]{2,1,0:T(8,128)S(1)} %get-tuple-element.28), channel_id=1, source_target_pairs={{0,1},{1,2},{2,3},{3,4},{4,5},{5,6},{6,7},{7,0},{8,9},{9,10},{10,1... | collective-permute-start | bytes 294920 | tf_op jit(solution)/shard_map/ppermute | solution.py:27
  14.3 19.0 %copy-start.1 = (f32[40,2,2,512]{3,2,1,0:T(2,128)S(1)}, f32[40,2,2,512]{3,2,1,0:T(2,128)}, u32[]{:S(2)}) copy-start(f32[40,2,2,512]{3,2,1,0:T(2,128)} %param.12) | copy-start | bytes 983044
  51.0 7.1 %collective-permute-start.2 = (f32[4,32,256]{2,1,0:T(8,128)S(1)}, f32[4,32,256]{2,1,0:T(8,128)S(1)}, u32[]{:S(2)}, u32[]{:S(2)}) collective-permute-start(f32[4,32,256]{2,1,0:T(8,128)S(1)} %shard_map.86), channel_id=1, source_target_pairs={{0,1},{1,2},{2,3},{3,4},{4,5},{5,6},{6,7},{7,0},{8,9},{9,10},{10,1... | collective-permute-start | bytes 393224 | tf_op jit(solution)/shard_map/ppermute | solution.py:27
  51.7 6.4 %collective-permute-start.3 = (f32[3,32,256]{2,1,0:T(8,128)S(1)}, f32[3,32,256]{2,1,0:T(8,128)S(1)}, u32[]{:S(2)}, u32[]{:S(2)}) collective-permute-start(f32[3,32,256]{2,1,0:T(8,128)S(1)} %shard_map.87), channel_id=1, source_target_pairs={{0,7},{1,0},{2,1},{3,2},{4,3},{5,4},{6,5},{7,6},{8,15},{9,8},{10,9... | collective-permute-start | bytes 294920 | tf_op jit(solution)/shard_map/ppermute | solution.py:27

commit v9 on v8

--- a/solution.py
+++ b/solution.py
@@ -73,9 +73,27 @@
     return child, parent
 
 
-def edge_rows(child, parent):
-    child = jnp.where(child < 4, child - 4, child + 12)
-    return child, jnp.where(parent < 8, parent, parent + 16)
+def above_rows(child, parent):
+    return child - 4, parent
+
+
+def below_rows(child, parent):
+    return child + OWN, parent + ROWS - 8
+
+
+def side_table(bands, place):
+    row = lax.broadcasted_iota(jnp.int32, (8, 256), 0)
+    column = lax.broadcasted_iota(jnp.int32, (8, 256), 1)
+    tap = tap_of(column % 4, row, place)
+    part = column // 64
+    high, low = (value.astype(WHOLE) for value in halves(bands))
+    block = jnp.zeros((8, 256), WHOLE)
+    for t in range(8):
+        value = jnp.where(part == 1, low[:, t : t + 1], high[:, t : t + 1])
+        block = jnp.where(jnp.logical_and(tap == t, part < 3), value, block)
+    owner = (column % 64) // 4
+    blocks = [jnp.where(owner == plane, block, 0.0) for plane in range(16)]
+    return jnp.concatenate(blocks, axis=0).astype(HALF)
 
 
 def tap_of(child, parent, place):
@@ -156,7 +174,7 @@
 
 def own_forward_kernel(
     source_hbm, offset_hbm, counts_hbm, phi_ref, taps_ref, children_ref, shift_ref,
-    packed_ref, phi_high_ref, phi_low_ref, edge_ref, back_high_ref, back_low_ref,
+    packed_ref, phi_high_ref, phi_low_ref, above_ref, below_ref, back_high_ref, back_low_ref,
     up_ref, down_ref, codes_ref, counts_ref,
     fine_ref, source_ref, offset_ref, sems, *, kinds,
 ):
@@ -190,13 +208,13 @@
         spread(group)
         if group == 2:
             collect(0)
-    edge = jnp.concatenate([bands[:8] * first, bands[ROWS - 8 :] * last], axis=0)
-    edge_ref[...] = jnp.concatenate(halves(forward_table(edge, 16, 8, edge_rows)), axis=1)
+    above_ref[...] = side_table(bands[:8] * first, above_rows)
+    below_ref[...] = side_table(bands[ROWS - 8 :] * last, below_rows)
     back_high_ref[...], back_low_ref[...] = backward_table(taps, 8, 16, same)
     upper, lower = taps[:, :8] * first, taps[:, ROWS - 8 :] * last
-    table = backward_table(upper, 16, 4, lambda child, parent: (child - 4, parent))
+    table = backward_table(upper, 16, 4, above_rows)
     up_ref[...] = jnp.concatenate(table, axis=1)
-    table = backward_table(lower, 16, 4, lambda child, parent: (child + 16, parent + 24))
+    table = backward_table(lower, 16, 4, below_rows)
     down_ref[...] = jnp.concatenate(table, axis=1)
     for copy in copies:
         copy.wait()
@@ -222,35 +240,45 @@
     return real, imag
 
 
-def edge_forward_kernel(
-    codes_src, above_ref, below_ref, phi_high_ref, phi_low_ref, edge_ref,
-    shift_ref, packed_ref, out_ref, codes_ref, halo_ref, fine_ref, sem,
-):
-    codes = pltpu.make_async_copy(codes_src, codes_ref, sem)
-    codes.start()
-    for side in range(2):
-        lanes = slice(128 * side, 128 * side + 128)
-        halo_ref[side, pl.ds(0, PLANES, stride=8), :] = jnp.zeros((PLANES, 128), WHOLE)
-        for row in range(3):
-            halo_ref[side, pl.ds(row + 1, PLANES, stride=8), :] = above_ref[row, :, lanes]
-        for row in range(4):
-            halo_ref[side, pl.ds(row + 4, PLANES, stride=8), :] = below_ref[row, :, lanes]
-    phi = (phi_high_ref[...], phi_low_ref[...])
-    edge = edge_ref[...]
-    for parent in range(2):
-        mixed = dot3(halves(both_sides(halo_ref, 128 * parent, 128)), phi)
-        fine_ref[256 * parent : 256 * (parent + 1)] = table_times(edge, halves(mixed))
-    out_ref[4:12] = packed_ref[4:12]
-    for side in range(2):
+def edge_forward_kernel(side):
+    first, count = 12 * side, 3 + side
+
+    def kernel(*refs):
+        if side == 0:
+            codes_src, halo_in, phi_high_ref, phi_low_ref, table_ref, shift_ref = refs[:6]
+            _, out_ref, codes_ref, halo_ref, fine_ref, sem = refs[6:]
+            codes = pltpu.make_async_copy(codes_src, codes_ref, sem)
+            codes.start()
+        else:
+            halo_in, phi_high_ref, phi_low_ref, table_ref, shift_ref = refs[:5]
+            _, out_ref, halo_ref, fine_ref = refs[5:]
+        for half in range(2):
+            lanes = slice(128 * half, 128 * half + 128)
+            if side == 0:
+                halo_ref[half, pl.ds(0, PLANES, stride=4), :] = jnp.zeros((PLANES, 128), WHOLE)
+            for row in range(count):
+                rows = pl.ds(row + 4 - count, PLANES, stride=4)
+                halo_ref[half, rows, :] = halo_in[row, :, lanes]
+        phi = (phi_high_ref[...], phi_low_ref[...])
+        high, low = halves(dot3(halves(both_sides(halo_ref, 0, 128)), phi))
+        table = table_ref[...]
+        for parent in range(2):
+            rows = slice(64 * parent, 64 * parent + 64)
+            value = jnp.concatenate([high[rows], high[rows], low[rows], high[rows]], axis=0)
+            fine = jnp.dot(table, value, preferred_element_type=WHOLE)
+            fine_ref[128 * parent : 128 * parent + 128] = fine
         rows = slice(24 * side, 24 * side + 8)
         for parent in range(2):
             for pol in range(2):
-                real, imag = gathered(fine_ref, shift_ref, parent, pol, 16, 8 * side, rows)
+                real, imag = gathered(fine_ref, shift_ref, parent, pol, 8, 0, rows)
                 for part, value in enumerate((real, imag)):
                     for pair, tile in enumerate(swap_blocks(lane_blocks(value))):
-                        at = (12 * side + pair, parent, 2 * pol + part)
-                        out_ref[at] = packed_ref[at] + tile
-    codes.wait()
+                        at = (first + pair, parent, 2 * pol + part)
+                        out_ref[at] = out_ref[at] + tile
+        if side == 0:
+            codes.wait()
+
+    return kernel
 
 
 def spread_back(local_ref, shift_ref, parent, pol, blocks, high_ref, low_ref):
@@ -318,7 +346,7 @@
                 own_ref[side, 128 * group : 128 * (group + 1)] = result[:, lanes]
 
 
-def translate_kernel(codes_ref, counts_ref, field_ref, operator_ref, out_ref, table_ref):
+def translate_kernel(codes_ref, counts_ref, field_ref, operator_ref, out_ref, table_ref, sum_ref):
     parents = counts_ref.shape[0]
     kinds = operator_ref.shape[0] // 16
     for kind in range(kinds):
@@ -327,6 +355,9 @@
         for at, value in enumerate((c, d - c, c + d)):
             table_ref[24 * kind + 8 * at : 24 * kind + 8 * at + 8] = value
     table_ref[24 * kinds : 24 * kinds + 24] = jnp.zeros((24, 128), WHOLE)
+    for at in range(2 * parents):
+        rows = slice(16 * at, 16 * at + 8)
+        sum_ref[8 * at : 8 * at + 8] = field_ref[rows] + field_ref[16 * at + 8 : 16 * at + 16]
 
     def one_pair(pair, carry):
         def some_slots(step, sums):
@@ -337,6 +368,7 @@
                     code = codes_ref[slot]
                     source = pl.multiple_of(code & 0xFFFF, 8)
                     offset = pl.multiple_of(code >> 16, 8)
+                    half = pl.multiple_of((code & 0xFFFF) >> 1, 8)
                     c = table_ref[pl.ds(offset, 8), :]
                     less = table_ref[pl.ds(offset + 8, 8), :]
                     more = table_ref[pl.ds(offset + 16, 8), :]
@@ -344,7 +376,7 @@
                         at = member * 6 + pol * 3
                         a = field_ref[pl.ds(source + pol * 16, 8), :]
                         b = field_ref[pl.ds(source + (pol * 16 + 8), 8), :]
-                        sums[at] = sums[at] + c * (a + b)
+                        sums[at] = sums[at] + c * sum_ref[pl.ds(half + pol * 8, 8), :]
                         sums[at + 1] = sums[at + 1] + a * less
                         sums[at + 2] = sums[at + 2] + b * more
             return tuple(sums)
@@ -376,7 +408,7 @@
     return pltpu.with_memory_space_constraint(value, pltpu.HBM)
 
 
-def call(kernel, outs, scratch, *operands, raw=0, out_specs=None):
+def call(kernel, outs, scratch, *operands, raw=0, out_specs=None, aliases={}):
     vmem = pl.BlockSpec(memory_space=pltpu.VMEM)
     hbm = pl.BlockSpec(memory_space=pltpu.HBM)
     return pl.pallas_call(
@@ -385,6 +417,7 @@
         in_specs=[hbm] * raw + [vmem] * (len(operands) - raw),
         out_specs=out_specs if out_specs is not None else jax.tree.map(lambda _: vmem, outs),
         scratch_shapes=scratch,
+        input_output_aliases=aliases,
         compiler_params=pltpu.CompilerParams(vmem_limit_bytes=GRANT),
     )(*map(in_hbm, operands[:raw]), *map(in_vmem, operands[raw:]))
 
@@ -404,7 +437,10 @@
         out_shape=jax.ShapeDtypeStruct(field.shape, WHOLE),
         in_specs=[smem, smem, vmem, vmem],
         out_specs=vmem,
-        scratch_shapes=[pltpu.VMEM((operators.shape[0] * 3 // 2 + 24, 128), WHOLE)],
+        scratch_shapes=[
+            pltpu.VMEM((operators.shape[0] * 3 // 2 + 24, 128), WHOLE),
+            pltpu.VMEM((field.shape[0] // 2, 128), WHOLE),
+        ],
         compiler_params=pltpu.CompilerParams(vmem_limit_bytes=GRANT),
         name="translate",
     )(in_smem(codes), in_smem(counts), in_vmem(field), in_vmem(operators))
@@ -449,7 +485,7 @@
     )
     above = shifted_ring(lower, "theta", 1)
     below = shifted_ring(upper, "theta", -1)
-    tables = (half(256, 512),) * 2 + (half(256, 256),) + (half(128, 256),) * 2
+    tables = (half(256, 512),) * 2 + (half(128, 256),) * 4
     packed, *tables, codes, counts = call(
         functools.partial(own_forward_kernel, kinds=translators.shape[0]),
         (whole(16, 2, 4, 8, 128),) + tables + (half(64, 256),) * 2
@@ -459,15 +495,20 @@
             pltpu.VMEM(far_source.shape, jnp.int32), dma((3,)),
         ],
         far_source, far_offset, far_count, phi, taps, planes, child_shift,
-        raw=3, out_specs=(vmem,) * 9 + (smem,),
-    )
-    *phi, edge, back_high, back_low, up_table, down_table = tables
+        raw=3, out_specs=(vmem,) * 10 + (smem,),
+    )
+    *phi, above_table, below_table, back_high, back_low, up_table, down_table = tables
     operators = in_vmem(operator_rows(translators))
+    scratch = [whole(2, 128, 128), whole(256, SAMPLES)]
     packed, codes = call(
-        edge_forward_kernel,
-        (whole(16, 2, 4, 8, 128), pltpu.SMEM((codes.size,), jnp.int32)),
-        [whole(2, 256, 128), whole(512, SAMPLES), dma],
-        codes.reshape(-1), above, below, *phi, edge, child_shift, packed, out_specs=(vmem, smem),
+        edge_forward_kernel(0),
+        (whole(16, 2, 4, 8, 128), pltpu.SMEM((codes.size,), jnp.int32)), scratch + [dma],
+        codes.reshape(-1), above, *phi, above_table, child_shift, packed,
+        out_specs=(vmem, smem), aliases={6: 0},
+    )
+    packed = call(
+        edge_forward_kernel(1), whole(16, 2, 4, 8, 128), scratch,
+        below, *phi, below_table, child_shift, packed, aliases={5: 0},
     )
     packed, operators = lax.optimization_barrier((packed, operators))
     field = lax.all_to_all(packed, "clus", 0, 0)

time: 59.3 us -> 59.6 us (level)
    pallas_call x7 -> x8, Pallas kernels: 9.02 us -> 9.12 us  [call(): pl.pallas_call(kernel, out_shape=outs, in_specs=[hbm] * raw + [vmem] * (l...]
  transfers between devices with their start and end apart: 4 -> 4, of which waited for: 2 -> 2; matrix products, arithmetic and copies ran while one was open for 0% -> 0% of each run, Pallas kernels for 9% -> 10%
where the time goes in v9:
time: 59.6 us; the launch traced here: 59.3 us
  blocking collectives  34 us (57%)
  Pallas kernels  11.3 us (19%)
  starting transfers between devices  9.41 us (16%)
  waiting for transfers between devices  4.46 us (7%)
    all_to_all x1, blocking collectives, on_device(): field = lax.all_to_all(packed, 'clus', 0, 0)  19 us
    all_to_all x1, blocking collectives, on_device(): local = lax.all_to_all(summed.reshape(packed.shape), 'clus', 0, 0)  15 us
    ppermute x4, starting transfers between devices, shifted_ring(): lax.ppermute(value, axis, [(i, (i + step) % count) for i in range(count)])  9.41 us
    pallas_call x8, Pallas kernels, call(): pl.pallas_call(kernel, out_shape=outs, in_specs=[hbm] * raw + [vmem] * (l...  9.12 us
    ppermute x4, waiting for transfers between devices, shifted_ring(): lax.ppermute(value, axis, [(i, (i + step) % count) for i in range(count)])  4.46 us
    pallas_call x1, Pallas kernels, translate(): pl.pallas_call(translate_kernel, out_shape=jax.ShapeDtypeStruct(field.sha...  2.2 us
  transfers between devices with their start and end apart: 4, of which 2 were waited for; matrix products, arithmetic and copies ran while one was open for 0% of the time, Pallas kernels for 10%

profile of v9, /device:TPU:0, one launch (start us, length us, event | category | flops | bytes accessed | tf_op | source)
XLA Modules:
  0.0 59.3 jit_solution(9334613326621731915)
XLA Ops:
  0.0 0.0 copy-start
  0.0 1.4 %shard_map.82 = (f32[2,512,128]{2,1,0:T(8,128)S(1)}, f32[8,32]{1,0:T(8,128)S(1)}, f32[256,512]{1,0:T(8,128)S(1)}, f32[4,32,256]{2,1,0:T(8,128)S(1)}, f32[3,32,256]{2,1,0:T(8,128)S(1)}) custom-call(f32[512,256]{1,0:T(8,128)} %bitcast.13, f32[8,32]{1,0:T(8,128)} %bitcast.14, f32[256,512]{1,0:T(8,128)} %phi_hbm.1), custom_call_target="tpu_custom_call" | custom-call | tf_op jit(solution)/shard_map/pallas_call | solution.py:414
  1.5 5.1 %collective-permute-start.1 = (f32[4,32,256]{2,1,0:T(8,128)S(1)}, f32[4,32,256]{2,1,0:T(8,128)S(1)}, u32[]{:S(2)}, u32[]{:S(2)}) collective-permute-start(f32[4,32,256]{2,1,0:T(8,128)S(1)} %get-tuple-element.36), channel_id=1, source_target_pairs={{0,7},{1,0},{2,1},{3,2},{4,3},{5,4},{6,5},{7,6},{8,15},{9,8},{10,9... | collective-permute-start | bytes 393224 | tf_op jit(solution)/shard_map/ppermute | solution.py:27
  6.6 0.0 collective-permute-start
  6.6 0.0 copy-done
  6.6 2.6 %shard_map.83 = (f32[16,2,4,8,128]{4,3,2,1,0:T(8,128)S(1)}, bf16[256,512]{1,0:T(8,128)(2,1)S(1)}, bf16[256,512]{1,0:T(8,128)(2,1)S(1)}, bf16[128,256]{1,0:T(8,12...) custom-call(s32[32,32]{1,0:T(8,128)} %source_hbm.1, ...), custom_call_target="tpu_custom_call" | custom-call | tf_op jit(solution)/shard_map/pallas_call | solution.py:414
  9.2 0.1 reshape.22.refs_0_
  9.2 4.1 %collective-permute-done.refs_1_ = f32[3,32,256]{2,1,0:T(8,128)S(1)} collective-permute-done((f32[3,32,256]{2,1,0:T(8,128)S(1)}, f32[3,32,256]{2,1,0:T(8,128)S(1)}, u32[]{:S(2)}, u32[]{:S(2)}) %collective-permute-start) | collective-permute-done | bytes 98336 | tf_op jit(solution)/shard_map/ppermute | solution.py:27
  13.3 0.6 %shard_map.84 = (f32[16,2,4,8,128]{4,3,2,1,0:T(8,128)S(1)}, s32[1024]{0:T(1024)S(4)}) custom-call(s32[1024]{0:T(1024)S(1)} %reshape.22.refs_0_, f32[3,32,256]{2,1,0:T(8,128)S(1)} %collective-permute-done.refs_1_, bf16[256,512]{1,0:T(8,128)(2,1)S(1)} %get-tuple-element.30.refs_2_.refs_1_.phi_high_ref, ...), custom_call_target="tpu_custom_call", output_to_operand_aliasing={{0}: (6, {})} | custom-call | tf_op jit(solution)/shard_map/pallas_call | solution.py:414
  14.0 0.0 collective-permute-done.1.refs_0_
  14.0 0.5 shard_map.85
  14.5 0.0 copy-start.1
  14.5 19.0 %all_to_all.10 = f32[16,2,4,8,128]{4,3,2,1,0:T(8,128)S(1)} all-to-all(f32[16,2,4,8,128]{4,3,2,1,0:T(8,128)S(1)} %shard_map.85), channel_id=1, replica_groups=mesh['clus'=16,'theta'=8] {'clus'}, dimensions={0} | all-to-all | bytes 1048576 | tf_op jit(solution)/shard_map/all_to_all | solution.py:514
  33.5 0.0 copy-done.1
  33.5 2.2 %translate.1 = f32[1024,128]{1,0:T(8,128)S(1)} custom-call(s32[1024]{0:T(1024)S(4)} %get-tuple-element.34.codes_ref, s32[32]{0:T(128)S(4)} %get-tuple-element.35.counts_ref, f32[1024,128]{1,0:T(8,128)S(1)} %bitcast.10, f32[640,128]{1,0:T(8,128)S(1)} %bitcast.12), custom_call_target="tpu_custom_call" | custom-call | tf_op jit(solution)/shard_map/translate/pallas_call | solution.py:435
  35.7 15.0 %all_to_all.11.local_ref = f32[16,2,4,8,128]{4,3,2,1,0:T(8,128)S(1)} all-to-all(f32[16,2,4,8,128]{4,3,2,1,0:T(8,128)S(1)} %bitcast.11), channel_id=1, replica_groups=mesh['clus'=16,'theta'=8] {'clus'}, dimensions={0} | all-to-all | bytes 1048576 | tf_op jit(solution)/shard_map/all_to_all | solution.py:516
  50.7 0.6 %shard_map.87 = f32[4,32,256]{2,1,0:T(8,128)S(1)} custom-call(f32[16,2,4,8,128]{4,3,2,1,0:T(8,128)S(1)} %all_to_all.11.local_ref, f32[4,2,32,512]{3,2,1,0:T(8,128)S(1)} %copy-done, bf16[256,512]{1,0:T(8,128)(2,1)S(1)} %get-tuple-element.30.refs_2_.refs_1_.phi_high_ref, bf16[256,512]{1,0:T(8,128)(2,1)S(1)} %get-tuple-element.31.refs_3_.refs_2_.phi_low_ref, ...), custom_call_target="tpu_custom_call" | custom-call | tf_op jit(solution)/shard_map/pallas_call | solution.py:414
  51.3 0.1 collective-permute-start.2
  51.4 0.6 %shard_map.88 = f32[3,32,256]{2,1,0:T(8,128)S(1)} custom-call(f32[16,2,4,8,128]{4,3,2,1,0:T(8,128)S(1)} %all_to_all.11.local_ref, f32[4,2,32,512]{3,2,1,0:T(8,128)S(1)} %copy-done, bf16[256,512]{1,0:T(8,128)(2,1)S(1)} %get-tuple-element.30.refs_2_.refs_1_.phi_high_ref, bf16[256,512]{1,0:T(8,128)(2,1)S(1)} %get-tuple-element.31.refs_3_.refs_2_.phi_low_ref, ...), custom_call_target="tpu_custom_call" | custom-call | tf_op jit(solution)/shard_map/pallas_call | solution.py:414
  52.0 4.2 %collective-permute-start.3 = (f32[3,32,256]{2,1,0:T(8,128)S(1)}, f32[3,32,256]{2,1,0:T(8,128)S(1)}, u32[]{:S(2)}, u32[]{:S(2)}) collective-permute-start(f32[3,32,256]{2,1,0:T(8,128)S(1)} %shard_map.88), channel_id=1, source_target_pairs={{0,7},{1,0},{2,1},{3,2},{4,3},{5,4},{6,5},{7,6},{8,15},{9,8},{10,9... | collective-permute-start | bytes 294920 | tf_op jit(solution)/shard_map/ppermute | solution.py:27
  56.2 1.9 %shard_map.86.own_ref = f32[2,512,128]{2,1,0:T(8,128)S(1)} custom-call(f32[16,2,4,8,128]{4,3,2,1,0:T(8,128)S(1)} %all_to_all.11.local_ref, f32[4,2,32,512]{3,2,1,0:T(8,128)S(1)} %copy-done, bf16[256,512]{1,0:T(8,128)(2,1)S(1)} %get-tuple-element.30.refs_2_.refs_1_.phi_high_ref, bf16[256,512]{1,0:T(8,128)(2,1)S(1)} %get-tuple-element.31.refs_3_.refs_2_.phi_low_ref, ...), custom_call_target="tpu_custom_call" | custom-call | tf_op jit(solution)/shard_map/pallas_call | solution.py:414
  58.1 0.3 collective-permute-done.3.bottom_ref
  58.4 0.0 collective-permute-done.2.top_ref
  58.4 0.9 %shard_map.89 = f32[512,256]{1,0:T(8,128)} custom-call(f32[2,512,128]{2,1,0:T(8,128)S(1)} %shard_map.86.own_ref, f32[4,32,256]{2,1,0:T(8,128)S(1)} %collective-permute-done.2.top_ref, f32[3,32,256]{2,1,0:T(8,128)S(1)} %collective-permute-done.3.bottom_ref), custom_call_target="tpu_custom_call" | custom-call | tf_op jit(solution)/shard_map/pallas_call | solution.py:414
Async XLA Ops:
  0.0 6.6 %copy-start = (f32[4,2,32,512]{3,2,1,0:T(8,128)S(1)}, f32[4,2,32,512]{3,2,1,0:T(8,128)}, u32[]{:S(2)}) copy-start(f32[4,2,32,512]{3,2,1,0:T(8,128)} %shift_ref.7) | copy-start | bytes 1572868
  1.5 12.5 %collective-permute-start.1 = (f32[4,32,256]{2,1,0:T(8,128)S(1)}, f32[4,32,256]{2,1,0:T(8,128)S(1)}, u32[]{:S(2)}, u32[]{:S(2)}) collective-permute-start(f32[4,32,256]{2,1,0:T(8,128)S(1)} %get-tuple-element.36), channel_id=1, source_target_pairs={{0,7},{1,0},{2,1},{3,2},{4,3},{5,4},{6,5},{7,6},{8,15},{9,8},{10,9... | collective-permute-start | bytes 393224 | tf_op jit(solution)/shard_map/ppermute | solution.py:27
  6.6 6.7 %collective-permute-start = (f32[3,32,256]{2,1,0:T(8,128)S(1)}, f32[3,32,256]{2,1,0:T(8,128)S(1)}, u32[]{:S(2)}, u32[]{:S(2)}) collective-permute-start(f32[3,32,256]{2,1,0:T(8,128)S(1)} %get-tuple-element.29), channel_id=1, source_target_pairs={{0,1},{1,2},{2,3},{3,4},{4,5},{5,6},{6,7},{7,0},{8,9},{9,10},{10,1... | collective-permute-start | bytes 294920 | tf_op jit(solution)/shard_map/ppermute | solution.py:27
  14.5 19.0 %copy-start.1 = (f32[40,2,2,512]{3,2,1,0:T(2,128)S(1)}, f32[40,2,2,512]{3,2,1,0:T(2,128)}, u32[]{:S(2)}) copy-start(f32[40,2,2,512]{3,2,1,0:T(2,128)} %param.12) | copy-start | bytes 983044
  51.3 7.1 %collective-permute-start.2 = (f32[4,32,256]{2,1,0:T(8,128)S(1)}, f32[4,32,256]{2,1,0:T(8,128)S(1)}, u32[]{:S(2)}, u32[]{:S(2)}) collective-permute-start(f32[4,32,256]{2,1,0:T(8,128)S(1)} %shard_map.87), channel_id=1, source_target_pairs={{0,1},{1,2},{2,3},{3,4},{4,5},{5,6},{6,7},{7,0},{8,9},{9,10},{10,1... | collective-permute-start | bytes 393224 | tf_op jit(solution)/shard_map/ppermute | solution.py:27
  52.0 6.4 %collective-permute-start.3 = (f32[3,32,256]{2,1,0:T(8,128)S(1)}, f32[3,32,256]{2,1,0:T(8,128)S(1)}, u32[]{:S(2)}, u32[]{:S(2)}) collective-permute-start(f32[3,32,256]{2,1,0:T(8,128)S(1)} %shard_map.88), channel_id=1, source_target_pairs={{0,7},{1,0},{2,1},{3,2},{4,3},{5,4},{6,5},{7,6},{8,15},{9,8},{10,9... | collective-permute-start | bytes 294920 | tf_op jit(solution)/shard_map/ppermute | solution.py:27

commit v10 on v9

--- a/solution.py
+++ b/solution.py
@@ -138,7 +138,7 @@
 
 
 def cut_kernel(
-    children_hbm, taps_hbm, phi_hbm, children_ref, taps_ref, phi_ref, upper_ref, lower_ref, sems
+    children_hbm, taps_hbm, children_ref, taps_ref, upper_ref, lower_ref, sems
 ):
     chunks = [slice(128 * i, 128 * i + 128) for i in range(4)]
     copies = [
@@ -154,8 +154,6 @@
         copy.start()
     taps = pltpu.make_async_copy(taps_hbm, taps_ref, sems.at[8])
     taps.start()
-    phi = pltpu.make_async_copy(phi_hbm, phi_ref, sems.at[9])
-    phi.start()
     for at, copy in enumerate(copies):
         copy.wait()
         i, side = divmod(at, 2)
@@ -165,7 +163,6 @@
                 value = children_ref[side, rows, :]
                 ref[row, 8 * i : 8 * i + 8, 128 * side : 128 * side + 128] = value
     taps.wait()
-    phi.wait()
 
 
 def both_sides(ref, first, count):
@@ -173,12 +170,15 @@
 
 
 def own_forward_kernel(
-    source_hbm, offset_hbm, counts_hbm, phi_ref, taps_ref, children_ref, shift_ref,
-    packed_ref, phi_high_ref, phi_low_ref, above_ref, below_ref, back_high_ref, back_low_ref,
+    shift_hbm, source_hbm, offset_hbm, counts_hbm, phi_ref, taps_ref, children_ref,
+    packed_ref, shift_ref, phi_high_ref, phi_low_ref, above_ref, below_ref, back_high_ref, back_low_ref,
     up_ref, down_ref, codes_ref, counts_ref,
     fine_ref, source_ref, offset_ref, sems, *, kinds,
 ):
-    pairs = ((source_hbm, source_ref), (offset_hbm, offset_ref), (counts_hbm, counts_ref))
+    pairs = (
+        (shift_hbm, shift_ref), (source_hbm, source_ref), (offset_hbm, offset_ref),
+        (counts_hbm, counts_ref),
+    )
     copies = [pltpu.make_async_copy(*pair, sems.at[i]) for i, pair in enumerate(pairs)]
     for copy in copies:
         copy.start()
@@ -204,10 +204,13 @@
                     for pair, tile in enumerate(swap_blocks(lane_blocks(value))):
                         packed_ref[4 * block + pair, parent, 2 * pol + part] = tile
 
-    for group in range(4):
-        spread(group)
-        if group == 2:
-            collect(0)
+    spread(0)
+    spread(1)
+    for copy in copies:
+        copy.wait()
+    spread(2)
+    collect(0)
+    spread(3)
     above_ref[...] = side_table(bands[:8] * first, above_rows)
     below_ref[...] = side_table(bands[ROWS - 8 :] * last, below_rows)
     back_high_ref[...], back_low_ref[...] = backward_table(taps, 8, 16, same)
@@ -216,8 +219,6 @@
     up_ref[...] = jnp.concatenate(table, axis=1)
     table = backward_table(lower, 16, 4, below_rows)
     down_ref[...] = jnp.concatenate(table, axis=1)
-    for copy in copies:
-        copy.wait()
     lane = lax.broadcasted_iota(jnp.int32, (1, LIST), 1)
     for parent in range(source_ref.shape[0]):
         live = lane < counts_ref[parent]
@@ -281,7 +282,7 @@
     return kernel
 
 
-def spread_back(local_ref, shift_ref, parent, pol, blocks, high_ref, low_ref):
+def spread_back(local_ref, shift_ref, parent, pol, blocks):
     parts = []
     for part in range(2):
         pieces = []
@@ -297,26 +298,25 @@
             d = shift_ref[kid, 1, 2 * first : 2 * first + 8]
             real.append(c * a + d * b)
             imag.append(c * b - d * a)
-        height = 16 * len(blocks)
-        at = ((parent * KIDS + kid) * 2 + pol) * height
-        value = halves(jnp.concatenate(real + imag, axis=0))
-        high_ref[at : at + height], low_ref[at : at + height] = value
+        yield kid, halves(jnp.concatenate(real + imag, axis=0))
 
 
 def edge_back_kernel(first, skipped):
     def kernel(
-        local_ref, shift_ref, phi_high_ref, phi_low_ref, table_ref,
-        out_ref, high_ref, low_ref, narrow_ref, result_ref,
+        local_ref, shift_ref, phi_high_ref, phi_low_ref, table_ref, out_ref, result_ref,
     ):
         phi = (phi_high_ref[...], phi_low_ref[...])
         table = table_ref[...]
+        narrow = []
         for parent in range(2):
+            pieces = {}
             for pol in range(2):
-                spread_back(local_ref, shift_ref, parent, pol, (first,), high_ref, low_ref)
-            rows = slice(128 * parent, 128 * (parent + 1))
-            narrow = table_times(table, (high_ref[rows], low_ref[rows]))
-            narrow_ref[64 * parent : 64 * (parent + 1)] = narrow
-        result = dot3(halves(narrow_ref[...]), phi, contract=1)
+                for kid, value in spread_back(local_ref, shift_ref, parent, pol, (first,)):
+                    pieces[kid, pol] = value
+            order = [(kid, pol) for kid in range(KIDS) for pol in range(2)]
+            value = [jnp.concatenate([pieces[at][i] for at in order], axis=0) for i in range(2)]
+            narrow.append(table_times(table, value))
+        result = dot3(halves(jnp.concatenate(narrow, axis=0)), phi, contract=1)
         for side in range(2):
             lanes = slice(128 * side, 128 * side + 128)
             result_ref[side] = result[:, lanes]
@@ -336,7 +336,9 @@
 
     for parent in range(2):
         for pol in range(2):
-            spread_back(local_ref, shift_ref, parent, pol, (0, 4, 8, 12), high_ref, low_ref)
+            for kid, value in spread_back(local_ref, shift_ref, parent, pol, (0, 4, 8, 12)):
+                at = ((parent * KIDS + kid) * 2 + pol) * 64
+                high_ref[at : at + 64], low_ref[at : at + 64] = value
         for group in (2 * parent, 2 * parent + 1):
             rows = slice(256 * group, 256 * (group + 1))
             narrowed = dot3(table, (high_ref[rows], low_ref[rows]))
@@ -446,20 +448,19 @@
     )(in_smem(codes), in_smem(counts), in_vmem(field), in_vmem(operators))
 
 
-def merge_kernel(own_ref, top_ref, bottom_ref, out_hbm, out_ref, sems):
+def merge_kernel(_, top_ref, bottom_ref, out_hbm, own_ref, sems):
     copies = []
     for i in range(4):
         chunk = slice(128 * i, 128 * i + 128)
         for side in range(2):
             lanes = slice(128 * side, 128 * side + 128)
-            out_ref[side, chunk] = own_ref[side, chunk]
             for ref, first, count in ((top_ref, 0, 4), (bottom_ref, OWN - 3, 3)):
                 for row in range(count):
                     rows = pl.ds(128 * i + first + row, 8, stride=OWN)
                     value = own_ref[side, rows, :] + ref[row, 8 * i : 8 * i + 8, lanes]
-                    out_ref[side, rows, :] = value
+                    own_ref[side, rows, :] = value
             target = out_hbm.at[chunk, lanes]
-            copy = pltpu.make_async_copy(out_ref.at[side, chunk], target, sems.at[2 * i + side])
+            copy = pltpu.make_async_copy(own_ref.at[side, chunk], target, sems.at[2 * i + side])
             copy.start()
             copies.append(copy)
     for copy in copies:
@@ -475,27 +476,27 @@
     vmem = pl.BlockSpec(memory_space=pltpu.VMEM)
     smem = pl.BlockSpec(memory_space=pltpu.SMEM)
     dma = pltpu.SemaphoreType.DMA
-    planes, taps, phi, upper, lower = call(
+    planes, taps, upper, lower = call(
         cut_kernel,
         (
-            whole(2, PLANES * OWN, 128), whole(8, ROWS), whole(*phi_interp.shape),
-            whole(4, PLANES, PHI), whole(3, PLANES, PHI),
+            whole(2, PLANES * OWN, 128), whole(8, ROWS), whole(4, PLANES, PHI),
+            whole(3, PLANES, PHI),
         ),
-        [dma((10,))], children.reshape(-1, PHI), theta_band.T, phi_interp, raw=3,
+        [dma((9,))], children.reshape(-1, PHI), theta_band.T, raw=2,
     )
     above = shifted_ring(lower, "theta", 1)
     below = shifted_ring(upper, "theta", -1)
     tables = (half(256, 512),) * 2 + (half(128, 256),) * 4
-    packed, *tables, codes, counts = call(
+    packed, shift, *tables, codes, counts = call(
         functools.partial(own_forward_kernel, kinds=translators.shape[0]),
-        (whole(16, 2, 4, 8, 128),) + tables + (half(64, 256),) * 2
+        (whole(16, 2, 4, 8, 128), whole(*child_shift.shape)) + tables + (half(64, 256),) * 2
         + (pltpu.VMEM(far_source.shape, jnp.int32), pltpu.SMEM(far_count.shape, jnp.int32)),
         [
             whole(1024, SAMPLES), pltpu.VMEM(far_source.shape, jnp.int32),
-            pltpu.VMEM(far_source.shape, jnp.int32), dma((3,)),
+            pltpu.VMEM(far_source.shape, jnp.int32), dma((4,)),
         ],
-        far_source, far_offset, far_count, phi, taps, planes, child_shift,
-        raw=3, out_specs=(vmem,) * 10 + (smem,),
+        child_shift, far_source, far_offset, far_count, phi_interp, taps, planes,
+        raw=4, out_specs=(vmem,) * 11 + (smem,),
     )
     *phi, above_table, below_table, back_high, back_low, up_table, down_table = tables
     operators = in_vmem(operator_rows(translators))
@@ -503,35 +504,36 @@
     packed, codes = call(
         edge_forward_kernel(0),
         (whole(16, 2, 4, 8, 128), pltpu.SMEM((codes.size,), jnp.int32)), scratch + [dma],
-        codes.reshape(-1), above, *phi, above_table, child_shift, packed,
+        codes.reshape(-1), above, *phi, above_table, shift, packed,
         out_specs=(vmem, smem), aliases={6: 0},
     )
     packed = call(
         edge_forward_kernel(1), whole(16, 2, 4, 8, 128), scratch,
-        below, *phi, below_table, child_shift, packed, aliases={5: 0},
+        below, *phi, below_table, shift, packed, aliases={5: 0},
     )
     packed, operators = lax.optimization_barrier((packed, operators))
     field = lax.all_to_all(packed, "clus", 0, 0)
     summed = translate(field, codes, counts, operators)
     local = lax.all_to_all(summed.reshape(packed.shape), "clus", 0, 0)
-    scratch = [half(256, SAMPLES)] * 2 + [whole(128, SAMPLES), whole(2, 128, 128)]
+    scratch = [whole(2, 128, 128)]
     down = call(
         edge_back_kernel(12, 0), whole(4, PLANES, PHI), scratch,
-        local, child_shift, *phi, down_table,
+        local, shift, *phi, down_table,
     )
     from_below = shifted_ring(down, "theta", 1)
     up = call(
         edge_back_kernel(0, 1), whole(3, PLANES, PHI), scratch,
-        local, child_shift, *phi, up_table,
+        local, shift, *phi, up_table,
     )
     from_above = shifted_ring(up, "theta", -1)
     own = call(
         own_back_kernel, whole(2, PLANES * OWN, 128), [half(1024, SAMPLES)] * 2,
-        local, child_shift, *phi, back_high, back_low,
-    )
-    result = call(
-        merge_kernel, jax.ShapeDtypeStruct((PLANES * OWN, PHI), WHOLE),
-        [whole(2, PLANES * OWN, 128), dma((8,))], own, from_below, from_above, out_specs=hbm,
+        local, shift, *phi, back_high, back_low,
+    )
+    result, _ = call(
+        merge_kernel,
+        (jax.ShapeDtypeStruct((PLANES * OWN, PHI), WHOLE), whole(2, PLANES * OWN, 128)),
+        [dma((8,))], own, from_below, from_above, out_specs=(hbm, vmem), aliases={0: 1},
     )
     return result.reshape(children.shape)
 

time: 59.6 us -> 59.3 us (level)
  transfers between devices with their start and end apart: 4 -> 4, of which waited for: 2 -> 2; matrix products, arithmetic and copies ran while one was open for 0% -> 0% of each run, Pallas kernels for 10% -> 9%
where the time goes in v10:
time: 59.3 us; the launch traced here: 59.1 us
  blocking collectives  34 us (57%)
  Pallas kernels  10.8 us (18%)
  starting transfers between devices  9.41 us (16%)
  waiting for transfers between devices  4.76 us (8%)
    all_to_all x1, blocking collectives, on_device(): field = lax.all_to_all(packed, 'clus', 0, 0)  19 us
    all_to_all x1, blocking collectives, on_device(): local = lax.all_to_all(summed.reshape(packed.shape), 'clus', 0, 0)  15 us
    ppermute x4, starting transfers between devices, shifted_ring(): lax.ppermute(value, axis, [(i, (i + step) % count) for i in range(count)])  9.41 us
    pallas_call x8, Pallas kernels, call(): pl.pallas_call(kernel, out_shape=outs, in_specs=[hbm] * raw + [vmem] * (l...  8.58 us
    ppermute x4, waiting for transfers between devices, shifted_ring(): lax.ppermute(value, axis, [(i, (i + step) % count) for i in range(count)])  4.76 us
    pallas_call x1, Pallas kernels, translate(): pl.pallas_call(translate_kernel, out_shape=jax.ShapeDtypeStruct(field.sha...  2.2 us
  transfers between devices with their start and end apart: 4, of which 2 were waited for; matrix products, arithmetic and copies ran while one was open for 0% of the time, Pallas kernels for 9%

profile of v10, /device:TPU:0, one launch (start us, length us, event | category | flops | bytes accessed | tf_op | source)
XLA Modules:
  0.0 59.1 jit_solution(14211309703770816189)
XLA Ops:
  0.0 0.0 copy-start
  0.0 1.2 %shard_map.82 = (f32[2,512,128]{2,1,0:T(8,128)S(1)}, f32[8,32]{1,0:T(8,128)S(1)}, f32[4,32,256]{2,1,0:T(8,128)S(1)}, f32[3,32,256]{2,1,0:T(8,128)S(1)}) custom-call(f32[512,256]{1,0:T(8,128)} %bitcast.13, f32[8,32]{1,0:T(8,128)} %bitcast.14), custom_call_target="tpu_custom_call" | custom-call | tf_op jit(solution)/shard_map/pallas_call | solution.py:416
  1.2 5.1 %collective-permute-start.1 = (f32[4,32,256]{2,1,0:T(8,128)S(1)}, f32[4,32,256]{2,1,0:T(8,128)S(1)}, u32[]{:S(2)}, u32[]{:S(2)}) collective-permute-start(f32[4,32,256]{2,1,0:T(8,128)S(1)} %get-tuple-element.37), channel_id=1, source_target_pairs={{0,7},{1,0},{2,1},{3,2},{4,3},{5,4},{6,5},{7,6},{8,15},{9,8},{10,9... | collective-permute-start | bytes 393224 | tf_op jit(solution)/shard_map/ppermute | solution.py:27
  6.4 0.0 collective-permute-start
  6.4 0.0 copy-done
  6.4 2.3 %shard_map.83 = (f32[16,2,4,8,128]{4,3,2,1,0:T(8,128)S(1)}, f32[4,2,32,512]{3,2,1,0:T(8,128)S(1)}, bf16[256,512]{1,0:T(8,128)(2,1)S(1)}, bf16[256,512]{1,0:T(8,1...) custom-call(f32[4,2,32,512]{3,2,1,0:T(8,128)} %shift_hbm.1, ...), custom_call_target="tpu_custom_call" | custom-call | tf_op jit(solution)/shard_map/pallas_call | solution.py:416
  8.6 0.1 reshape.22.refs_0_
  8.7 4.4 %collective-permute-done.refs_1_ = f32[3,32,256]{2,1,0:T(8,128)S(1)} collective-permute-done((f32[3,32,256]{2,1,0:T(8,128)S(1)}, f32[3,32,256]{2,1,0:T(8,128)S(1)}, u32[]{:S(2)}, u32[]{:S(2)}) %collective-permute-start) | collective-permute-done | bytes 98336 | tf_op jit(solution)/shard_map/ppermute | solution.py:27
  13.1 0.6 %shard_map.84 = (f32[16,2,4,8,128]{4,3,2,1,0:T(8,128)S(1)}, s32[1024]{0:T(1024)S(4)}) custom-call(s32[1024]{0:T(1024)S(1)} %reshape.22.refs_0_, f32[3,32,256]{2,1,0:T(8,128)S(1)} %collective-permute-done.refs_1_, bf16[256,512]{1,0:T(8,128)(2,1)S(1)} %get-tuple-element.30.refs_2_.refs_1_.phi_high_ref, ...), custom_call_target="tpu_custom_call", output_to_operand_aliasing={{0}: (6, {})} | custom-call | tf_op jit(solution)/shard_map/pallas_call | solution.py:416
  13.7 0.0 collective-permute-done.1.refs_0_
  13.7 0.5 shard_map.85
  14.3 0.0 copy-start.1
  14.3 19.0 %all_to_all.10 = f32[16,2,4,8,128]{4,3,2,1,0:T(8,128)S(1)} all-to-all(f32[16,2,4,8,128]{4,3,2,1,0:T(8,128)S(1)} %shard_map.85), channel_id=1, replica_groups=mesh['clus'=16,'theta'=8] {'clus'}, dimensions={0} | all-to-all | bytes 1048576 | tf_op jit(solution)/shard_map/all_to_all | solution.py:515
  33.3 0.0 copy-done.1
  33.3 2.2 %translate.1 = f32[1024,128]{1,0:T(8,128)S(1)} custom-call(s32[1024]{0:T(1024)S(4)} %get-tuple-element.35.codes_ref, s32[32]{0:T(128)S(4)} %get-tuple-element.36.counts_ref, f32[1024,128]{1,0:T(8,128)S(1)} %bitcast.10, f32[640,128]{1,0:T(8,128)S(1)} %bitcast.12), custom_call_target="tpu_custom_call" | custom-call | tf_op jit(solution)/shard_map/translate/pallas_call | solution.py:437
  35.5 15.0 %all_to_all.11.local_ref = f32[16,2,4,8,128]{4,3,2,1,0:T(8,128)S(1)} all-to-all(f32[16,2,4,8,128]{4,3,2,1,0:T(8,128)S(1)} %bitcast.11), channel_id=1, replica_groups=mesh['clus'=16,'theta'=8] {'clus'}, dimensions={0} | all-to-all | bytes 1048576 | tf_op jit(solution)/shard_map/all_to_all | solution.py:517
  50.4 0.6 %shard_map.87 = f32[4,32,256]{2,1,0:T(8,128)S(1)} custom-call(f32[16,2,4,8,128]{4,3,2,1,0:T(8,128)S(1)} %all_to_all.11.local_ref, f32[4,2,32,512]{3,2,1,0:T(8,128)S(1)} %get-tuple-element.33.refs_5_.refs_4_.shift_ref, bf16[256,512]{1,0:T(8,128)(2,1)S(1)} %get-tuple-element.30.refs_2_.refs_1_.phi_high_ref, ...), custom_call_target="tpu_custom_call" | custom-call | tf_op jit(solution)/shard_map/pallas_call | solution.py:416
  51.1 0.1 collective-permute-start.2
  51.1 0.6 %shard_map.88 = f32[3,32,256]{2,1,0:T(8,128)S(1)} custom-call(f32[16,2,4,8,128]{4,3,2,1,0:T(8,128)S(1)} %all_to_all.11.local_ref, f32[4,2,32,512]{3,2,1,0:T(8,128)S(1)} %get-tuple-element.33.refs_5_.refs_4_.shift_ref, bf16[256,512]{1,0:T(8,128)(2,1)S(1)} %get-tuple-element.30.refs_2_.refs_1_.phi_high_ref, ...), custom_call_target="tpu_custom_call" | custom-call | tf_op jit(solution)/shard_map/pallas_call | solution.py:416
  51.8 4.2 %collective-permute-start.3 = (f32[3,32,256]{2,1,0:T(8,128)S(1)}, f32[3,32,256]{2,1,0:T(8,128)S(1)}, u32[]{:S(2)}, u32[]{:S(2)}) collective-permute-start(f32[3,32,256]{2,1,0:T(8,128)S(1)} %shard_map.88), channel_id=1, source_target_pairs={{0,7},{1,0},{2,1},{3,2},{4,3},{5,4},{6,5},{7,6},{8,15},{9,8},{10,9... | collective-permute-start | bytes 294920 | tf_op jit(solution)/shard_map/ppermute | solution.py:27
  55.9 1.9 %shard_map.86._ = f32[2,512,128]{2,1,0:T(8,128)S(1)} custom-call(f32[16,2,4,8,128]{4,3,2,1,0:T(8,128)S(1)} %all_to_all.11.local_ref, f32[4,2,32,512]{3,2,1,0:T(8,128)S(1)} %get-tuple-element.33.refs_5_.refs_4_.shift_ref, bf16[256,512]{1,0:T(8,128)(2,1)S(1)} %get-tuple-element.30.refs_2_.refs_1_.phi_high_ref, ...), custom_call_target="tpu_custom_call" | custom-call | tf_op jit(solution)/shard_map/pallas_call | solution.py:416
  57.8 0.3 collective-permute-done.3.bottom_ref
  58.2 0.0 collective-permute-done.2.top_ref
  58.2 0.9 %shard_map.89 = (f32[512,256]{1,0:T(8,128)}, f32[2,512,128]{2,1,0:T(8,128)S(1)}) custom-call(f32[2,512,128]{2,1,0:T(8,128)S(1)} %shard_map.86._, f32[4,32,256]{2,1,0:T(8,128)S(1)} %collective-permute-done.2.top_ref, f32[3,32,256]{2,1,0:T(8,128)S(1)} %collective-permute-done.3.bottom_ref), custom_call_target="tpu_custom_call", output_to_operand_aliasing={{1}: (0, {})} | custom-call | tf_op jit(solution)/shard_map/pallas_call | solution.py:416
Async XLA Ops:
  0.0 6.4 %copy-start = (f32[256,512]{1,0:T(8,128)S(1)}, f32[256,512]{1,0:T(8,128)}, u32[]{:S(2)}) copy-start(f32[256,512]{1,0:T(8,128)} %phi_ref.1) | copy-start | bytes 1572868
  1.2 12.5 %collective-permute-start.1 = (f32[4,32,256]{2,1,0:T(8,128)S(1)}, f32[4,32,256]{2,1,0:T(8,128)S(1)}, u32[]{:S(2)}, u32[]{:S(2)}) collective-permute-start(f32[4,32,256]{2,1,0:T(8,128)S(1)} %get-tuple-element.37), channel_id=1, source_target_pairs={{0,7},{1,0},{2,1},{3,2},{4,3},{5,4},{6,5},{7,6},{8,15},{9,8},{10,9... | collective-permute-start | bytes 393224 | tf_op jit(solution)/shard_map/ppermute | solution.py:27
  6.4 6.7 %collective-permute-start = (f32[3,32,256]{2,1,0:T(8,128)S(1)}, f32[3,32,256]{2,1,0:T(8,128)S(1)}, u32[]{:S(2)}, u32[]{:S(2)}) collective-permute-start(f32[3,32,256]{2,1,0:T(8,128)S(1)} %get-tuple-element.29), channel_id=1, source_target_pairs={{0,1},{1,2},{2,3},{3,4},{4,5},{5,6},{6,7},{7,0},{8,9},{9,10},{10,1... | collective-permute-start | bytes 294920 | tf_op jit(solution)/shard_map/ppermute | solution.py:27
  14.3 19.0 %copy-start.1 = (f32[40,2,2,512]{3,2,1,0:T(2,128)S(1)}, f32[40,2,2,512]{3,2,1,0:T(2,128)}, u32[]{:S(2)}) copy-start(f32[40,2,2,512]{3,2,1,0:T(2,128)} %param.12) | copy-start | bytes 983044
  51.1 7.1 %collective-permute-start.2 = (f32[4,32,256]{2,1,0:T(8,128)S(1)}, f32[4,32,256]{2,1,0:T(8,128)S(1)}, u32[]{:S(2)}, u32[]{:S(2)}) collective-permute-start(f32[4,32,256]{2,1,0:T(8,128)S(1)} %shard_map.87), channel_id=1, source_target_pairs={{0,1},{1,2},{2,3},{3,4},{4,5},{5,6},{6,7},{7,0},{8,9},{9,10},{10,1... | collective-permute-start | bytes 393224 | tf_op jit(solution)/shard_map/ppermute | solution.py:27
  51.8 6.4 %collective-permute-start.3 = (f32[3,32,256]{2,1,0:T(8,128)S(1)}, f32[3,32,256]{2,1,0:T(8,128)S(1)}, u32[]{:S(2)}, u32[]{:S(2)}) collective-permute-start(f32[3,32,256]{2,1,0:T(8,128)S(1)} %shard_map.88), channel_id=1, source_target_pairs={{0,7},{1,0},{2,1},{3,2},{4,3},{5,4},{6,5},{7,6},{8,15},{9,8},{10,9... | collective-permute-start | bytes 294920 | tf_op jit(solution)/shard_map/ppermute | solution.py:27

commit v11 on v10

--- a/solution.py
+++ b/solution.py
@@ -1,5 +1,3 @@
-import functools
-
 import jax
 import jax.numpy as jnp
 from jax import lax
@@ -137,32 +135,19 @@
     return tables
 
 
-def cut_kernel(
-    children_hbm, taps_hbm, children_ref, taps_ref, upper_ref, lower_ref, sems
-):
-    chunks = [slice(128 * i, 128 * i + 128) for i in range(4)]
+def cut_kernel(children_hbm, taps_hbm, upper_ref, lower_ref, taps_ref, sems):
     copies = [
-        pltpu.make_async_copy(
-            children_hbm.at[chunk, 128 * side : 128 * side + 128],
-            children_ref.at[side, chunk],
-            sems.at[2 * i + side],
-        )
-        for i, chunk in enumerate(chunks)
-        for side in range(2)
+        pltpu.make_async_copy(children_hbm.at[:, row], upper_ref.at[row], sems.at[row])
+        for row in range(4)
     ]
+    for row in range(3):
+        source = children_hbm.at[:, OWN - 3 + row]
+        copies.append(pltpu.make_async_copy(source, lower_ref.at[row], sems.at[4 + row]))
+    copies.append(pltpu.make_async_copy(taps_hbm, taps_ref, sems.at[7]))
     for copy in copies:
         copy.start()
-    taps = pltpu.make_async_copy(taps_hbm, taps_ref, sems.at[8])
-    taps.start()
-    for at, copy in enumerate(copies):
+    for copy in copies:
         copy.wait()
-        i, side = divmod(at, 2)
-        for ref, first, count in ((upper_ref, 0, 4), (lower_ref, OWN - 3, 3)):
-            for row in range(count):
-                rows = pl.ds(128 * i + first + row, 8, stride=OWN)
-                value = children_ref[side, rows, :]
-                ref[row, 8 * i : 8 * i + 8, 128 * side : 128 * side + 128] = value
-    taps.wait()
 
 
 def both_sides(ref, first, count):
@@ -170,14 +155,16 @@
 
 
 def own_forward_kernel(
-    shift_hbm, source_hbm, offset_hbm, counts_hbm, phi_ref, taps_ref, children_ref,
-    packed_ref, shift_ref, phi_high_ref, phi_low_ref, above_ref, below_ref, back_high_ref, back_low_ref,
+    children_hbm, shift_hbm, source_hbm, offset_hbm, counts_hbm, operators_hbm, phi_ref, taps_ref,
+    packed_ref, shift_ref, operators_ref, phi_high_ref, phi_low_ref, above_ref, below_ref, back_high_ref, back_low_ref,
     up_ref, down_ref, codes_ref, counts_ref,
-    fine_ref, source_ref, offset_ref, sems, *, kinds,
+    fine_ref, source_ref, offset_ref, children_ref, raw_ref, sems,
 ):
+    kinds = raw_ref.shape[0] // 16
     pairs = (
+        (children_hbm.at[:, :128], children_ref.at[0]), (children_hbm.at[:, 128:], children_ref.at[1]),
         (shift_hbm, shift_ref), (source_hbm, source_ref), (offset_hbm, offset_ref),
-        (counts_hbm, counts_ref),
+        (counts_hbm, counts_ref), (operators_hbm, raw_ref),
     )
     copies = [pltpu.make_async_copy(*pair, sems.at[i]) for i, pair in enumerate(pairs)]
     for copy in copies:
@@ -204,9 +191,11 @@
                     for pair, tile in enumerate(swap_blocks(lane_blocks(value))):
                         packed_ref[4 * block + pair, parent, 2 * pol + part] = tile
 
+    for copy in copies[:2]:
+        copy.wait()
     spread(0)
     spread(1)
-    for copy in copies:
+    for copy in copies[2:]:
         copy.wait()
     spread(2)
     collect(0)
@@ -219,6 +208,12 @@
     up_ref[...] = jnp.concatenate(table, axis=1)
     table = backward_table(lower, 16, 4, below_rows)
     down_ref[...] = jnp.concatenate(table, axis=1)
+    for kind in range(kinds):
+        c = raw_ref[16 * kind : 16 * kind + 8]
+        d = raw_ref[16 * kind + 8 : 16 * kind + 16]
+        for at, value in enumerate((c, d - c, c + d)):
+            operators_ref[24 * kind + 8 * at : 24 * kind + 8 * at + 8] = value
+    operators_ref[24 * kinds : 24 * kinds + 24] = jnp.zeros((24, 128), WHOLE)
     lane = lax.broadcasted_iota(jnp.int32, (1, LIST), 1)
     for parent in range(source_ref.shape[0]):
         live = lane < counts_ref[parent]
@@ -301,13 +296,14 @@
         yield kid, halves(jnp.concatenate(real + imag, axis=0))
 
 
-def edge_back_kernel(first, skipped):
-    def kernel(
-        local_ref, shift_ref, phi_high_ref, phi_low_ref, table_ref, out_ref, result_ref,
-    ):
-        phi = (phi_high_ref[...], phi_low_ref[...])
+def edge_back_kernel(
+    local_ref, shift_ref, phi_high_ref, phi_low_ref, up_table_ref, down_table_ref,
+    up_ref, down_ref, result_ref,
+):
+    phi = (phi_high_ref[...], phi_low_ref[...])
+    narrow = []
+    for first, table_ref in ((12, down_table_ref), (0, up_table_ref)):
         table = table_ref[...]
-        narrow = []
         for parent in range(2):
             pieces = {}
             for pol in range(2):
@@ -316,15 +312,15 @@
             order = [(kid, pol) for kid in range(KIDS) for pol in range(2)]
             value = [jnp.concatenate([pieces[at][i] for at in order], axis=0) for i in range(2)]
             narrow.append(table_times(table, value))
-        result = dot3(halves(jnp.concatenate(narrow, axis=0)), phi, contract=1)
-        for side in range(2):
-            lanes = slice(128 * side, 128 * side + 128)
-            result_ref[side] = result[:, lanes]
-            for row in range(4 - skipped):
-                rows = pl.ds(row + skipped, PLANES, stride=4)
-                out_ref[row, :, lanes] = result_ref[side, rows, :]
-
-    return kernel
+    result = dot3(halves(jnp.concatenate(narrow, axis=0)), phi, contract=1)
+    for side in range(2):
+        lanes = slice(128 * side, 128 * side + 128)
+        result_ref[side] = result[:, lanes]
+        for row in range(4):
+            down_ref[row, :, lanes] = result_ref[side, pl.ds(row, PLANES, stride=4), :]
+        for row in range(3):
+            rows = pl.ds(4 * PLANES + row + 1, PLANES, stride=4)
+            up_ref[row, :, lanes] = result_ref[side, rows, :]
 
 
 def own_back_kernel(
@@ -348,15 +344,8 @@
                 own_ref[side, 128 * group : 128 * (group + 1)] = result[:, lanes]
 
 
-def translate_kernel(codes_ref, counts_ref, field_ref, operator_ref, out_ref, table_ref, sum_ref):
+def translate_kernel(codes_ref, counts_ref, field_ref, table_ref, out_ref, sum_ref):
     parents = counts_ref.shape[0]
-    kinds = operator_ref.shape[0] // 16
-    for kind in range(kinds):
-        c = operator_ref[16 * kind : 16 * kind + 8]
-        d = operator_ref[16 * kind + 8 : 16 * kind + 16]
-        for at, value in enumerate((c, d - c, c + d)):
-            table_ref[24 * kind + 8 * at : 24 * kind + 8 * at + 8] = value
-    table_ref[24 * kinds : 24 * kinds + 24] = jnp.zeros((24, 128), WHOLE)
     for at in range(2 * parents):
         rows = slice(16 * at, 16 * at + 8)
         sum_ref[8 * at : 8 * at + 8] = field_ref[rows] + field_ref[16 * at + 8 : 16 * at + 16]
@@ -440,7 +429,6 @@
         in_specs=[smem, smem, vmem, vmem],
         out_specs=vmem,
         scratch_shapes=[
-            pltpu.VMEM((operators.shape[0] * 3 // 2 + 24, 128), WHOLE),
             pltpu.VMEM((field.shape[0] // 2, 128), WHOLE),
         ],
         compiler_params=pltpu.CompilerParams(vmem_limit_bytes=GRANT),
@@ -476,30 +464,31 @@
     vmem = pl.BlockSpec(memory_space=pltpu.VMEM)
     smem = pl.BlockSpec(memory_space=pltpu.SMEM)
     dma = pltpu.SemaphoreType.DMA
-    planes, taps, upper, lower = call(
-        cut_kernel,
-        (
-            whole(2, PLANES * OWN, 128), whole(8, ROWS), whole(4, PLANES, PHI),
-            whole(3, PLANES, PHI),
-        ),
-        [dma((9,))], children.reshape(-1, PHI), theta_band.T, raw=2,
+    upper, lower, taps = call(
+        cut_kernel, (whole(4, PLANES, PHI), whole(3, PLANES, PHI), whole(8, ROWS)),
+        [dma((8,))], children.reshape(PLANES, OWN, PHI), theta_band.T, raw=2,
     )
     above = shifted_ring(lower, "theta", 1)
     below = shifted_ring(upper, "theta", -1)
     tables = (half(256, 512),) * 2 + (half(128, 256),) * 4
-    packed, shift, *tables, codes, counts = call(
-        functools.partial(own_forward_kernel, kinds=translators.shape[0]),
-        (whole(16, 2, 4, 8, 128), whole(*child_shift.shape)) + tables + (half(64, 256),) * 2
+    operators = operator_rows(translators)
+    packed, shift, operators, *tables, codes, counts = call(
+        own_forward_kernel,
+        (
+            whole(16, 2, 4, 8, 128), whole(*child_shift.shape),
+            whole(operators.shape[0] * 3 // 2 + 24, 128),
+        )
+        + tables + (half(64, 256),) * 2
         + (pltpu.VMEM(far_source.shape, jnp.int32), pltpu.SMEM(far_count.shape, jnp.int32)),
         [
             whole(1024, SAMPLES), pltpu.VMEM(far_source.shape, jnp.int32),
-            pltpu.VMEM(far_source.shape, jnp.int32), dma((4,)),
+            pltpu.VMEM(far_source.shape, jnp.int32), whole(2, PLANES * OWN, 128),
+            whole(*operators.shape), dma((7,)),
         ],
-        child_shift, far_source, far_offset, far_count, phi_interp, taps, planes,
-        raw=4, out_specs=(vmem,) * 11 + (smem,),
+        children.reshape(-1, PHI), child_shift, far_source, far_offset, far_count, operators,
+        phi_interp, taps, raw=6, out_specs=(vmem,) * 12 + (smem,),
     )
     *phi, above_table, below_table, back_high, back_low, up_table, down_table = tables
-    operators = in_vmem(operator_rows(translators))
     scratch = [whole(2, 128, 128), whole(256, SAMPLES)]
     packed, codes = call(
         edge_forward_kernel(0),
@@ -511,20 +500,14 @@
         edge_forward_kernel(1), whole(16, 2, 4, 8, 128), scratch,
         below, *phi, below_table, shift, packed, aliases={5: 0},
     )
-    packed, operators = lax.optimization_barrier((packed, operators))
     field = lax.all_to_all(packed, "clus", 0, 0)
     summed = translate(field, codes, counts, operators)
     local = lax.all_to_all(summed.reshape(packed.shape), "clus", 0, 0)
-    scratch = [whole(2, 128, 128)]
-    down = call(
-        edge_back_kernel(12, 0), whole(4, PLANES, PHI), scratch,
-        local, shift, *phi, down_table,
+    up, down = call(
+        edge_back_kernel, (whole(3, PLANES, PHI), whole(4, PLANES, PHI)),
+        [whole(2, 256, 128)], local, shift, *phi, up_table, down_table,
     )
     from_below = shifted_ring(down, "theta", 1)
-    up = call(
-        edge_back_kernel(0, 1), whole(3, PLANES, PHI), scratch,
-        local, shift, *phi, up_table,
-    )
     from_above = shifted_ring(up, "theta", -1)
     own = call(
         own_back_kernel, whole(2, PLANES * OWN, 128), [half(1024, SAMPLES)] * 2,

time: 59.3 us -> 59.1 us (level)
    pallas_call x8 -> x7, Pallas kernels: 8.58 us -> 9.05 us  [call(): pl.pallas_call(kernel, out_shape=outs, in_specs=[hbm] * raw + [vmem] * (l...]
  transfers between devices with their start and end apart: 4 -> 4, of which waited for: 2 -> 3; matrix products, arithmetic and copies ran while one was open for 0% -> 0% of each run, Pallas kernels for 9% -> 10%
where the time goes in v11:
time: 59.1 us; the launch traced here: 58.9 us
  blocking collectives  33.8 us (57%)
  Pallas kernels  11.2 us (19%)
  starting transfers between devices  9.34 us (16%)
  waiting for transfers between devices  4.36 us (7%)
    all_to_all x1, blocking collectives, on_device(): field = lax.all_to_all(packed, 'clus', 0, 0)  18.9 us
    all_to_all x1, blocking collectives, on_device(): local = lax.all_to_all(summed.reshape(packed.shape), 'clus', 0, 0)  15 us
    ppermute x4, starting transfers between devices, shifted_ring(): lax.ppermute(value, axis, [(i, (i + step) % count) for i in range(count)])  9.34 us
    pallas_call x7, Pallas kernels, call(): pl.pallas_call(kernel, out_shape=outs, in_specs=[hbm] * raw + [vmem] * (l...  9.05 us
    ppermute x4, waiting for transfers between devices, shifted_ring(): lax.ppermute(value, axis, [(i, (i + step) % count) for i in range(count)])  4.36 us
    pallas_call x1, Pallas kernels, translate(): pl.pallas_call(translate_kernel, out_shape=jax.ShapeDtypeStruct(field.sha...  2.18 us
  transfers between devices with their start and end apart: 4, of which 3 were waited for; matrix products, arithmetic and copies ran while one was open for 0% of the time, Pallas kernels for 10%

profile of v11, /device:TPU:0, one launch (start us, length us, event | category | flops | bytes accessed | tf_op | source)
XLA Modules:
  0.0 58.9 jit_solution(11968048397060677798)
XLA Ops:
  0.0 0.0 copy-start
  0.0 1.0 %shard_map.82 = (f32[4,32,256]{2,1,0:T(8,128)S(1)}, f32[3,32,256]{2,1,0:T(8,128)S(1)}, f32[8,32]{1,0:T(8,128)S(1)}) custom-call(f32[32,16,256]{2,1,0:T(8,128)} %bitcast.13, f32[8,32]{1,0:T(8,128)} %bitcast.16), custom_call_target="tpu_custom_call" | custom-call | tf_op jit(solution)/shard_map/pallas_call | solution.py:405
  1.0 5.1 %collective-permute-start.1 = (f32[4,32,256]{2,1,0:T(8,128)S(1)}, f32[4,32,256]{2,1,0:T(8,128)S(1)}, u32[]{:S(2)}, u32[]{:S(2)}) collective-permute-start(f32[4,32,256]{2,1,0:T(8,128)S(1)} %get-tuple-element.36), channel_id=1, source_target_pairs={{0,7},{1,0},{2,1},{3,2},{4,3},{5,4},{6,5},{7,6},{8,15},{9,8},{10,9... | collective-permute-start | bytes 393224 | tf_op jit(solution)/shard_map/ppermute | solution.py:25
  6.2 0.0 collective-permute-start
  6.2 0.0 copy-done
  6.2 3.3 %shard_map.83 = (f32[16,2,4,8,128]{4,3,2,1,0:T(8,128)S(1)}, f32[4,2,32,512]{3,2,1,0:T(8,128)S(1)}, f32[984,128]{1,0:T(8,128)S(1)}, bf16[256,512]{1,0:T(8,128)(2,...) custom-call(f32[512,256]{1,0:T(8,128)} %bitcast.14, ...), custom_call_target="tpu_custom_call" | custom-call | tf_op jit(solution)/shard_map/pallas_call | solution.py:405
  9.5 0.1 reshape.28.refs_0_
  9.6 3.3 %collective-permute-done.refs_1_ = f32[3,32,256]{2,1,0:T(8,128)S(1)} collective-permute-done((f32[3,32,256]{2,1,0:T(8,128)S(1)}, f32[3,32,256]{2,1,0:T(8,128)S(1)}, u32[]{:S(2)}, u32[]{:S(2)}) %collective-permute-start) | collective-permute-done | bytes 98336 | tf_op jit(solution)/shard_map/ppermute | solution.py:25
  12.9 0.6 %shard_map.84 = (f32[16,2,4,8,128]{4,3,2,1,0:T(8,128)S(1)}, s32[1024]{0:T(1024)S(4)}) custom-call(s32[1024]{0:T(1024)S(1)} %reshape.28.refs_0_, f32[3,32,256]{2,1,0:T(8,128)S(1)} %collective-permute-done.refs_1_, bf16[256,512]{1,0:T(8,128)(2,1)S(1)} %get-tuple-element.29.refs_2_.refs_1_.phi_high_ref, ...), custom_call_target="tpu_custom_call", output_to_operand_aliasing={{0}: (6, {})} | custom-call | tf_op jit(solution)/shard_map/pallas_call | solution.py:405
  13.5 0.0 collective-permute-done.1.refs_0_
  13.5 0.5 shard_map.85
  14.1 18.9 %all_to_all.10 = f32[16,2,4,8,128]{4,3,2,1,0:T(8,128)S(1)} all-to-all(f32[16,2,4,8,128]{4,3,2,1,0:T(8,128)S(1)} %shard_map.85), channel_id=1, replica_groups=mesh['clus'=16,'theta'=8] {'clus'}, dimensions={0} | all-to-all | bytes 1048576 | tf_op jit(solution)/shard_map/all_to_all | solution.py:503
  32.9 2.2 %translate.1 = f32[1024,128]{1,0:T(8,128)S(1)} custom-call(s32[1024]{0:T(1024)S(4)} %get-tuple-element.34.codes_ref, s32[32]{0:T(128)S(4)} %get-tuple-element.35.counts_ref, f32[1024,128]{1,0:T(8,128)S(1)} %bitcast.11, f32[984,128]{1,0:T(8,128)S(1)} %get-tuple-element.39.table_ref), custom_call_target="tpu_custom_call" | custom-call | tf_op jit(solution)/shard_map/translate/pallas_call | solution.py:426
  35.1 15.0 %all_to_all.11.local_ref = f32[16,2,4,8,128]{4,3,2,1,0:T(8,128)S(1)} all-to-all(f32[16,2,4,8,128]{4,3,2,1,0:T(8,128)S(1)} %bitcast.12), channel_id=1, replica_groups=mesh['clus'=16,'theta'=8] {'clus'}, dimensions={0} | all-to-all | bytes 1048576 | tf_op jit(solution)/shard_map/all_to_all | solution.py:505
  50.1 0.8 %shard_map.87 = (f32[3,32,256]{2,1,0:T(8,128)S(1)}, f32[4,32,256]{2,1,0:T(8,128)S(1)}) custom-call(f32[16,2,4,8,128]{4,3,2,1,0:T(8,128)S(1)} %all_to_all.11.local_ref, f32[4,2,32,512]{3,2,1,0:T(8,128)S(1)} %get-tuple-element.32.refs_5_.refs_4_.shift_ref, bf16[256,512]{1,0:T(8,128)(2,1)S(1)} %get-tuple-element.29.refs_2_.refs_1_.phi_high_ref, ...), custom_call_target="tpu_custom_call" | custom-call | tf_op jit(solution)/shard_map/pallas_call | solution.py:405
  50.9 0.1 collective-permute-start.2
  51.0 4.1 %collective-permute-start.3 = (f32[3,32,256]{2,1,0:T(8,128)S(1)}, f32[3,32,256]{2,1,0:T(8,128)S(1)}, u32[]{:S(2)}, u32[]{:S(2)}) collective-permute-start(f32[3,32,256]{2,1,0:T(8,128)S(1)} %get-tuple-element.45), channel_id=1, source_target_pairs={{0,7},{1,0},{2,1},{3,2},{4,3},{5,4},{6,5},{7,6},{8,15},{9,8},{10,9... | collective-permute-start | bytes 294920 | tf_op jit(solution)/shard_map/ppermute | solution.py:25
  55.1 1.9 %shard_map.86._ = f32[2,512,128]{2,1,0:T(8,128)S(1)} custom-call(f32[16,2,4,8,128]{4,3,2,1,0:T(8,128)S(1)} %all_to_all.11.local_ref, f32[4,2,32,512]{3,2,1,0:T(8,128)S(1)} %get-tuple-element.32.refs_5_.refs_4_.shift_ref, bf16[256,512]{1,0:T(8,128)(2,1)S(1)} %get-tuple-element.29.refs_2_.refs_1_.phi_high_ref, ...), custom_call_target="tpu_custom_call" | custom-call | tf_op jit(solution)/shard_map/pallas_call | solution.py:405
  57.0 0.3 collective-permute-done.3.bottom_ref
  57.3 0.7 %collective-permute-done.2.top_ref = f32[4,32,256]{2,1,0:T(8,128)S(1)} collective-permute-done((f32[4,32,256]{2,1,0:T(8,128)S(1)}, f32[4,32,256]{2,1,0:T(8,128)S(1)}, u32[]{:S(2)}, u32[]{:S(2)}) %collective-permute-start.2) | collective-permute-done | bytes 131104 | tf_op jit(solution)/shard_map/ppermute | solution.py:25
  58.0 0.9 %shard_map.88 = (f32[512,256]{1,0:T(8,128)}, f32[2,512,128]{2,1,0:T(8,128)S(1)}) custom-call(f32[2,512,128]{2,1,0:T(8,128)S(1)} %shard_map.86._, f32[4,32,256]{2,1,0:T(8,128)S(1)} %collective-permute-done.2.top_ref, f32[3,32,256]{2,1,0:T(8,128)S(1)} %collective-permute-done.3.bottom_ref), custom_call_target="tpu_custom_call", output_to_operand_aliasing={{1}: (0, {})} | custom-call | tf_op jit(solution)/shard_map/pallas_call | solution.py:405
Async XLA Ops:
  0.0 6.2 %copy-start = (f32[256,512]{1,0:T(8,128)S(1)}, f32[256,512]{1,0:T(8,128)}, u32[]{:S(2)}) copy-start(f32[256,512]{1,0:T(8,128)} %phi_ref.1) | copy-start | bytes 1572868
  1.0 12.5 %collective-permute-start.1 = (f32[4,32,256]{2,1,0:T(8,128)S(1)}, f32[4,32,256]{2,1,0:T(8,128)S(1)}, u32[]{:S(2)}, u32[]{:S(2)}) collective-permute-start(f32[4,32,256]{2,1,0:T(8,128)S(1)} %get-tuple-element.36), channel_id=1, source_target_pairs={{0,7},{1,0},{2,1},{3,2},{4,3},{5,4},{6,5},{7,6},{8,15},{9,8},{10,9... | collective-permute-start | bytes 393224 | tf_op jit(solution)/shard_map/ppermute | solution.py:25
  6.2 6.7 %collective-permute-start = (f32[3,32,256]{2,1,0:T(8,128)S(1)}, f32[3,32,256]{2,1,0:T(8,128)S(1)}, u32[]{:S(2)}, u32[]{:S(2)}) collective-permute-start(f32[3,32,256]{2,1,0:T(8,128)S(1)} %get-tuple-element.28), channel_id=1, source_target_pairs={{0,1},{1,2},{2,3},{3,4},{4,5},{5,6},{6,7},{7,0},{8,9},{9,10},{10,1... | collective-permute-start | bytes 294920 | tf_op jit(solution)/shard_map/ppermute | solution.py:25
  50.9 7.1 %collective-permute-start.2 = (f32[4,32,256]{2,1,0:T(8,128)S(1)}, f32[4,32,256]{2,1,0:T(8,128)S(1)}, u32[]{:S(2)}, u32[]{:S(2)}) collective-permute-start(f32[4,32,256]{2,1,0:T(8,128)S(1)} %get-tuple-element.44), channel_id=1, source_target_pairs={{0,1},{1,2},{2,3},{3,4},{4,5},{5,6},{6,7},{7,0},{8,9},{9,10},{10,1... | collective-permute-start | bytes 393224 | tf_op jit(solution)/shard_map/ppermute | solution.py:25
  51.0 6.3 %collective-permute-start.3 = (f32[3,32,256]{2,1,0:T(8,128)S(1)}, f32[3,32,256]{2,1,0:T(8,128)S(1)}, u32[]{:S(2)}, u32[]{:S(2)}) collective-permute-start(f32[3,32,256]{2,1,0:T(8,128)S(1)} %get-tuple-element.45), channel_id=1, source_target_pairs={{0,7},{1,0},{2,1},{3,2},{4,3},{5,4},{6,5},{7,6},{8,15},{9,8},{10,9... | collective-permute-start | bytes 294920 | tf_op jit(solution)/shard_map/ppermute | solution.py:25

commit v12 on v10

--- a/solution.py
+++ b/solution.py
@@ -301,13 +301,14 @@
         yield kid, halves(jnp.concatenate(real + imag, axis=0))
 
 
-def edge_back_kernel(first, skipped):
-    def kernel(
-        local_ref, shift_ref, phi_high_ref, phi_low_ref, table_ref, out_ref, result_ref,
-    ):
-        phi = (phi_high_ref[...], phi_low_ref[...])
+def edge_back_kernel(
+    local_ref, shift_ref, phi_high_ref, phi_low_ref, up_table_ref, down_table_ref,
+    up_ref, down_ref, result_ref,
+):
+    phi = (phi_high_ref[...], phi_low_ref[...])
+    narrow = []
+    for first, table_ref in ((12, down_table_ref), (0, up_table_ref)):
         table = table_ref[...]
-        narrow = []
         for parent in range(2):
             pieces = {}
             for pol in range(2):
@@ -316,15 +317,15 @@
             order = [(kid, pol) for kid in range(KIDS) for pol in range(2)]
             value = [jnp.concatenate([pieces[at][i] for at in order], axis=0) for i in range(2)]
             narrow.append(table_times(table, value))
-        result = dot3(halves(jnp.concatenate(narrow, axis=0)), phi, contract=1)
-        for side in range(2):
-            lanes = slice(128 * side, 128 * side + 128)
-            result_ref[side] = result[:, lanes]
-            for row in range(4 - skipped):
-                rows = pl.ds(row + skipped, PLANES, stride=4)
-                out_ref[row, :, lanes] = result_ref[side, rows, :]
-
-    return kernel
+    result = dot3(halves(jnp.concatenate(narrow, axis=0)), phi, contract=1)
+    for side in range(2):
+        lanes = slice(128 * side, 128 * side + 128)
+        result_ref[side] = result[:, lanes]
+        for row in range(4):
+            down_ref[row, :, lanes] = result_ref[side, pl.ds(row, PLANES, stride=4), :]
+        for row in range(3):
+            rows = pl.ds(4 * PLANES + row + 1, PLANES, stride=4)
+            up_ref[row, :, lanes] = result_ref[side, rows, :]
 
 
 def own_back_kernel(
@@ -515,16 +516,11 @@
     field = lax.all_to_all(packed, "clus", 0, 0)
     summed = translate(field, codes, counts, operators)
     local = lax.all_to_all(summed.reshape(packed.shape), "clus", 0, 0)
-    scratch = [whole(2, 128, 128)]
-    down = call(
-        edge_back_kernel(12, 0), whole(4, PLANES, PHI), scratch,
-        local, shift, *phi, down_table,
+    up, down = call(
+        edge_back_kernel, (whole(3, PLANES, PHI), whole(4, PLANES, PHI)),
+        [whole(2, 256, 128)], local, shift, *phi, up_table, down_table,
     )
     from_below = shifted_ring(down, "theta", 1)
-    up = call(
-        edge_back_kernel(0, 1), whole(3, PLANES, PHI), scratch,
-        local, shift, *phi, up_table,
-    )
     from_above = shifted_ring(up, "theta", -1)
     own = call(
         own_back_kernel, whole(2, PLANES * OWN, 128), [half(1024, SAMPLES)] * 2,

time: 59.3 us -> 59.5 us (level)
  waiting for transfers between devices: 4.76 us -> 5.44 us
    ppermute x4, waiting for transfers between devices: 4.76 us -> 5.44 us  [shifted_ring(): lax.ppermute(value, axis, [(i, (i + step) % count) for i in range(count)])]
    pallas_call x8 -> x7, Pallas kernels: 8.58 us -> 8.16 us  [call(): pl.pallas_call(kernel, out_shape=outs, in_specs=[hbm] * raw + [vmem] * (l...]
  transfers between devices with their start and end apart: 4 -> 4, of which waited for: 2 -> 3; matrix products, arithmetic and copies ran while one was open for 0% -> 0% of each run, Pallas kernels for 9% -> 8%
where the time goes in v12:
time: 59.5 us; the launch traced here: 59.3 us
  blocking collectives  34 us (57%)
  Pallas kernels  10.4 us (17%)
  starting transfers between devices  9.34 us (16%)
  waiting for transfers between devices  5.44 us (9%)
    all_to_all x1, blocking collectives, on_device(): field = lax.all_to_all(packed, 'clus', 0, 0)  19 us
    all_to_all x1, blocking collectives, on_device(): local = lax.all_to_all(summed.reshape(packed.shape), 'clus', 0, 0)  15 us
    ppermute x4, starting transfers between devices, shifted_ring(): lax.ppermute(value, axis, [(i, (i + step) % count) for i in range(count)])  9.34 us
    pallas_call x7, Pallas kernels, call(): pl.pallas_call(kernel, out_shape=outs, in_specs=[hbm] * raw + [vmem] * (l...  8.16 us
    ppermute x4, waiting for transfers between devices, shifted_ring(): lax.ppermute(value, axis, [(i, (i + step) % count) for i in range(count)])  5.44 us
    pallas_call x1, Pallas kernels, translate(): pl.pallas_call(translate_kernel, out_shape=jax.ShapeDtypeStruct(field.sha...  2.2 us
  transfers between devices with their start and end apart: 4, of which 3 were waited for; matrix products, arithmetic and copies ran while one was open for 0% of the time, Pallas kernels for 8%

profile of v12, /device:TPU:0, one launch (start us, length us, event | category | flops | bytes accessed | tf_op | source)
XLA Modules:
  0.0 59.3 jit_solution(9067680810097722832)
XLA Ops:
  0.0 0.0 copy-start
  0.0 1.2 %shard_map.82 = (f32[2,512,128]{2,1,0:T(8,128)S(1)}, f32[8,32]{1,0:T(8,128)S(1)}, f32[4,32,256]{2,1,0:T(8,128)S(1)}, f32[3,32,256]{2,1,0:T(8,128)S(1)}) custom-call(f32[512,256]{1,0:T(8,128)} %bitcast.13, f32[8,32]{1,0:T(8,128)} %bitcast.14), custom_call_target="tpu_custom_call" | custom-call | tf_op jit(solution)/shard_map/pallas_call | solution.py:417
  1.2 5.1 %collective-permute-start.1 = (f32[4,32,256]{2,1,0:T(8,128)S(1)}, f32[4,32,256]{2,1,0:T(8,128)S(1)}, u32[]{:S(2)}, u32[]{:S(2)}) collective-permute-start(f32[4,32,256]{2,1,0:T(8,128)S(1)} %get-tuple-element.39), channel_id=1, source_target_pairs={{0,7},{1,0},{2,1},{3,2},{4,3},{5,4},{6,5},{7,6},{8,15},{9,8},{10,9... | collective-permute-start | bytes 393224 | tf_op jit(solution)/shard_map/ppermute | solution.py:27
  6.4 0.0 collective-permute-start
  6.4 0.0 copy-done
  6.4 2.3 %shard_map.83 = (f32[16,2,4,8,128]{4,3,2,1,0:T(8,128)S(1)}, f32[4,2,32,512]{3,2,1,0:T(8,128)S(1)}, bf16[256,512]{1,0:T(8,128)(2,1)S(1)}, bf16[256,512]{1,0:T(8,1...) custom-call(f32[4,2,32,512]{3,2,1,0:T(8,128)} %shift_hbm.1, ...), custom_call_target="tpu_custom_call" | custom-call | tf_op jit(solution)/shard_map/pallas_call | solution.py:417
  8.6 0.1 reshape.22.refs_0_
  8.7 4.4 %collective-permute-done.refs_1_ = f32[3,32,256]{2,1,0:T(8,128)S(1)} collective-permute-done((f32[3,32,256]{2,1,0:T(8,128)S(1)}, f32[3,32,256]{2,1,0:T(8,128)S(1)}, u32[]{:S(2)}, u32[]{:S(2)}) %collective-permute-start) | collective-permute-done | bytes 98336 | tf_op jit(solution)/shard_map/ppermute | solution.py:27
  13.1 0.6 %shard_map.84 = (f32[16,2,4,8,128]{4,3,2,1,0:T(8,128)S(1)}, s32[1024]{0:T(1024)S(4)}) custom-call(s32[1024]{0:T(1024)S(1)} %reshape.22.refs_0_, f32[3,32,256]{2,1,0:T(8,128)S(1)} %collective-permute-done.refs_1_, bf16[256,512]{1,0:T(8,128)(2,1)S(1)} %get-tuple-element.32.refs_2_.refs_1_.phi_high_ref, ...), custom_call_target="tpu_custom_call", output_to_operand_aliasing={{0}: (6, {})} | custom-call | tf_op jit(solution)/shard_map/pallas_call | solution.py:417
  13.7 0.0 collective-permute-done.1.refs_0_
  13.7 0.5 shard_map.85
  14.3 0.0 copy-start.1
  14.3 19.0 %all_to_all.10 = f32[16,2,4,8,128]{4,3,2,1,0:T(8,128)S(1)} all-to-all(f32[16,2,4,8,128]{4,3,2,1,0:T(8,128)S(1)} %shard_map.85), channel_id=1, replica_groups=mesh['clus'=16,'theta'=8] {'clus'}, dimensions={0} | all-to-all | bytes 1048576 | tf_op jit(solution)/shard_map/all_to_all | solution.py:516
  33.3 0.0 copy-done.1
  33.3 2.2 %translate.1 = f32[1024,128]{1,0:T(8,128)S(1)} custom-call(s32[1024]{0:T(1024)S(4)} %get-tuple-element.37.codes_ref, s32[32]{0:T(128)S(4)} %get-tuple-element.38.counts_ref, f32[1024,128]{1,0:T(8,128)S(1)} %bitcast.10, f32[640,128]{1,0:T(8,128)S(1)} %bitcast.12), custom_call_target="tpu_custom_call" | custom-call | tf_op jit(solution)/shard_map/translate/pallas_call | solution.py:438
  35.5 15.0 %all_to_all.11.local_ref = f32[16,2,4,8,128]{4,3,2,1,0:T(8,128)S(1)} all-to-all(f32[16,2,4,8,128]{4,3,2,1,0:T(8,128)S(1)} %bitcast.11), channel_id=1, replica_groups=mesh['clus'=16,'theta'=8] {'clus'}, dimensions={0} | all-to-all | bytes 1048576 | tf_op jit(solution)/shard_map/all_to_all | solution.py:518
  50.4 0.8 %shard_map.87 = (f32[3,32,256]{2,1,0:T(8,128)S(1)}, f32[4,32,256]{2,1,0:T(8,128)S(1)}) custom-call(f32[16,2,4,8,128]{4,3,2,1,0:T(8,128)S(1)} %all_to_all.11.local_ref, f32[4,2,32,512]{3,2,1,0:T(8,128)S(1)} %get-tuple-element.35.refs_5_.refs_4_.shift_ref, bf16[256,512]{1,0:T(8,128)(2,1)S(1)} %get-tuple-element.32.refs_2_.refs_1_.phi_high_ref, ...), custom_call_target="tpu_custom_call" | custom-call | tf_op jit(solution)/shard_map/pallas_call | solution.py:417
  51.2 0.1 collective-permute-start.2
  51.3 4.1 %collective-permute-start.3 = (f32[3,32,256]{2,1,0:T(8,128)S(1)}, f32[3,32,256]{2,1,0:T(8,128)S(1)}, u32[]{:S(2)}, u32[]{:S(2)}) collective-permute-start(f32[3,32,256]{2,1,0:T(8,128)S(1)} %get-tuple-element.49), channel_id=1, source_target_pairs={{0,7},{1,0},{2,1},{3,2},{4,3},{5,4},{6,5},{7,6},{8,15},{9,8},{10,9... | collective-permute-start | bytes 294920 | tf_op jit(solution)/shard_map/ppermute | solution.py:27
  55.5 1.9 %shard_map.86._ = f32[2,512,128]{2,1,0:T(8,128)S(1)} custom-call(f32[16,2,4,8,128]{4,3,2,1,0:T(8,128)S(1)} %all_to_all.11.local_ref, f32[4,2,32,512]{3,2,1,0:T(8,128)S(1)} %get-tuple-element.35.refs_5_.refs_4_.shift_ref, bf16[256,512]{1,0:T(8,128)(2,1)S(1)} %get-tuple-element.32.refs_2_.refs_1_.phi_high_ref, ...), custom_call_target="tpu_custom_call" | custom-call | tf_op jit(solution)/shard_map/pallas_call | solution.py:417
  57.3 0.3 collective-permute-done.3.bottom_ref
  57.7 0.7 %collective-permute-done.2.top_ref = f32[4,32,256]{2,1,0:T(8,128)S(1)} collective-permute-done((f32[4,32,256]{2,1,0:T(8,128)S(1)}, f32[4,32,256]{2,1,0:T(8,128)S(1)}, u32[]{:S(2)}, u32[]{:S(2)}) %collective-permute-start.2) | collective-permute-done | bytes 131104 | tf_op jit(solution)/shard_map/ppermute | solution.py:27
  58.4 0.9 %shard_map.88 = (f32[512,256]{1,0:T(8,128)}, f32[2,512,128]{2,1,0:T(8,128)S(1)}) custom-call(f32[2,512,128]{2,1,0:T(8,128)S(1)} %shard_map.86._, f32[4,32,256]{2,1,0:T(8,128)S(1)} %collective-permute-done.2.top_ref, f32[3,32,256]{2,1,0:T(8,128)S(1)} %collective-permute-done.3.bottom_ref), custom_call_target="tpu_custom_call", output_to_operand_aliasing={{1}: (0, {})} | custom-call | tf_op jit(solution)/shard_map/pallas_call | solution.py:417
Async XLA Ops:
  0.0 6.4 %copy-start = (f32[256,512]{1,0:T(8,128)S(1)}, f32[256,512]{1,0:T(8,128)}, u32[]{:S(2)}) copy-start(f32[256,512]{1,0:T(8,128)} %phi_ref.1) | copy-start | bytes 1572868
  1.2 12.5 %collective-permute-start.1 = (f32[4,32,256]{2,1,0:T(8,128)S(1)}, f32[4,32,256]{2,1,0:T(8,128)S(1)}, u32[]{:S(2)}, u32[]{:S(2)}) collective-permute-start(f32[4,32,256]{2,1,0:T(8,128)S(1)} %get-tuple-element.39), channel_id=1, source_target_pairs={{0,7},{1,0},{2,1},{3,2},{4,3},{5,4},{6,5},{7,6},{8,15},{9,8},{10,9... | collective-permute-start | bytes 393224 | tf_op jit(solution)/shard_map/ppermute | solution.py:27
  6.4 6.7 %collective-permute-start = (f32[3,32,256]{2,1,0:T(8,128)S(1)}, f32[3,32,256]{2,1,0:T(8,128)S(1)}, u32[]{:S(2)}, u32[]{:S(2)}) collective-permute-start(f32[3,32,256]{2,1,0:T(8,128)S(1)} %get-tuple-element.31), channel_id=1, source_target_pairs={{0,1},{1,2},{2,3},{3,4},{4,5},{5,6},{6,7},{7,0},{8,9},{9,10},{10,1... | collective-permute-start | bytes 294920 | tf_op jit(solution)/shard_map/ppermute | solution.py:27
  14.3 19.0 %copy-start.1 = (f32[40,2,2,512]{3,2,1,0:T(2,128)S(1)}, f32[40,2,2,512]{3,2,1,0:T(2,128)}, u32[]{:S(2)}) copy-start(f32[40,2,2,512]{3,2,1,0:T(2,128)} %param.12) | copy-start | bytes 983044
  51.2 7.1 %collective-permute-start.2 = (f32[4,32,256]{2,1,0:T(8,128)S(1)}, f32[4,32,256]{2,1,0:T(8,128)S(1)}, u32[]{:S(2)}, u32[]{:S(2)}) collective-permute-start(f32[4,32,256]{2,1,0:T(8,128)S(1)} %get-tuple-element.48), channel_id=1, source_target_pairs={{0,1},{1,2},{2,3},{3,4},{4,5},{5,6},{6,7},{7,0},{8,9},{9,10},{10,1... | collective-permute-start | bytes 393224 | tf_op jit(solution)/shard_map/ppermute | solution.py:27
  51.3 6.3 %collective-permute-start.3 = (f32[3,32,256]{2,1,0:T(8,128)S(1)}, f32[3,32,256]{2,1,0:T(8,128)S(1)}, u32[]{:S(2)}, u32[]{:S(2)}) collective-permute-start(f32[3,32,256]{2,1,0:T(8,128)S(1)} %get-tuple-element.49), channel_id=1, source_target_pairs={{0,7},{1,0},{2,1},{3,2},{4,3},{5,4},{6,5},{7,6},{8,15},{9,8},{10,9... | collective-permute-start | bytes 294920 | tf_op jit(solution)/shard_map/ppermute | solution.py:27

commit v13 on v10

--- a/solution.py
+++ b/solution.py
@@ -171,7 +171,7 @@
 
 def own_forward_kernel(
     shift_hbm, source_hbm, offset_hbm, counts_hbm, phi_ref, taps_ref, children_ref,
-    packed_ref, shift_ref, phi_high_ref, phi_low_ref, above_ref, below_ref, back_high_ref, back_low_ref,
+    packed_ref, shift_ref, phi_high_ref, phi_low_ref, above_ref, below_ref,
     up_ref, down_ref, codes_ref, counts_ref,
     fine_ref, source_ref, offset_ref, sems, *, kinds,
 ):
@@ -213,7 +213,6 @@
     spread(3)
     above_ref[...] = side_table(bands[:8] * first, above_rows)
     below_ref[...] = side_table(bands[ROWS - 8 :] * last, below_rows)
-    back_high_ref[...], back_low_ref[...] = backward_table(taps, 8, 16, same)
     upper, lower = taps[:, :8] * first, taps[:, ROWS - 8 :] * last
     table = backward_table(upper, 16, 4, above_rows)
     up_ref[...] = jnp.concatenate(table, axis=1)
@@ -328,11 +327,11 @@
 
 
 def own_back_kernel(
-    local_ref, shift_ref, phi_high_ref, phi_low_ref, table_high_ref, table_low_ref,
+    local_ref, shift_ref, phi_high_ref, phi_low_ref, taps_ref,
     own_ref, high_ref, low_ref,
 ):
     phi = (phi_high_ref[...], phi_low_ref[...])
-    table = (table_high_ref[...], table_low_ref[...])
+    table = backward_table(taps_ref[...], 8, 16, same)
 
     for parent in range(2):
         for pol in range(2):
@@ -486,7 +485,7 @@
     )
     above = shifted_ring(lower, "theta", 1)
     below = shifted_ring(upper, "theta", -1)
-    tables = (half(256, 512),) * 2 + (half(128, 256),) * 4
+    tables = (half(256, 512),) * 2 + (half(128, 256),) * 2
     packed, shift, *tables, codes, counts = call(
         functools.partial(own_forward_kernel, kinds=translators.shape[0]),
         (whole(16, 2, 4, 8, 128), whole(*child_shift.shape)) + tables + (half(64, 256),) * 2
@@ -496,9 +495,9 @@
             pltpu.VMEM(far_source.shape, jnp.int32), dma((4,)),
         ],
         child_shift, far_source, far_offset, far_count, phi_interp, taps, planes,
-        raw=4, out_specs=(vmem,) * 11 + (smem,),
-    )
-    *phi, above_table, below_table, back_high, back_low, up_table, down_table = tables
+        raw=4, out_specs=(vmem,) * 9 + (smem,),
+    )
+    *phi, above_table, below_table, up_table, down_table = tables
     operators = in_vmem(operator_rows(translators))
     scratch = [whole(2, 128, 128), whole(256, SAMPLES)]
     packed, codes = call(
@@ -528,7 +527,7 @@
     from_above = shifted_ring(up, "theta", -1)
     own = call(
         own_back_kernel, whole(2, PLANES * OWN, 128), [half(1024, SAMPLES)] * 2,
-        local, shift, *phi, back_high, back_low,
+        local, shift, *phi, taps,
     )
     result, _ = call(
         merge_kernel,

time: 59.3 us -> 59.3 us (level)
  no operation moved by 1% of the time
where the time goes in v13:
time: 59.3 us; the launch traced here: 59.1 us
  blocking collectives  34 us (57%)
  Pallas kernels  10.7 us (18%)
  starting transfers between devices  9.41 us (16%)
  waiting for transfers between devices  4.79 us (8%)
    all_to_all x1, blocking collectives, on_device(): field = lax.all_to_all(packed, 'clus', 0, 0)  19 us
    all_to_all x1, blocking collectives, on_device(): local = lax.all_to_all(summed.reshape(packed.shape), 'clus', 0, 0)  15 us
    ppermute x4, starting transfers between devices, shifted_ring(): lax.ppermute(value, axis, [(i, (i + step) % count) for i in range(count)])  9.41 us
    pallas_call x8, Pallas kernels, call(): pl.pallas_call(kernel, out_shape=outs, in_specs=[hbm] * raw + [vmem] * (l...  8.54 us
    ppermute x4, waiting for transfers between devices, shifted_ring(): lax.ppermute(value, axis, [(i, (i + step) % count) for i in range(count)])  4.79 us
    pallas_call x1, Pallas kernels, translate(): pl.pallas_call(translate_kernel, out_shape=jax.ShapeDtypeStruct(field.sha...  2.2 us
  transfers between devices with their start and end apart: 4, of which 2 were waited for; matrix products, arithmetic and copies ran while one was open for 0% of the time, Pallas kernels for 9%

profile of v13, /device:TPU:0, one launch (start us, length us, event | category | flops | bytes accessed | tf_op | source)
XLA Modules:
  0.0 59.1 jit_solution(517066068728066985)
XLA Ops:
  0.0 0.0 copy-start
  0.0 1.2 %shard_map.82 = (f32[2,512,128]{2,1,0:T(8,128)S(1)}, f32[8,32]{1,0:T(8,128)S(1)}, f32[4,32,256]{2,1,0:T(8,128)S(1)}, f32[3,32,256]{2,1,0:T(8,128)S(1)}) custom-call(f32[512,256]{1,0:T(8,128)} %bitcast.13, f32[8,32]{1,0:T(8,128)} %bitcast.14), custom_call_target="tpu_custom_call" | custom-call | tf_op jit(solution)/shard_map/pallas_call | solution.py:415
  1.2 5.1 %collective-permute-start.1 = (f32[4,32,256]{2,1,0:T(8,128)S(1)}, f32[4,32,256]{2,1,0:T(8,128)S(1)}, u32[]{:S(2)}, u32[]{:S(2)}) collective-permute-start(f32[4,32,256]{2,1,0:T(8,128)S(1)} %get-tuple-element.35), channel_id=1, source_target_pairs={{0,7},{1,0},{2,1},{3,2},{4,3},{5,4},{6,5},{7,6},{8,15},{9,8},{10,9... | collective-permute-start | bytes 393224 | tf_op jit(solution)/shard_map/ppermute | solution.py:27
  6.4 0.0 collective-permute-start
  6.4 0.0 copy-done
  6.4 2.2 %shard_map.83 = (f32[16,2,4,8,128]{4,3,2,1,0:T(8,128)S(1)}, f32[4,2,32,512]{3,2,1,0:T(8,128)S(1)}, bf16[256,512]{1,0:T(8,128)(2,1)S(1)}, bf16[256,512]{1,0:T(8,1...) custom-call(f32[4,2,32,512]{3,2,1,0:T(8,128)} %shift_hbm.1, ...), custom_call_target="tpu_custom_call" | custom-call | tf_op jit(solution)/shard_map/pallas_call | solution.py:415
  8.6 0.1 reshape.22.refs_0_
  8.7 4.4 %collective-permute-done.refs_1_ = f32[3,32,256]{2,1,0:T(8,128)S(1)} collective-permute-done((f32[3,32,256]{2,1,0:T(8,128)S(1)}, f32[3,32,256]{2,1,0:T(8,128)S(1)}, u32[]{:S(2)}, u32[]{:S(2)}) %collective-permute-start) | collective-permute-done | bytes 98336 | tf_op jit(solution)/shard_map/ppermute | solution.py:27
  13.1 0.6 %shard_map.84 = (f32[16,2,4,8,128]{4,3,2,1,0:T(8,128)S(1)}, s32[1024]{0:T(1024)S(4)}) custom-call(s32[1024]{0:T(1024)S(1)} %reshape.22.refs_0_, f32[3,32,256]{2,1,0:T(8,128)S(1)} %collective-permute-done.refs_1_, bf16[256,512]{1,0:T(8,128)(2,1)S(1)} %get-tuple-element.28.refs_2_.refs_1_.phi_high_ref, ...), custom_call_target="tpu_custom_call", output_to_operand_aliasing={{0}: (6, {})} | custom-call | tf_op jit(solution)/shard_map/pallas_call | solution.py:415
  13.7 0.0 collective-permute-done.1.refs_0_
  13.7 0.5 shard_map.85
  14.3 0.0 copy-start.1
  14.3 19.0 %all_to_all.10 = f32[16,2,4,8,128]{4,3,2,1,0:T(8,128)S(1)} all-to-all(f32[16,2,4,8,128]{4,3,2,1,0:T(8,128)S(1)} %shard_map.85), channel_id=1, replica_groups=mesh['clus'=16,'theta'=8] {'clus'}, dimensions={0} | all-to-all | bytes 1048576 | tf_op jit(solution)/shard_map/all_to_all | solution.py:514
  33.3 0.0 copy-done.1
  33.3 2.2 %translate.1 = f32[1024,128]{1,0:T(8,128)S(1)} custom-call(s32[1024]{0:T(1024)S(4)} %get-tuple-element.33.codes_ref, s32[32]{0:T(128)S(4)} %get-tuple-element.34.counts_ref, f32[1024,128]{1,0:T(8,128)S(1)} %bitcast.10, f32[640,128]{1,0:T(8,128)S(1)} %bitcast.12), custom_call_target="tpu_custom_call" | custom-call | tf_op jit(solution)/shard_map/translate/pallas_call | solution.py:436
  35.5 15.0 %all_to_all.11.local_ref = f32[16,2,4,8,128]{4,3,2,1,0:T(8,128)S(1)} all-to-all(f32[16,2,4,8,128]{4,3,2,1,0:T(8,128)S(1)} %bitcast.11), channel_id=1, replica_groups=mesh['clus'=16,'theta'=8] {'clus'}, dimensions={0} | all-to-all | bytes 1048576 | tf_op jit(solution)/shard_map/all_to_all | solution.py:516
  50.4 0.6 %shard_map.87 = f32[4,32,256]{2,1,0:T(8,128)S(1)} custom-call(f32[16,2,4,8,128]{4,3,2,1,0:T(8,128)S(1)} %all_to_all.11.local_ref, f32[4,2,32,512]{3,2,1,0:T(8,128)S(1)} %get-tuple-element.31.refs_5_.refs_4_.shift_ref, bf16[256,512]{1,0:T(8,128)(2,1)S(1)} %get-tuple-element.28.refs_2_.refs_1_.phi_high_ref, ...), custom_call_target="tpu_custom_call" | custom-call | tf_op jit(solution)/shard_map/pallas_call | solution.py:415
  51.1 0.1 collective-permute-start.2
  51.1 0.6 %shard_map.88 = f32[3,32,256]{2,1,0:T(8,128)S(1)} custom-call(f32[16,2,4,8,128]{4,3,2,1,0:T(8,128)S(1)} %all_to_all.11.local_ref, f32[4,2,32,512]{3,2,1,0:T(8,128)S(1)} %get-tuple-element.31.refs_5_.refs_4_.shift_ref, bf16[256,512]{1,0:T(8,128)(2,1)S(1)} %get-tuple-element.28.refs_2_.refs_1_.phi_high_ref, ...), custom_call_target="tpu_custom_call" | custom-call | tf_op jit(solution)/shard_map/pallas_call | solution.py:415
  51.8 4.2 %collective-permute-start.3 = (f32[3,32,256]{2,1,0:T(8,128)S(1)}, f32[3,32,256]{2,1,0:T(8,128)S(1)}, u32[]{:S(2)}, u32[]{:S(2)}) collective-permute-start(f32[3,32,256]{2,1,0:T(8,128)S(1)} %shard_map.88), channel_id=1, source_target_pairs={{0,7},{1,0},{2,1},{3,2},{4,3},{5,4},{6,5},{7,6},{8,15},{9,8},{10,9... | collective-permute-start | bytes 294920 | tf_op jit(solution)/shard_map/ppermute | solution.py:27
  55.9 1.9 %shard_map.86._ = f32[2,512,128]{2,1,0:T(8,128)S(1)} custom-call(f32[16,2,4,8,128]{4,3,2,1,0:T(8,128)S(1)} %all_to_all.11.local_ref, f32[4,2,32,512]{3,2,1,0:T(8,128)S(1)} %get-tuple-element.31.refs_5_.refs_4_.shift_ref, bf16[256,512]{1,0:T(8,128)(2,1)S(1)} %get-tuple-element.28.refs_2_.refs_1_.phi_high_ref, ...), custom_call_target="tpu_custom_call" | custom-call | tf_op jit(solution)/shard_map/pallas_call | solution.py:415
  57.8 0.3 collective-permute-done.3.bottom_ref
  58.2 0.0 collective-permute-done.2.top_ref
  58.2 0.9 %shard_map.89 = (f32[512,256]{1,0:T(8,128)}, f32[2,512,128]{2,1,0:T(8,128)S(1)}) custom-call(f32[2,512,128]{2,1,0:T(8,128)S(1)} %shard_map.86._, f32[4,32,256]{2,1,0:T(8,128)S(1)} %collective-permute-done.2.top_ref, f32[3,32,256]{2,1,0:T(8,128)S(1)} %collective-permute-done.3.bottom_ref), custom_call_target="tpu_custom_call", output_to_operand_aliasing={{1}: (0, {})} | custom-call | tf_op jit(solution)/shard_map/pallas_call | solution.py:415
Async XLA Ops:
  0.0 6.4 %copy-start = (f32[256,512]{1,0:T(8,128)S(1)}, f32[256,512]{1,0:T(8,128)}, u32[]{:S(2)}) copy-start(f32[256,512]{1,0:T(8,128)} %phi_ref.1) | copy-start | bytes 1572868
  1.2 12.5 %collective-permute-start.1 = (f32[4,32,256]{2,1,0:T(8,128)S(1)}, f32[4,32,256]{2,1,0:T(8,128)S(1)}, u32[]{:S(2)}, u32[]{:S(2)}) collective-permute-start(f32[4,32,256]{2,1,0:T(8,128)S(1)} %get-tuple-element.35), channel_id=1, source_target_pairs={{0,7},{1,0},{2,1},{3,2},{4,3},{5,4},{6,5},{7,6},{8,15},{9,8},{10,9... | collective-permute-start | bytes 393224 | tf_op jit(solution)/shard_map/ppermute | solution.py:27
  6.4 6.7 %collective-permute-start = (f32[3,32,256]{2,1,0:T(8,128)S(1)}, f32[3,32,256]{2,1,0:T(8,128)S(1)}, u32[]{:S(2)}, u32[]{:S(2)}) collective-permute-start(f32[3,32,256]{2,1,0:T(8,128)S(1)} %get-tuple-element.27), channel_id=1, source_target_pairs={{0,1},{1,2},{2,3},{3,4},{4,5},{5,6},{6,7},{7,0},{8,9},{9,10},{10,1... | collective-permute-start | bytes 294920 | tf_op jit(solution)/shard_map/ppermute | solution.py:27
  14.3 19.0 %copy-start.1 = (f32[40,2,2,512]{3,2,1,0:T(2,128)S(1)}, f32[40,2,2,512]{3,2,1,0:T(2,128)}, u32[]{:S(2)}) copy-start(f32[40,2,2,512]{3,2,1,0:T(2,128)} %param.12) | copy-start | bytes 983044
  51.1 7.1 %collective-permute-start.2 = (f32[4,32,256]{2,1,0:T(8,128)S(1)}, f32[4,32,256]{2,1,0:T(8,128)S(1)}, u32[]{:S(2)}, u32[]{:S(2)}) collective-permute-start(f32[4,32,256]{2,1,0:T(8,128)S(1)} %shard_map.87), channel_id=1, source_target_pairs={{0,1},{1,2},{2,3},{3,4},{4,5},{5,6},{6,7},{7,0},{8,9},{9,10},{10,1... | collective-permute-start | bytes 393224 | tf_op jit(solution)/shard_map/ppermute | solution.py:27
  51.8 6.4 %collective-permute-start.3 = (f32[3,32,256]{2,1,0:T(8,128)S(1)}, f32[3,32,256]{2,1,0:T(8,128)S(1)}, u32[]{:S(2)}, u32[]{:S(2)}) collective-permute-start(f32[3,32,256]{2,1,0:T(8,128)S(1)} %shard_map.88), channel_id=1, source_target_pairs={{0,7},{1,0},{2,1},{3,2},{4,3},{5,4},{6,5},{7,6},{8,15},{9,8},{10,9... | collective-permute-start | bytes 294920 | tf_op jit(solution)/shard_map/ppermute | solution.py:27
